TPU v7x, 128 devices: a whole 4x4x4 slice. The times are simulated.
128 devices in a mesh: gx: 16 (over y_hi, z, core), gy: 8 (over x, y_lo).
Axes of the slice: x: 4, y: 4 (y_hi: 2, y_lo: 2; y = y_hi * 2 + y_lo), z: 4, core: 2. Of those that a mesh axis runs over, the one named last changes fastest.
Arguments:
- cotangent: float32 [64, 128, 1024], P(None, 'gx', 'gy'), may hold values from -6 to 6
- saved_temp: float32 [64, 128, 1024], P(None, 'gx', 'gy'), may hold values from -6 to 6
- substrate_top: int32 [128, 1024], P('gx', 'gy'), may hold values from 16 to 31
- deposit_top: int32 [128, 1024], P('gx', 'gy'), may hold values from 32 to 64
- top_class: int32 [128, 1024], P('gx', 'gy'), may hold values from 0 to 3
Outputs:
- grad_temp: float32 [64, 128, 1024], P(None, 'gx', 'gy')
- grad_source: float32 [64, 128, 1024], P(None, 'gx', 'gy')
All inputs are finite; a program needn't handle non-finite values.
Results may differ from a plain program's by a relative error of at most 0.0005.
Values sent between devices are 32-bit elements; how exact they have to be, the bound alone decides.
No kernel may reach another device: no remote copies, remote signals or barrier semaphores. Data moves between devices by JAX's collectives and lax.ppermute only.
A program may use at most 64 MiB of HBM per device.

v0:
```python
import jax
import jax.numpy as jnp
from jax import lax
from jax.sharding import PartitionSpec as P

step_ratio = 1000.0
side_film = 0.3
bottom_film = 0.5
top_films = (0.05, 0.25, 0.8, 2.0)


def extended(cells, sides, width):
    for axis, dim in sides:
        count = lax.axis_size(axis)
        ends = count - 1
        head = lax.slice_in_dim(cells, 0, width, axis=dim)
        tail = lax.slice_in_dim(cells, cells.shape[dim] - width, cells.shape[dim], axis=dim)
        cells = jnp.concatenate(
            [
                lax.ppermute(tail, axis, [(i, (i + 1) % count) for i in range(ends)]),
                cells,
                lax.ppermute(head, axis, [((i + 1) % count, i) for i in range(ends)]),
            ],
            axis=dim,
        )
    return cells


def neighbor(values, axis_extent, offset, filler):
    length = values.shape[axis_extent]
    edge_shape = list(values.shape)
    edge_shape[axis_extent] = abs(offset)
    border = jnp.full(edge_shape, filler, values.dtype)
    if offset > 0:
        inside = lax.slice_in_dim(values, offset, length, axis=axis_extent)
        return jnp.concatenate([inside, border], axis=axis_extent)
    inside = lax.slice_in_dim(values, 0, length + offset, axis=axis_extent)
    return jnp.concatenate([border, inside], axis=axis_extent)


def film_table(classes):
    total = jnp.zeros(classes.shape, jnp.float32)
    for number in range(4):
        total = total + top_films[number] * (classes == number).astype(jnp.float32)
    return total


def material_fields(saved_temp, substrate_top, deposit_top, z_index):
    substrate = z_index < substrate_top[None]
    active = z_index < deposit_top[None]
    ones_field = jnp.ones_like(saved_temp)
    capacity = jnp.where(substrate, ones_field, 0.6 * ones_field)
    base = jnp.where(substrate, ones_field, 0.45 * ones_field)
    conduct = jnp.where(
        active, base * (0.5 + jax.nn.sigmoid(saved_temp)), jnp.zeros_like(saved_temp)
    )
    return (capacity, conduct)


def band(conduct_before, conduct, conduct_after, capacity, film_line):
    flux_low = jnp.minimum(conduct_before, conduct)
    flux_high = jnp.minimum(conduct, conduct_after)
    main_diagonal = capacity + step_ratio * (flux_low + flux_high + film_line)
    return (-step_ratio * flux_low, main_diagonal, -step_ratio * flux_high)


def parallel_cyclic_reduction(
    lower_diagonal, main_diagonal, upper_diagonal, right_hand_vector, axis_extent
):
    length = main_diagonal.shape[axis_extent]
    for level_bit in range((length - 1).bit_length()):
        stride = 1 << level_bit
        main_before = neighbor(main_diagonal, axis_extent, -stride, 1.0)
        main_after = neighbor(main_diagonal, axis_extent, stride, 1.0)
        factor_low = -lower_diagonal / main_before
        factor_high = -upper_diagonal / main_after
        new_main = (
            main_diagonal
            + factor_low * neighbor(upper_diagonal, axis_extent, -stride, 0.0)
            + factor_high * neighbor(lower_diagonal, axis_extent, stride, 0.0)
        )
        right_hand_vector = (
            right_hand_vector
            + factor_low * neighbor(right_hand_vector, axis_extent, -stride, 0.0)
            + factor_high * neighbor(right_hand_vector, axis_extent, stride, 0.0)
        )
        lower_diagonal = factor_low * neighbor(lower_diagonal, axis_extent, -stride, 0.0)
        upper_diagonal = factor_high * neighbor(upper_diagonal, axis_extent, stride, 0.0)
        main_diagonal = new_main
    return right_hand_vector / main_diagonal


def line_solve(pieces, axis_extent):
    right_hand_piece, conduct_piece, capacity_piece = pieces
    line_cells = right_hand_piece.shape[axis_extent]
    position = lax.broadcasted_iota(jnp.int32, right_hand_piece.shape, axis_extent)
    film_line = side_film * ((position == 0) | (position == line_cells - 1)).astype(jnp.float32)
    band_triple = band(
        neighbor(conduct_piece, axis_extent, -1, 0.0),
        conduct_piece,
        neighbor(conduct_piece, axis_extent, 1, 0.0),
        capacity_piece,
        film_line,
    )
    return parallel_cyclic_reduction(
        band_triple[0], band_triple[1], band_triple[2], right_hand_piece, axis_extent
    )


def body(cotangent, saved_temp, substrate_top, deposit_top, top_class):
    depth_cells, rows_x, cols_y = cotangent.shape
    first_y = lax.axis_index("gy") * cols_y
    full_y = cols_y * lax.axis_size("gy")
    z_index = lax.broadcasted_iota(jnp.int32, (depth_cells, 1, 1), 0)
    y_index = lax.broadcasted_iota(jnp.int32, (1, 1, cols_y), 2) + first_y
    capacity, conduct = material_fields(saved_temp, substrate_top, deposit_top, z_index)
    film_z = bottom_film * (z_index == 0).astype(jnp.float32) + film_table(top_class)[None] * (
        z_index == deposit_top[None] - 1
    ).astype(jnp.float32)
    film_y = side_film * ((y_index == 0) | (y_index == full_y - 1)).astype(jnp.float32)
    depth_band = band(
        neighbor(conduct, 0, -1, 0.0), conduct, neighbor(conduct, 0, 1, 0.0), capacity, film_z
    )
    scaled_third = parallel_cyclic_reduction(
        depth_band[0], depth_band[1], depth_band[2], cotangent, 0
    )
    adjoint_three = capacity * scaled_third
    solved_y = line_solve(
        (
            lax.all_to_all(adjoint_three, "gy", split_axis=0, concat_axis=2, tiled=True),
            lax.all_to_all(conduct, "gy", split_axis=0, concat_axis=2, tiled=True),
            lax.all_to_all(capacity, "gy", split_axis=0, concat_axis=2, tiled=True),
        ),
        2,
    )
    adjoint_two = capacity * lax.all_to_all(solved_y, "gy", split_axis=2, concat_axis=0, tiled=True)
    solved_x = line_solve(
        (
            lax.all_to_all(adjoint_two, "gx", split_axis=0, concat_axis=1, tiled=True),
            lax.all_to_all(conduct, "gx", split_axis=0, concat_axis=1, tiled=True),
            lax.all_to_all(capacity, "gx", split_axis=0, concat_axis=1, tiled=True),
        ),
        1,
    )
    scaled_one = lax.all_to_all(solved_x, "gx", split_axis=1, concat_axis=0, tiled=True)
    rim_cells = extended(jnp.stack([scaled_one, conduct]), (("gy", 3),), 1)
    s_before = rim_cells[0, :, :, :-2]
    s_after = rim_cells[0, :, :, 2:]
    k_before = rim_cells[1, :, :, :-2]
    k_after = rim_cells[1, :, :, 2:]
    grad_source = capacity * scaled_one
    flux_low_y = jnp.minimum(k_before, conduct)
    flux_high_y = jnp.minimum(conduct, k_after)
    lateral = (
        flux_low_y * (s_before - scaled_one)
        + flux_high_y * (s_after - scaled_one)
        - film_y * scaled_one
    )
    flux_low_z = jnp.minimum(neighbor(conduct, 0, -1, 0.0), conduct)
    flux_high_z = jnp.minimum(conduct, neighbor(conduct, 0, 1, 0.0))
    vertical = (
        flux_low_z * (neighbor(scaled_one, 0, -1, 0.0) - scaled_one)
        + flux_high_z * (neighbor(scaled_one, 0, 1, 0.0) - scaled_one)
        - film_z * scaled_one
    )
    grad_temp = (
        2.0 * grad_source - 2.0 * adjoint_two + cotangent + 2.0 * step_ratio * (lateral + vertical)
    )
    return (grad_temp, grad_source)


def solution(mesh):
    in_specs = (
        P(None, "gx", "gy"),
        P(None, "gx", "gy"),
        P("gx", "gy"),
        P("gx", "gy"),
        P("gx", "gy"),
    )
    out_specs = (P(None, "gx", "gy"), P(None, "gx", "gy"))
    return jax.shard_map(body, mesh=mesh, in_specs=in_specs, out_specs=out_specs, check_vma=False)
```

profile of v0, /device:TPU:1, one launch (start us, length us, event | category | flops | bytes accessed | tf_op | source)
XLA Modules:
  0.0 155.0 jit_solution(5579515328025429708)
XLA Ops:
  0.7 0.7 broadcast_add_fusion
  1.4 1.8 %multiply_select_fusion = f32[64,8,128]{2,1,0:T(8,128)} fusion(f32[64,8,128]{2,1,0:T(8,128)} %param.6, s32[8,128]{1,0:T(8,128)} %param.8, s32[8,128]{1,0:T(8,128)} %param.7), kind=kLoop, calls=%fused_computation.163 | loop fusion | flops 589824 | bytes 532480 | tf_op jit(solution)/shard_map/jit(_where)/select_n | solution.py:54
  3.2 1.1 fusion.104
  4.3 0.7 select_add_fusion.2
  5.0 1.8 %fusion.13 = (f32[64,8,128]{2,1,0:T(8,128)}, f32[64,8,128]{2,1,0:T(8,128)S(1)}) fusion(s32[8,128]{1,0:T(8,128)} %param.7, f32[8,128]{1,0:T(8,128)S(1)} %select_add_fusion.2, s32[8,128]{1,0:T(8,128)S(1)} %broadcast_add_fusion, f32[64]{0:T(128)S(1)} %compare_select_fusion, f32[63,8,128]{2,1,0:T(8,128)S(1)} %get-tuple-element.251, ...), kind=kLoop, calls=%fused_computation.166 | loop fusion | flops 1245184 | bytes 1319168 | tf_op jit(solution)/shard_map/jit(_where)/select_n | solution.py:52
  9.7 11.6 %all_to_all.144 = f32[64,8,128]{2,1,0:T(8,128)S(1)} all-to-all(f32[64,8,128]{2,1,0:T(8,128)S(1)} %select_multiply_fusion.2), channel_id=1, replica_groups=mesh['gx'=16,'gy'=8] {'gy'}, dimensions={0} | all-to-all | bytes 524288 | tf_op jit(solution)/shard_map/all_to_all | solution.py:130
  21.3 3.4 %all-to-all-start.2 = ((f32[64,8,128]{2,1,0:T(8,128)}), f32[64,8,128]{2,1,0:T(8,128)S(1)}, u32[]{:S(2)}, u32[]{:S(2)}) async-start(f32[64,8,128]{2,1,0:T(8,128)} %get-tuple-element.255), calls=%async_computation.2 | async-start | bytes 524288 | tf_op jit(solution)/shard_map/all_to_all | solution.py:132
  24.9 5.5 %all-to-all-done.2 = f32[64,8,128]{2,1,0:T(8,128)S(1)} async-done(((f32[64,8,128]{2,1,0:T(8,128)}), f32[64,8,128]{2,1,0:T(8,128)S(1)}, u32[]{:S(2)}, u32[]{:S(2)}) %all-to-all-start.2) | async-done | bytes 262176 | tf_op jit(solution)/shard_map/all_to_all | solution.py:132
  30.5 3.4 %all-to-all-start.1 = ((f32[64,8,128]{2,1,0:T(8,128)}), f32[64,8,128]{2,1,0:T(8,128)S(1)}, u32[]{:S(2)}, u32[]{:S(2)}) async-start(f32[64,8,128]{2,1,0:T(8,128)} %multiply_select_fusion), calls=%async_computation.1 | async-start | bytes 524288 | tf_op jit(solution)/shard_map/all_to_all | solution.py:131
  34.3 5.4 %all-to-all-done.1 = f32[64,8,128]{2,1,0:T(8,128)S(1)} async-done(((f32[64,8,128]{2,1,0:T(8,128)}), f32[64,8,128]{2,1,0:T(8,128)S(1)}, u32[]{:S(2)}, u32[]{:S(2)}) %all-to-all-start.1) | async-done | bytes 262176 | tf_op jit(solution)/shard_map/all_to_all | solution.py:131
  39.6 12.1 %all-to-all-start.5 = ((f32[64,8,128]{2,1,0:T(8,128)}), f32[64,8,128]{2,1,0:T(8,128)S(1)}, u32[]{:S(2)}, u32[]{:S(2)}) async-start(f32[64,8,128]{2,1,0:T(8,128)} %multiply_select_fusion), calls=%async_computation.5 | async-start | bytes 524288 | tf_op jit(solution)/shard_map/all_to_all | solution.py:140
  54.7 0.4 multiply_add_fusion.25
  57.0 0.4 multiply_add_fusion.21
  61.5 2.7 %copy.22 = f32[8,8,1024]{1,0,2:T(8,128)} copy(f32[8,8,1024]{2,1,0:T(8,128)S(1)} %add_divide_fusion.1) | data formatting | bytes 524288 | tf_op jit(solution)/shard_map/div | solution.py:90
  64.2 4.4 %reshape.30 = f32[8,1,8192]{2,1,0:T(1,128)} reshape(f32[1024,8,8]{2,1,0:T(8,128)} %bitcast.103) | data formatting | bytes 524288
  68.6 3.4 %all-to-all-start.3 = ((f32[8,1,8192]{2,1,0:T(1,128)}), f32[8,1,8192]{2,1,0:T(1,128)S(1)}, u32[]{:S(2)}, u32[]{:S(2)}) async-start(f32[8,1,8192]{2,1,0:T(1,128)} %reshape.30), calls=%async_computation.3 | async-start | bytes 524288 | tf_op jit(solution)/shard_map/all_to_all | solution.py:136
  72.1 6.5 %all-to-all-done.3 = f32[8,1,8192]{2,1,0:T(1,128)S(1)} async-done(((f32[8,1,8192]{2,1,0:T(1,128)}), f32[8,1,8192]{2,1,0:T(1,128)S(1)}, u32[]{:S(2)}, u32[]{:S(2)}) %all-to-all-start.3) | async-done | bytes 262176 | tf_op jit(solution)/shard_map/all_to_all | solution.py:136
  78.5 8.1 %all-to-all-start.6 = ((f32[64,8,128]{2,1,0:T(8,128)}), f32[64,8,128]{2,1,0:T(8,128)S(1)}, u32[]{:S(2)}, u32[]{:S(2)}) async-start(f32[64,8,128]{2,1,0:T(8,128)} %get-tuple-element.255), calls=%async_computation.6 | async-start | bytes 524288 | tf_op jit(solution)/shard_map/all_to_all | solution.py:141
  86.7 0.5 broadcast.556
  87.2 1.3 reduce
  88.5 4.3 %reshape.31 = f32[1024,8,8]{2,1,0:T(8,128)} reshape(f32[8,8192]{1,0:T(8,128)S(1)} %reduce) | data formatting | bytes 524288
  92.8 2.8 %copy.24 = f32[8,8,8,128]{3,2,1,0:T(8,128)S(1)} copy(f32[8,8,8,128]{2,1,3,0:T(8,128)} %bitcast.104) | data formatting | bytes 524288 | tf_op jit(solution)/shard_map/all_to_all | solution.py:136
  95.6 0.7 select_multiply_fusion.1
  96.3 7.2 %all-to-all-start.4 = ((f32[64,8,128]{2,1,0:T(8,128)}), f32[64,8,128]{2,1,0:T(8,128)S(1)}, u32[]{:S(2)}, u32[]{:S(2)}) async-start(f32[64,8,128]{2,1,0:T(8,128)} %select_multiply_fusion.1), calls=%async_computation.4 | async-start | bytes 524288 | tf_op jit(solution)/shard_map/all_to_all | solution.py:139
  103.7 8.5 %all-to-all-done.4 = f32[64,8,128]{2,1,0:T(8,128)S(1)} async-done(((f32[64,8,128]{2,1,0:T(8,128)}), f32[64,8,128]{2,1,0:T(8,128)S(1)}, u32[]{:S(2)}, u32[]{:S(2)}) %all-to-all-start.4) | async-done | bytes 262176 | tf_op jit(solution)/shard_map/all_to_all | solution.py:139
  115.8 0.9 copy.28
  116.7 4.2 %all-to-all-start.7 = ((f32[4,128,128]{2,0,1:T(4,128)}), f32[4,128,128]{2,0,1:T(4,128)S(1)}, u32[]{:S(2)}, u32[]{:S(2)}) async-start(f32[4,128,128]{2,0,1:T(4,128)} %copy.28), calls=%async_computation.7 | async-start | bytes 524288 | tf_op jit(solution)/shard_map/all_to_all | solution.py:145
  121.0 8.7 %all-to-all-done.7 = f32[4,128,128]{2,0,1:T(4,128)S(1)} async-done(((f32[4,128,128]{2,0,1:T(4,128)}), f32[4,128,128]{2,0,1:T(4,128)S(1)}, u32[]{:S(2)}, u32[]{:S(2)}) %all-to-all-start.7) | async-done | bytes 262176 | tf_op jit(solution)/shard_map/all_to_all | solution.py:145
  130.0 2.2 %collective-permute-start = (f32[2,64,8,1]{3,2,1,0:T(8,128)S(1)}, f32[2,64,8,1]{3,2,1,0:T(8,128)S(1)}, u32[]{:S(2)}, u32[]{:S(2)}) collective-permute-start(f32[2,64,8,1]{3,2,1,0:T(8,128)S(1)} %get-tuple-element.64), channel_id=1, source_target_pairs={{0,1},{1,2},{2,3},{3,4},{4,5},{5,6},{6,7},{8,9},{9,10},{10,11},{11... | collective-permute-start | bytes 12296 | tf_op jit(solution)/shard_map/ppermute | solution.py:20
  132.2 1.3 collective-permute-start.1
  133.6 20.2 %collective-permute-done = f32[2,64,8,1]{3,2,1,0:T(8,128)S(1)} collective-permute-done((f32[2,64,8,1]{3,2,1,0:T(8,128)S(1)}, f32[2,64,8,1]{3,2,1,0:T(8,128)S(1)}, u32[]{:S(2)}, u32[]{:S(2)}) %collective-permute-start) | collective-permute-done | bytes 4128 | tf_op jit(solution)/shard_map/ppermute | solution.py:20
  153.7 1.3 fusion.7
  (164 shorter events, 15.7 us)
Async XLA Ops:
  0.6 6.3 %copy-start.3 = (s32[8,128]{1,0:T(8,128)S(1)}, s32[8,128]{1,0:T(8,128)}, u32[]{:S(2)}) copy-start(s32[8,128]{1,0:T(8,128)} %param.8) | copy-start | bytes 12292
  0.6 6.3 %copy-start = (f32[64,8,128]{2,1,0:T(8,128)S(1)}, f32[64,8,128]{2,1,0:T(8,128)}, u32[]{:S(2)}) copy-start(f32[64,8,128]{2,1,0:T(8,128)} %param.6) | copy-start | bytes 786436
  0.7 6.3 %copy-start.2 = (s32[8,128]{1,0:T(8,128)S(1)}, s32[8,128]{1,0:T(8,128)}, u32[]{:S(2)}) copy-start(s32[8,128]{1,0:T(8,128)} %param.7) | copy-start | bytes 12292
  0.7 6.2 %copy-start.1 = (f32[64,8,128]{2,1,0:T(8,128)S(1)}, f32[64,8,128]{2,1,0:T(8,128)}, u32[]{:S(2)}) copy-start(f32[64,8,128]{2,1,0:T(8,128)} %param.5) | copy-start | bytes 786436
  21.3 9.2 %all-to-all-start.2 = ((f32[64,8,128]{2,1,0:T(8,128)}), f32[64,8,128]{2,1,0:T(8,128)S(1)}, u32[]{:S(2)}, u32[]{:S(2)}) async-start(f32[64,8,128]{2,1,0:T(8,128)} %get-tuple-element.255), calls=%async_computation.2 | async-start | bytes 524288 | tf_op jit(solution)/shard_map/all_to_all | solution.py:132
  30.5 9.1 %all-to-all-start.1 = ((f32[64,8,128]{2,1,0:T(8,128)}), f32[64,8,128]{2,1,0:T(8,128)S(1)}, u32[]{:S(2)}, u32[]{:S(2)}) async-start(f32[64,8,128]{2,1,0:T(8,128)} %multiply_select_fusion), calls=%async_computation.1 | async-start | bytes 524288 | tf_op jit(solution)/shard_map/all_to_all | solution.py:131
  39.6 29.0 %all-to-all-start.5 = ((f32[64,8,128]{2,1,0:T(8,128)}), f32[64,8,128]{2,1,0:T(8,128)S(1)}, u32[]{:S(2)}, u32[]{:S(2)}) async-start(f32[64,8,128]{2,1,0:T(8,128)} %multiply_select_fusion), calls=%async_computation.5 | async-start | bytes 524288 | tf_op jit(solution)/shard_map/all_to_all | solution.py:140
  68.6 9.9 %all-to-all-start.3 = ((f32[8,1,8192]{2,1,0:T(1,128)}), f32[8,1,8192]{2,1,0:T(1,128)S(1)}, u32[]{:S(2)}, u32[]{:S(2)}) async-start(f32[8,1,8192]{2,1,0:T(1,128)} %reshape.30), calls=%async_computation.3 | async-start | bytes 524288 | tf_op jit(solution)/shard_map/all_to_all | solution.py:136
  78.5 17.8 %all-to-all-start.6 = ((f32[64,8,128]{2,1,0:T(8,128)}), f32[64,8,128]{2,1,0:T(8,128)S(1)}, u32[]{:S(2)}, u32[]{:S(2)}) async-start(f32[64,8,128]{2,1,0:T(8,128)} %get-tuple-element.255), calls=%async_computation.6 | async-start | bytes 524288 | tf_op jit(solution)/shard_map/all_to_all | solution.py:141
  96.3 15.9 %all-to-all-start.4 = ((f32[64,8,128]{2,1,0:T(8,128)}), f32[64,8,128]{2,1,0:T(8,128)S(1)}, u32[]{:S(2)}, u32[]{:S(2)}) async-start(f32[64,8,128]{2,1,0:T(8,128)} %select_multiply_fusion.1), calls=%async_computation.4 | async-start | bytes 524288 | tf_op jit(solution)/shard_map/all_to_all | solution.py:139
  116.7 13.0 %all-to-all-start.7 = ((f32[4,128,128]{2,0,1:T(4,128)}), f32[4,128,128]{2,0,1:T(4,128)S(1)}, u32[]{:S(2)}, u32[]{:S(2)}) async-start(f32[4,128,128]{2,0,1:T(4,128)} %copy.28), calls=%async_computation.7 | async-start | bytes 524288 | tf_op jit(solution)/shard_map/all_to_all | solution.py:145
  130.0 23.8 %collective-permute-start = (f32[2,64,8,1]{3,2,1,0:T(8,128)S(1)}, f32[2,64,8,1]{3,2,1,0:T(8,128)S(1)}, u32[]{:S(2)}, u32[]{:S(2)}) collective-permute-start(f32[2,64,8,1]{3,2,1,0:T(8,128)S(1)} %get-tuple-element.64), channel_id=1, source_target_pairs={{0,1},{1,2},{2,3},{3,4},{4,5},{5,6},{6,7},{8,9},{9,10},{10,11},{11... | collective-permute-start | bytes 12296 | tf_op jit(solution)/shard_map/ppermute | solution.py:20
  132.2 21.5 %collective-permute-start.1 = (f32[2,64,8,1]{3,2,1,0:T(8,128)S(1)}, f32[2,64,8,1]{3,2,1,0:T(8,128)S(1)}, u32[]{:S(2)}, u32[]{:S(2)}) collective-permute-start(f32[2,64,8,1]{3,2,1,0:T(8,128)S(1)} %get-tuple-element.65), channel_id=1, source_target_pairs={{1,0},{2,1},{3,2},{4,3},{5,4},{6,5},{7,6},{9,8},{10,9},{11,10},{12... | collective-permute-start | bytes 12296 | tf_op jit(solution)/shard_map/ppermute | solution.py:22
where the time goes:
time: 158 us; the launch traced here: 155 us
  waiting for transfers between devices  54.8 us (35%)
  starting transfers between devices  45.5 us (29%)
  local copies, waits for them, and re-layouts  23.2 us (15%)
  other arithmetic  18.3 us (12%)
  blocking collectives  11.6 us (7%)
  between operations  1.73 us (1%)
    ppermute x1, waiting for transfers between devices, extended(): lax.ppermute(tail, axis, [(i, (i + 1) % count) for i in range(ends)])  20.2 us
    all_to_all x1, starting transfers between devices, body(): lax.all_to_all(conduct, 'gx', split_axis=0, concat_axis=1, tiled=True)  12.1 us
    all_to_all x1, blocking collectives, body(): lax.all_to_all(adjoint_three, 'gy', split_axis=0, concat_axis=2, tiled=True)  11.6 us
    unnamed x10, local copies, waits for them, and re-layouts  8.77 us
    all_to_all x1, waiting for transfers between devices, body(): lax.all_to_all(solved_x, 'gx', split_axis=1, concat_axis=0, tiled=True)  8.66 us
    all_to_all x1, waiting for transfers between devices, body(): lax.all_to_all(adjoint_two, 'gx', split_axis=0, concat_axis=1, tiled=True)  8.54 us
    all_to_all x1, starting transfers between devices, body(): lax.all_to_all(capacity, 'gx', split_axis=0, concat_axis=1, tiled=True)  8.13 us
    all_to_all x1, starting transfers between devices, body(): lax.all_to_all(adjoint_two, 'gx', split_axis=0, concat_axis=1, tiled=True)  7.23 us
  transfers between devices with their start and end apart: 9, of which 6 were waited for; matrix products, arithmetic and copies ran while one was open for 17% of the time, Pallas kernels for 0%

commit v1 on v0

v1 whole, which is shorter than its diff:
```python
import functools

import jax
import jax.numpy as jnp
from jax import lax
from jax.experimental import pallas as pl
from jax.experimental.pallas import tpu as pltpu
from jax.sharding import PartitionSpec as P

R = 1000.0
SIDE = 0.3
BOTTOM = 0.5
TOPS = (0.05, 0.25, 0.8, 2.0)
F32 = jnp.float32
NLEV = 6


def recip(v):
    return 1.0 / v


def reduce_chain(c, s, d, track):
    levels, port, ties = [], None, []
    while len(s) > 1:
        half = len(s) // 2
        ml, mr, dv = [], [], []
        for j in range(half):
            i = 2 * j
            total = s[i] + c[i]
            if j:
                total = total + c[i - 1]
            inv = recip(total)
            mr.append(c[i] * inv)
            ml.append(c[i - 1] * inv if j else None)
            dv.append(d[i] * inv)
            if track and j == 0:
                if port is None:
                    port = [dv[0], inv, mr[0]]
                    ties.append(inv)
                else:
                    p, z, t = port
                    tie = t * inv
                    ties.append(tie)
                    port = [p + t * dv[0], z + t * tie, t * mr[0]]
        ns, nd, nc = [], [], []
        for j in range(half):
            e, o = 2 * j, 2 * j + 1
            sv = s[o] + mr[j] * s[e]
            dn = d[o] + mr[j] * d[e]
            if j + 1 < half:
                sv = sv + ml[j + 1] * s[e + 2]
                dn = dn + ml[j + 1] * d[e + 2]
                nc.append(ml[j + 1] * c[e + 2])
            ns.append(sv)
            nd.append(dn)
        levels.append((dv, ml, mr))
        c, s, d = nc, ns, nd
    return s[0], d[0], levels, port, ties


def expand_chain(u_last, levels, ties, flux):
    u = [u_last]
    for lev in range(len(levels) - 1, -1, -1):
        dv, ml, mr = levels[lev]
        out = []
        for j in range(len(u)):
            even = dv[j] + mr[j] * u[j]
            if j:
                even = even + ml[j] * u[j - 1]
            elif ties is not None:
                even = even + ties[lev] * flux
            out += [even, u[j]]
        u = out
    return u


def merge_ports(a, b):
    kfa, kla, za, ta, ga, pa, qa = a
    kfb, klb, zb, tb, gb, pb, qb = b
    link = R * jnp.minimum(kla, kfb)
    lk = link * recip(1.0 + link * zb)
    inv = recip(ga + lk)
    h = inv * (qa + lk * pb)
    ti = ta * inv
    lt = lk * tb
    w = lt * inv
    merged = (
        kfa,
        klb,
        za + ta * ti,
        ta * w,
        gb + lt * tb * (ga * inv),
        pa + ta * h,
        qb + lt * (h - pb),
    )
    return merged, (h, ti, w, lk, pb, tb)


def descend(saved, flux, u_b):
    h, ti, w, lk, pb, tb = saved
    u_a = h + ti * flux + w * u_b
    flux_b = lk * (u_a - pb - tb * u_b)
    return u_a, flux_b


def film_top(cls):
    total = jnp.zeros(cls.shape, F32)
    for n in range(4):
        total = total + TOPS[n] * (cls == n).astype(F32)
    return total


def node_order(half, lev):
    base, n = 0, half
    for _ in range(lev):
        base += n
        n //= 2
    return base, n


def put_levels(ref, levels):
    half = len(levels[0][0])
    for lev, triple in enumerate(levels):
        base, n = node_order(half, lev)
        for kind in range(3):
            for j in range(n):
                if triple[kind][j] is not None:
                    ref[kind, base + j] = triple[kind][j]


def get_levels(read, half):
    levels, lev = [], 0
    while half >> lev:
        base, n = node_order(half, lev)
        levels.append(
            tuple([None if kind == 1 and j == 0 else read(kind, base + j) for j in range(n)] for kind in range(3))
        )
        lev += 1
    return levels


def first_kernel(cot, temp, sub, dep, cls, ypack, cond, fac, tie_out, mid, tr):
    me_y = lax.axis_index("gy")
    sub_v, dep_v = sub[...], dep[...]
    top = film_top(cls[...])
    k, cap, s = [], [], []
    for z in range(64):
        under = z < sub_v
        sg = 0.5 + jax.nn.sigmoid(temp[8 * z : 8 * z + 8])
        kz = jnp.where(z < dep_v, jnp.where(under, 1.0, 0.45) * sg, 0.0)
        cond[8 * z : 8 * z + 8] = kz
        k.append(kz)
        cap.append(jnp.where(under, 1.0, 0.6))
        film = top * (dep_v - 1 == z).astype(F32)
        if z == 0:
            film = film + BOTTOM
        s.append(cap[z] + R * film)
    c = [R * jnp.minimum(k[z], k[z + 1]) for z in range(63)] + [None]
    d = [cot[8 * z : 8 * z + 8] for z in range(64)]
    g, q, levels, _, _ = reduce_chain(c, s, d, False)
    u = expand_chain(q * recip(g), levels, None, None)
    for z in range(64):
        tr[8 * z : 8 * z + 8] = cap[z] * u[z]

    def turned(src, dst):
        for pair in range(4):
            rows = jnp.concatenate(
                [src[pl.ds(2 * pair, 64, stride=8), :], src[pl.ds(2 * pair + 1, 64, stride=8), :]], axis=0
            )
            block = jnp.transpose(rows)
            for h in range(2):
                dst[pl.ds(4 * h + pair, 64, stride=8), :] = block[64 * h : 64 * h + 64]

    turned(cond, mid.at[0])
    turned(tr, mid.at[1])

    subf = sub_v.astype(F32)
    for pair in range(4):
        rows = jnp.concatenate(
            [
                jnp.broadcast_to(subf[2 * pair : 2 * pair + 1], (64, 128)),
                jnp.broadcast_to(subf[2 * pair + 1 : 2 * pair + 2], (64, 128)),
            ],
            axis=0,
        )
        block = jnp.transpose(rows)
        for h in range(2):
            mid[2, pl.ds(4 * h + pair, 64, stride=8), :] = block[64 * h : 64 * h + 64]
    z_lane = (lax.broadcasted_iota(jnp.int32, (8, 128), 1) & 63).astype(F32)
    row = lax.broadcasted_iota(jnp.int32, (8, 128), 0)
    ky, sy, dy = [], [], []
    for y in range(64):
        ky.append(mid[0, 8 * y : 8 * y + 8])
        dy.append(mid[1, 8 * y : 8 * y + 8])
        sy.append(jnp.where(z_lane < mid[2, 8 * y : 8 * y + 8], 1.0, 0.6))
    cap_first, cap_last = sy[0][0:4], sy[63][4:8]
    low = jnp.where(me_y == 0, R * SIDE, 0.0)
    high = jnp.where(me_y == 7, R * SIDE, 0.0)
    sy[0] = sy[0] + jnp.where(row < 4, low, 0.0)
    sy[63] = sy[63] + jnp.where(row >= 4, high, 0.0)
    cy = [R * jnp.minimum(ky[y], ky[y + 1]) for y in range(63)] + [None]
    g, q, levels, (p, zz, t), ties = reduce_chain(cy, sy, dy, True)
    put_levels(fac, levels)
    for lev in range(NLEV):
        tie_out[lev] = ties[lev]
    kf, kl = ky[0], ky[63]
    side_a = tuple(v[0:4] for v in (kf, kl, zz, t, g, p, q))
    side_b = tuple(v[4:8] for v in (kf, kl, zz, t, g, p, q))
    merged, saved = merge_ports(side_a, side_b)
    for i, v in enumerate(saved):
        tie_out[NLEV + i, 0:4] = v
    pack = jnp.concatenate(list(merged) + [cap_first, cap_last, jnp.zeros((4, 128), F32)], axis=0)
    for n in range(8):
        ypack[n] = pack


def second_kernel(gat, fac, ties, cond, sub, keep, send, xfac, xhfac, a2_out, kh_out, pick, flat, planes, xp):
    me_y = lax.axis_index("gy")
    me_x = lax.axis_index("gx")
    seg = [[gat[n, 4 * i : 4 * i + 4] for i in range(9)] for n in range(8)]
    gam, rhs = seg[0][4], seg[0][6]
    down, links = [None], [None]
    for n in range(1, 8):
        kf, kl, z, t, g, p, q = seg[n][:7]
        link = R * jnp.minimum(seg[n - 1][1], kf)
        lk = link * recip(1.0 + link * z)
        inv = recip(gam + lk)
        h = inv * (rhs + lk * p)
        lt = lk * t
        down.append((h, lt * inv))
        links.append(lk)
        rhs = q + lt * (h - p)
        gam = g + lt * t * (gam * inv)
    u = [None] * 8
    u[7] = rhs * recip(gam)
    for n in range(7, 0, -1):
        u[n - 1] = down[n][0] + down[n][1] * u[n]
    zero4 = jnp.zeros((4, 128), F32)
    fl, uf = [zero4], [None]
    for n in range(1, 8):
        kf, kl, z, t, g, p, q = seg[n][:7]
        fl.append(links[n] * (u[n - 1] - p - t * u[n]))
        uf.append(p + z * fl[n] + t * u[n])
    for n in range(8):
        rows = [fl[n], u[n]]
        if n:
            rows += [seg[n - 1][8] * u[n - 1], seg[n - 1][1], seg[n - 1][8]]
        else:
            rows += [zero4, zero4, zero4 + 1.0]
        if n < 7:
            rows += [seg[n + 1][7] * uf[n + 1], seg[n + 1][0], seg[n + 1][7]]
        else:
            rows += [zero4, zero4, zero4 + 1.0]
        for i, v in enumerate(rows):
            pick[n, 4 * i : 4 * i + 4] = v
    mine = [pick[me_y, 4 * i : 4 * i + 4] for i in range(8)]
    flux, u_b = mine[0], mine[1]
    saved = tuple(ties[NLEV + i, 0:4] for i in range(6))
    u_a, flux_b = descend(saved, flux, u_b)
    flux8 = jnp.concatenate([flux, flux_b], axis=0)
    last8 = jnp.concatenate([u_a, u_b], axis=0)
    levels = get_levels(lambda kind, i: fac[kind, i], 32)
    u_nodes = expand_chain(last8, levels, [ties[i] for i in range(NLEV)], flux8)
    for y in range(64):
        flat[8 * y : 8 * y + 8] = u_nodes[y]
    subf = sub[...]
    for pair in range(4):
        block = jnp.transpose(
            jnp.concatenate([flat[pl.ds(pair, 64, stride=8), :], flat[pl.ds(4 + pair, 64, stride=8), :]], axis=0)
        )
        for odd in range(2):
            x = 2 * pair + odd
            planes[x] = block[64 * odd : 64 * odd + 64]

    lane = lax.broadcasted_iota(jnp.int32, (4, 128), 1)

    def both(left, right):
        even = jnp.where(lane < 64, left, pltpu.roll(right, 64, 1))
        odd = jnp.where(lane < 64, pltpu.roll(left, 64, 1), right)
        return [(odd if x & 1 else even)[x // 2 : x // 2 + 1] for x in range(8)]

    dh, kh, caph = both(mine[2], mine[5]), both(mine[3], mine[6]), both(mine[4], mine[7])
    for x in range(8):
        kh_out[x : x + 1] = kh[x]

    low = jnp.where(me_x == 0, R * SIDE, 0.0)
    high = jnp.where(me_x == 15, R * SIDE, 0.0)

    def x_chain(k, cap, d):
        s = list(cap)
        s[0] = s[0] + low
        s[7] = s[7] + high
        c = [R * jnp.minimum(k[x], k[x + 1]) for x in range(7)] + [None]
        g, q, levels, (p, z, t), tie = reduce_chain(c, s, d, True)
        return levels, tie, (k[0], k[7], z, t, g, p, q)

    base_z = lax.broadcasted_iota(jnp.int32, (8, 128), 0)
    for chunk in range(8):
        zi = base_z + 8 * chunk
        k, cap, d = [], [], []
        for x in range(8):
            k.append(cond[pl.ds(64 * chunk + x, 8, stride=8), :])
            cap.append(jnp.where(zi < subf[x : x + 1], 1.0, 0.6))
            dx = cap[x] * planes[x, 8 * chunk : 8 * chunk + 8]
            a2_out[pl.ds(64 * chunk + x, 8, stride=8), :] = dx
            d.append(dx)
        levels, tie, port = x_chain(k, cap, d)
        store_x(xfac.at[chunk], levels, tie)
        for i in range(7):
            xp[i, 8 * chunk : 8 * chunk + 8] = port[i]
    levels, tie, port = x_chain(kh, caph, dh)
    store_x(xhfac, levels, tie)
    core = lax.rem(me_x, 2)
    for i in range(7):
        keep[32 * i : 32 * i + 32] = xp[i, pl.ds(pl.multiple_of(32 * core, 32), 32), :]
        send[32 * i : 32 * i + 32] = xp[i, pl.ds(pl.multiple_of(32 - 32 * core, 32), 32), :]
    tile = jnp.concatenate(list(port) + [jnp.zeros((1, 128), F32)], axis=0)
    keep[224:232] = tile
    send[224:232] = tile


def store_x(ref, levels, tie):
    for lev, triple in enumerate(levels):
        base, n = node_order(4, lev)
        for kind in range(3):
            for j in range(n):
                if triple[kind][j] is not None:
                    ref[7 * kind + base + j] = triple[kind][j]
    for lev in range(3):
        ref[21 + lev] = tie[lev]


def load_x(ref):
    levels = get_levels(lambda kind, i: ref[7 * kind + i], 4)
    return levels, [ref[21 + lev] for lev in range(3)]


def read_pack(ref, n):
    main = tuple(ref[32 * i : 32 * i + 32] for i in range(n))
    edge = tuple(ref[32 * n + i : 32 * n + i + 1] for i in range(n))
    return main, edge


def write_pack(ref, main, edge):
    n = len(main)
    for i in range(n):
        ref[32 * i : 32 * i + 32] = main[i]
        ref[32 * n + i : 32 * n + i + 1] = edge[i]


def order(right, mine, theirs):
    a = tuple(jnp.where(right, t, m) for m, t in zip(mine, theirs))
    b = tuple(jnp.where(right, m, t) for m, t in zip(mine, theirs))
    return a, b


def merge_kernel(bit, last, mine, theirs, merged_out, saved_out, *rest):
    me_x = lax.axis_index("gx")
    right = lax.rem(lax.div(me_x, bit), 2) == 1
    m, t = read_pack(mine, 7), read_pack(theirs, 7)
    done = []
    for part in range(2):
        a, b = order(right, m[part], t[part])
        done.append(merge_ports(a, b))
    write_pack(merged_out, done[0][0], done[1][0])
    write_pack(saved_out, done[0][1], done[1][1])
    if last:
        far = lax.div(me_x, 8) == 1
        outs = []
        for part in range(2):
            kf, kl, z, tt, g, p, q = done[part][0]
            gi = recip(g)
            tg = tt * gi
            outs.append(
                (
                    jnp.where(far, z + tt * tg, g),
                    jnp.where(far, p + tg * q, q),
                    jnp.where(far, kf, kl),
                )
            )
        write_pack(rest[0], outs[0], outs[1])


def top_kernel(merged, near, theirs, sv1, sv2, sv3, own, send):
    me_x = lax.axis_index("gx")
    far = lax.div(me_x, 8) == 1
    mm = read_pack(merged, 7)
    n, t = read_pack(near, 3), read_pack(theirs, 3)
    saved = [read_pack(r, 6) for r in (sv1, sv2, sv3)]
    final = []
    for part in range(2):
        (ga, qa, ka), (zb, pb, kb) = order(far, n[part], t[part])
        link = R * jnp.minimum(ka, kb)
        lk = link * recip(1.0 + link * zb)
        u_a = (qa + lk * pb) * recip(ga + lk)
        kf, kl, z, tt, g, p, q = mm[part]
        flux = jnp.where(far, lk * (u_a - pb), 0.0)
        u = jnp.where(far, (q + tt * flux) * recip(g), u_a)
        for bit, lev in ((4, 2), (2, 1)):
            right = lax.rem(lax.div(me_x, bit), 2) == 1
            ua, fb = descend(saved[lev][part], flux, u)
            flux = jnp.where(right, fb, flux)
            u = jnp.where(right, u, ua)
        ua, fb = descend(saved[0][part], flux, u)
        odd = lax.rem(me_x, 2) == 1
        final.append((jnp.where(odd, fb, flux), jnp.where(odd, u, ua), jnp.where(odd, flux, fb), jnp.where(odd, ua, u)))
    write_pack(own, final[0][:2], final[1][:2])
    send[0:32] = final[0][2]
    send[32:64] = final[0][3]


def last_kernel(own, got, xfac, xhfac, kh, cond, a2, cot, sub, dep, cls, temp_out, src_out, s1, fu):
    me_x = lax.axis_index("gx")
    me_y = lax.axis_index("gy")
    core = lax.rem(me_x, 2)
    for i in range(2):
        fu[i, pl.ds(pl.multiple_of(32 * core, 32), 32), :] = own[32 * i : 32 * i + 32]
        fu[i, pl.ds(pl.multiple_of(32 - 32 * core, 32), 32), :] = got[32 * i : 32 * i + 32]
    for chunk in range(8):
        levels, tie = load_x(xfac.at[chunk])
        u = expand_chain(fu[1, 8 * chunk : 8 * chunk + 8], levels, tie, fu[0, 8 * chunk : 8 * chunk + 8])
        for x in range(8):
            s1[pl.ds(64 * chunk + x, 8, stride=8), :] = u[x]
    levels, tie = load_x(xhfac)
    uh = jnp.concatenate(expand_chain(own[65:66], levels, tie, own[64:65]), axis=0)
    kh_v = kh[...]
    sub_v, dep_v = sub[...], dep[...]
    top = film_top(cls[...])
    lane = lax.broadcasted_iota(jnp.int32, (8, 128), 1)
    first, final = lane == 0, lane == 127
    film_y = jnp.where(first & (me_y == 0), SIDE, 0.0) + jnp.where(final & (me_y == 7), SIDE, 0.0)
    up = None
    for z in range(64):
        rows = slice(8 * z, 8 * z + 8)
        s, k = s1[rows], cond[rows]
        s_r = jnp.where(final, pltpu.roll(uh, 63 - z, 1), pltpu.roll(s, 127, 1))
        k_r = jnp.where(final, pltpu.roll(kh_v, 63 - z, 1), pltpu.roll(k, 127, 1))
        s_l = pltpu.roll(uh, (128 - z) % 128, 1) if z else uh
        k_l = pltpu.roll(kh_v, (128 - z) % 128, 1) if z else kh_v
        f_y = jnp.minimum(k, k_r) * (s_r - s)
        f_l = jnp.minimum(k, k_l) * (s - s_l)
        total = f_y - jnp.where(first, f_l, pltpu.roll(f_y, 1, 1))
        film = film_y + top * (dep_v - 1 == z).astype(F32)
        if z == 0:
            film = film + BOTTOM
        if z < 63:
            nxt = slice(8 * z + 8, 8 * z + 16)
            f_z = jnp.minimum(k, cond[nxt]) * (s1[nxt] - s)
            total = total + f_z
        if z:
            total = total - up
        up = f_z
        total = total - film * s
        src = jnp.where(z < sub_v, 1.0, 0.6) * s
        src_out[rows] = src
        temp_out[rows] = 2.0 * src - 2.0 * a2[rows] + cot[rows] + (2.0 * R) * total


def call(kernel, outs, scratch, name, *args):
    vmem = pl.BlockSpec(memory_space=pltpu.VMEM)
    return pl.pallas_call(
        kernel,
        out_shape=[jax.ShapeDtypeStruct(s, F32) for s in outs],
        in_specs=[vmem] * len(args),
        out_specs=[vmem] * len(outs),
        scratch_shapes=[pltpu.VMEM(s, F32) for s in scratch],
        compiler_params=pltpu.CompilerParams(vmem_limit_bytes=40 * 1024 * 1024),
        name=name,
    )(*args)


def swap(v, bit):
    return lax.ppermute(v, "gx", [(i, i ^ bit) for i in range(16)])


def body(cotangent, saved_temp, substrate_top, deposit_top, top_class):
    cot = cotangent.reshape(512, 128)
    temp = saved_temp.reshape(512, 128)
    ypack, cond, fac, ties = call(
        first_kernel,
        [(8, 40, 128), (512, 128), (3, 63, 8, 128), (12, 8, 128)],
        [(3, 512, 128), (512, 128)],
        "first",
        cot, temp, substrate_top, deposit_top, top_class,
    )
    gat = lax.all_to_all(ypack, "gy", split_axis=0, concat_axis=0, tiled=True)
    keep, send, xfac, xhfac, a2, kh = call(
        second_kernel,
        [(232, 128), (232, 128), (8, 24, 8, 128), (24, 1, 128), (512, 128), (8, 128)],
        [(8, 32, 128), (512, 128), (8, 64, 128), (7, 64, 128)],
        "second",
        gat, fac, ties, cond, substrate_top,
    )
    m1, sv1 = call(functools.partial(merge_kernel, 1, False), [(232, 128), (200, 128)], [], "merge_core", keep, swap(send, 1))
    m2, sv2 = call(functools.partial(merge_kernel, 2, False), [(232, 128), (200, 128)], [], "merge_near", m1, swap(m1, 2))
    m3, sv3, near = call(
        functools.partial(merge_kernel, 4, True), [(232, 128), (200, 128), (104, 128)], [], "merge_far", m2, swap(m2, 6)
    )
    own, out = call(top_kernel, [(72, 128), (64, 128)], [], "top", m3, near, swap(near, 8), sv1, sv2, sv3)
    got = swap(out, 1)
    grad_temp, grad_source = call(
        last_kernel,
        [(512, 128), (512, 128)],
        [(512, 128), (2, 64, 128)],
        "last",
        own, got, xfac, xhfac, kh, cond, a2, cot, substrate_top, deposit_top, top_class,
    )
    return grad_temp.reshape(cotangent.shape), grad_source.reshape(cotangent.shape)


def solution(mesh):
    in_specs = (
        P(None, "gx", "gy"),
        P(None, "gx", "gy"),
        P("gx", "gy"),
        P("gx", "gy"),
        P("gx", "gy"),
    )
    out_specs = (P(None, "gx", "gy"), P(None, "gx", "gy"))
    return jax.shard_map(body, mesh=mesh, in_specs=in_specs, out_specs=out_specs, check_vma=False)
```

time: 158 us -> 44.4 us (0.28); the launches traced: 155 us -> 44.1 us
  waiting for transfers between devices: 54.8 us -> 9.07 us
  starting transfers between devices: 45.5 us -> 13.4 us
  local copies, waits for them, and re-layouts: 23.2 us -> 4.65 us
  other arithmetic: 18.3 us -> 0 us
  Pallas kernels: 0 us -> 5.25 us
    all_to_all x7 -> x0, starting transfers between devices: 42 us -> none  [the longest x1 12.1 us: body(): lax.all_to_all(conduct, 'gx', split_axis=0, concat_axis=1, tiled=True)]
    all_to_all x7 -> x0, waiting for transfers between devices: 34.6 us -> none  [the longest x1 8.66 us: body(): lax.all_to_all(solved_x, 'gx', split_axis=1, concat_axis=0, tiled=True)]
    ppermute x2 -> x5, waiting for transfers between devices: 20.2 us -> 9.07 us  [swap(): return lax.ppermute(v, 'gx', [(i, i ^ bit) for i in range(16)])]
    add x41 -> x0, other arithmetic: 10.7 us -> none  [the longest x20 5.48 us: parallel_cyclic_reduction(): right_hand_vector + factor_low * neighbor(right_hand_vector, axis_extent,...]
    ppermute x2 -> x5, starting transfers between devices: 3.54 us -> 13.4 us  [swap(): return lax.ppermute(v, 'gx', [(i, i ^ bit) for i in range(16)])]
    slice x95 -> x0, local copies, waits for them, and re-layouts: 6.88 us -> none  [the longest x48 4.05 us: neighbor(): inside = lax.slice_in_dim(values, offset, length, axis=axis_extent)]
    pallas_call x0 -> x7, Pallas kernels: none -> 5.25 us  [call(): pl.pallas_call(kernel, out_shape=[jax.ShapeDtypeStruct(s, F32) for s in o...]
    unnamed x10 -> x18, local copies, waits for them, and re-layouts: 8.77 us -> 4.65 us
  transfers between devices with their start and end apart: 9 -> 5, of which waited for: 6 -> 5; matrix products, arithmetic and copies ran while one was open for 17% -> 0% of each run, Pallas kernels for 0% -> 0%
where the time goes in v1:
time: 44.4 us; the launch traced here: 44.1 us
  starting transfers between devices  13.4 us (30%)
  blocking collectives  11.1 us (25%)
  waiting for transfers between devices  9.07 us (20%)
  Pallas kernels  5.25 us (12%)
  local copies, waits for them, and re-layouts  4.65 us (10%)
  between operations  0.68 us (2%)
    ppermute x5, starting transfers between devices, swap(): return lax.ppermute(v, 'gx', [(i, i ^ bit) for i in range(16)])  13.4 us
    all_to_all x1, blocking collectives, body(): gat = lax.all_to_all(ypack, 'gy', split_axis=0, concat_axis=0, tiled=True)  11.1 us
    ppermute x5, waiting for transfers between devices, swap(): return lax.ppermute(v, 'gx', [(i, i ^ bit) for i in range(16)])  9.07 us
    pallas_call x7, Pallas kernels, call(): pl.pallas_call(kernel, out_shape=[jax.ShapeDtypeStruct(s, F32) for s in o...  5.25 us
    unnamed x18, local copies, waits for them, and re-layouts  4.65 us
  transfers between devices with their start and end apart: 5, of which 5 were waited for; matrix products, arithmetic and copies ran while one was open for 0% of the time, Pallas kernels for 0%

profile of v1, /device:TPU:1, one launch (start us, length us, event | category | flops | bytes accessed | tf_op | source)
XLA Modules:
  0.0 44.1 jit_solution(4413334017672487779)
XLA Ops:
  0.6 0.0 copy-start
  0.6 0.9 %copy-done = f32[64,8,128]{2,1,0:T(8,128)S(1)} copy-done((f32[64,8,128]{2,1,0:T(8,128)S(1)}, f32[64,8,128]{2,1,0:T(8,128)}, u32[]{:S(2)}) %copy-start) | copy-done | bytes 262168
  1.6 0.0 copy-start.2
  1.6 0.9 %copy-done.2 = f32[64,8,128]{2,1,0:T(8,128)S(1)} copy-done((f32[64,8,128]{2,1,0:T(8,128)S(1)}, f32[64,8,128]{2,1,0:T(8,128)}, u32[]{:S(2)}) %copy-start.2) | copy-done | bytes 262168
  2.5 0.0 copy-start.3
  2.5 0.7 %copy-done.3 = s32[8,128]{1,0:T(8,128)S(1)} copy-done((s32[8,128]{1,0:T(8,128)S(1)}, s32[8,128]{1,0:T(8,128)}, u32[]{:S(2)}) %copy-start.3) | copy-done | bytes 4120
  3.2 0.0 copy-start.5
  3.2 0.7 %copy-done.5 = s32[8,128]{1,0:T(8,128)S(1)} copy-done((s32[8,128]{1,0:T(8,128)S(1)}, s32[8,128]{1,0:T(8,128)}, u32[]{:S(2)}) %copy-start.5) | copy-done | bytes 4120
  3.9 0.0 copy-start.7
  3.9 0.7 %copy-done.7 = s32[8,128]{1,0:T(8,128)S(1)} copy-done((s32[8,128]{1,0:T(8,128)S(1)}, s32[8,128]{1,0:T(8,128)}, u32[]{:S(2)}) %copy-start.7) | copy-done | bytes 4120
  4.6 0.7 %first.1 = (f32[8,40,128]{2,1,0:T(8,128)S(1)}, f32[512,128]{1,0:T(8,128)S(1)}, f32[3,63,8,128]{3,2,1,0:T(8,128)S(1)}, f32[12,8,128]{2,1,0:T(8,128)S(1)}) custom-call(f32[512,128]{1,0:T(8,128)S(1)} %bitcast.4, f32[512,128]{1,0:T(8,128)S(1)} %bitcast.6, s32[8,128]{1,0:T(8,128)S(1)} %copy-done.3, s32[8,128]{1,0:T(8,128)S(1)} %copy-done.5, s32[8,128]{1,0:T(8,128)S(1)} %copy-done.7), custom_call_target="tpu_custom_call" | custom-call | tf_op jit(solution)/shard_map/first/pallas_call | solution.py:461
  5.3 11.1 %all_to_all.5.gat = f32[8,40,128]{2,1,0:T(8,128)S(1)} all-to-all(f32[8,40,128]{2,1,0:T(8,128)S(1)} %get-tuple-element.23), channel_id=1, replica_groups=mesh['gx'=16,'gy'=8] {'gy'}, dimensions={0} | all-to-all | bytes 327680 | tf_op jit(solution)/shard_map/all_to_all | solution.py:486
  16.4 0.4 %second.1 = (f32[232,128]{1,0:T(8,128)S(1)}, f32[232,128]{1,0:T(8,128)S(1)}, f32[8,24,8,128]{3,2,1,0:T(8,128)S(1)}, f32[24,1,128]{2,1,0:T(1,128)S(1)}, f32[512,128]{1,0:T(8,128)S(1)}, /*index=5*/f32[8,128]{1,0:T(8,128)S(1)}) custom-call(f32[8,40,128]{2,1,0:T(8,128)S(1)} %all_to_all.5.gat, f32[3,63,8,128]{3,2,1,0:T(8,128)S(1)} %get-tuple-element.24.fac, ...), custom_call_target="tpu_custom_call" | custom-call | tf_op jit(solution)/shard_map/second/pallas_call | solution.py:461
  16.8 2.2 %collective-permute-start = (f32[232,128]{1,0:T(8,128)S(1)}, f32[232,128]{1,0:T(8,128)S(1)}, u32[]{:S(2)}, u32[]{:S(2)}) collective-permute-start(f32[232,128]{1,0:T(8,128)S(1)} %get-tuple-element.28), channel_id=1, source_target_pairs={{0,8},{8,0},{16,24},{24,16},{32,40},{40,32},{48,56},{56,48},{64,72... | collective-permute-start | bytes 356360 | tf_op jit(solution)/shard_map/ppermute | solution.py:473
  19.0 1.0 %collective-permute-done.theirs = f32[232,128]{1,0:T(8,128)S(1)} collective-permute-done((f32[232,128]{1,0:T(8,128)S(1)}, f32[232,128]{1,0:T(8,128)S(1)}, u32[]{:S(2)}, u32[]{:S(2)}) %collective-permute-start) | collective-permute-done | bytes 118816 | tf_op jit(solution)/shard_map/ppermute | solution.py:473
  20.0 1.7 %collective-permute-start.1 = (f32[232,128]{1,0:T(8,128)S(1)}, f32[232,128]{1,0:T(8,128)S(1)}, u32[]{:S(2)}, u32[]{:S(2)}) collective-permute-start(f32[232,128]{1,0:T(8,128)S(1)} %get-tuple-element.29.mine), channel_id=1, source_target_pairs={{0,16},{8,24},{16,0},{24,8},{32,48},{40,56},{48,32},{56,40},{64,80... | collective-permute-start | bytes 356360 | tf_op jit(solution)/shard_map/ppermute | solution.py:473
  21.7 3.1 %collective-permute-done.1.theirs = f32[232,128]{1,0:T(8,128)S(1)} collective-permute-done((f32[232,128]{1,0:T(8,128)S(1)}, f32[232,128]{1,0:T(8,128)S(1)}, u32[]{:S(2)}, u32[]{:S(2)}) %collective-permute-start.1) | collective-permute-done | bytes 118816 | tf_op jit(solution)/shard_map/ppermute | solution.py:473
  24.9 3.5 %collective-permute-start.2 = (f32[232,128]{1,0:T(8,128)S(1)}, f32[232,128]{1,0:T(8,128)S(1)}, u32[]{:S(2)}, u32[]{:S(2)}) collective-permute-start(f32[232,128]{1,0:T(8,128)S(1)} %get-tuple-element.30.mine), channel_id=1, source_target_pairs={{0,48},{8,56},{16,32},{24,40},{32,16},{40,24},{48,0},{56,8},{64,11... | collective-permute-start | bytes 356360 | tf_op jit(solution)/shard_map/ppermute | solution.py:473
  28.4 2.2 %collective-permute-done.2.theirs = f32[232,128]{1,0:T(8,128)S(1)} collective-permute-done((f32[232,128]{1,0:T(8,128)S(1)}, f32[232,128]{1,0:T(8,128)S(1)}, u32[]{:S(2)}, u32[]{:S(2)}) %collective-permute-start.2) | collective-permute-done | bytes 118816 | tf_op jit(solution)/shard_map/ppermute | solution.py:473
  30.6 0.1 merge_far.1
  30.7 2.7 %collective-permute-start.3 = (f32[104,128]{1,0:T(8,128)S(1)}, f32[104,128]{1,0:T(8,128)S(1)}, u32[]{:S(2)}, u32[]{:S(2)}) collective-permute-start(f32[104,128]{1,0:T(8,128)S(1)} %get-tuple-element.32.near), channel_id=1, source_target_pairs={{0,64},{8,72},{16,80},{24,88},{32,96},{40,104},{48,112},{56,120},{... | collective-permute-start | bytes 159752 | tf_op jit(solution)/shard_map/ppermute | solution.py:473
  33.4 1.9 %collective-permute-done.3.theirs = f32[104,128]{1,0:T(8,128)S(1)} collective-permute-done((f32[104,128]{1,0:T(8,128)S(1)}, f32[104,128]{1,0:T(8,128)S(1)}, u32[]{:S(2)}, u32[]{:S(2)}) %collective-permute-start.3) | collective-permute-done | bytes 53280 | tf_op jit(solution)/shard_map/ppermute | solution.py:473
  35.2 0.0 copy-start.1
  35.2 0.0 copy-start.8
  35.2 0.1 top.1
  35.3 3.3 %collective-permute-start.4 = (f32[64,128]{1,0:T(8,128)S(1)}, f32[64,128]{1,0:T(8,128)S(1)}, u32[]{:S(2)}, u32[]{:S(2)}) collective-permute-start(f32[64,128]{1,0:T(8,128)S(1)} %get-tuple-element.37), channel_id=1, source_target_pairs={{0,8},{8,0},{16,24},{24,16},{32,40},{40,32},{48,56},{56,48},{64,72... | collective-permute-start | bytes 98312 | tf_op jit(solution)/shard_map/ppermute | solution.py:473
  38.6 0.9 %collective-permute-done.4.got = f32[64,128]{1,0:T(8,128)S(1)} collective-permute-done((f32[64,128]{1,0:T(8,128)S(1)}, f32[64,128]{1,0:T(8,128)S(1)}, u32[]{:S(2)}, u32[]{:S(2)}) %collective-permute-start.4) | collective-permute-done | bytes 32800 | tf_op jit(solution)/shard_map/ppermute | solution.py:473
  39.5 0.0 copy-done.1
  39.5 0.0 copy-done.8
  39.5 0.7 %copy-done.6 = s32[8,128]{1,0:T(8,128)S(1)} copy-done((s32[8,128]{1,0:T(8,128)S(1)}, s32[8,128]{1,0:T(8,128)}, u32[]{:S(2)}) %copy-start.6) | copy-done | bytes 4120
  40.2 0.0 copy-done.4
  40.2 3.9 %last.1 = (f32[512,128]{1,0:T(8,128)}, f32[512,128]{1,0:T(8,128)}) custom-call(f32[72,128]{1,0:T(8,128)S(1)} %get-tuple-element.36.own, f32[64,128]{1,0:T(8,128)S(1)} %collective-permute-done.4.got, f32[8,24,8,128]{3,2,1,0:T(8,128)S(1)} %get-tuple-element.38.xfac, f32[24,1,128]{2,1,0:T(1,128)S(1)} %get-tuple-element.39.xhfac, ...), custom_call_target="tpu_custom_call" | custom-call | tf_op jit(solution)/shard_map/last/pallas_call | solution.py:461
  (4 shorter events, 0.1 us)
Async XLA Ops:
  0.6 1.0 %copy-start = (f32[64,8,128]{2,1,0:T(8,128)S(1)}, f32[64,8,128]{2,1,0:T(8,128)}, u32[]{:S(2)}) copy-start(f32[64,8,128]{2,1,0:T(8,128)} %param.5) | copy-start | bytes 786436
  1.6 0.9 %copy-start.2 = (f32[64,8,128]{2,1,0:T(8,128)S(1)}, f32[64,8,128]{2,1,0:T(8,128)}, u32[]{:S(2)}) copy-start(f32[64,8,128]{2,1,0:T(8,128)} %param.6) | copy-start | bytes 786436
  2.5 0.7 %copy-start.3 = (s32[8,128]{1,0:T(8,128)S(1)}, s32[8,128]{1,0:T(8,128)}, u32[]{:S(2)}) copy-start(s32[8,128]{1,0:T(8,128)} %sub.5) | copy-start | bytes 12292
  3.2 0.7 %copy-start.5 = (s32[8,128]{1,0:T(8,128)S(1)}, s32[8,128]{1,0:T(8,128)}, u32[]{:S(2)}) copy-start(s32[8,128]{1,0:T(8,128)} %dep.3) | copy-start | bytes 12292
  3.9 0.7 %copy-start.7 = (s32[8,128]{1,0:T(8,128)S(1)}, s32[8,128]{1,0:T(8,128)}, u32[]{:S(2)}) copy-start(s32[8,128]{1,0:T(8,128)} %cls.3) | copy-start | bytes 12292
  16.8 3.1 %collective-permute-start = (f32[232,128]{1,0:T(8,128)S(1)}, f32[232,128]{1,0:T(8,128)S(1)}, u32[]{:S(2)}, u32[]{:S(2)}) collective-permute-start(f32[232,128]{1,0:T(8,128)S(1)} %get-tuple-element.28), channel_id=1, source_target_pairs={{0,8},{8,0},{16,24},{24,16},{32,40},{40,32},{48,56},{56,48},{64,72... | collective-permute-start | bytes 356360 | tf_op jit(solution)/shard_map/ppermute | solution.py:473
  20.0 4.9 %collective-permute-start.1 = (f32[232,128]{1,0:T(8,128)S(1)}, f32[232,128]{1,0:T(8,128)S(1)}, u32[]{:S(2)}, u32[]{:S(2)}) collective-permute-start(f32[232,128]{1,0:T(8,128)S(1)} %get-tuple-element.29.mine), channel_id=1, source_target_pairs={{0,16},{8,24},{16,0},{24,8},{32,48},{40,56},{48,32},{56,40},{64,80... | collective-permute-start | bytes 356360 | tf_op jit(solution)/shard_map/ppermute | solution.py:473
  24.9 5.7 %collective-permute-start.2 = (f32[232,128]{1,0:T(8,128)S(1)}, f32[232,128]{1,0:T(8,128)S(1)}, u32[]{:S(2)}, u32[]{:S(2)}) collective-permute-start(f32[232,128]{1,0:T(8,128)S(1)} %get-tuple-element.30.mine), channel_id=1, source_target_pairs={{0,48},{8,56},{16,32},{24,40},{32,16},{40,24},{48,0},{56,8},{64,11... | collective-permute-start | bytes 356360 | tf_op jit(solution)/shard_map/ppermute | solution.py:473
  30.7 4.6 %collective-permute-start.3 = (f32[104,128]{1,0:T(8,128)S(1)}, f32[104,128]{1,0:T(8,128)S(1)}, u32[]{:S(2)}, u32[]{:S(2)}) collective-permute-start(f32[104,128]{1,0:T(8,128)S(1)} %get-tuple-element.32.near), channel_id=1, source_target_pairs={{0,64},{8,72},{16,80},{24,88},{32,96},{40,104},{48,112},{56,120},{... | collective-permute-start | bytes 159752 | tf_op jit(solution)/shard_map/ppermute | solution.py:473
  35.2 4.3 %copy-start.1 = (f32[64,8,128]{2,1,0:T(8,128)S(1)}, f32[64,8,128]{2,1,0:T(8,128)}, u32[]{:S(2)}) copy-start(f32[64,8,128]{2,1,0:T(8,128)} %param.5) | copy-start | bytes 786436
  35.2 4.3 %copy-start.8 = (s32[8,128]{1,0:T(8,128)S(1)}, s32[8,128]{1,0:T(8,128)}, u32[]{:S(2)}) copy-start(s32[8,128]{1,0:T(8,128)} %cls.3) | copy-start | bytes 12292
  35.3 4.2 %collective-permute-start.4 = (f32[64,128]{1,0:T(8,128)S(1)}, f32[64,128]{1,0:T(8,128)S(1)}, u32[]{:S(2)}, u32[]{:S(2)}) collective-permute-start(f32[64,128]{1,0:T(8,128)S(1)} %get-tuple-element.37), channel_id=1, source_target_pairs={{0,8},{8,0},{16,24},{24,16},{32,40},{40,32},{48,56},{56,48},{64,72... | collective-permute-start | bytes 98312 | tf_op jit(solution)/shard_map/ppermute | solution.py:473
  39.5 0.7 %copy-start.6 = (s32[8,128]{1,0:T(8,128)S(1)}, s32[8,128]{1,0:T(8,128)}, u32[]{:S(2)}) copy-start(s32[8,128]{1,0:T(8,128)} %dep.3) | copy-start | bytes 12292
  39.5 0.7 %copy-start.4 = (s32[8,128]{1,0:T(8,128)S(1)}, s32[8,128]{1,0:T(8,128)}, u32[]{:S(2)}) copy-start(s32[8,128]{1,0:T(8,128)} %sub.5) | copy-start | bytes 12292

commit v2 on v1

--- a/solution.py
+++ b/solution.py
@@ -139,8 +139,16 @@
     return levels
 
 
-def first_kernel(cot, temp, sub, dep, cls, ypack, cond, fac, tie_out, mid, tr):
+def first_kernel(
+    cot_in, temp_in, sub_in, dep_in, cls_in, ypack, cond, fac, tie_out, cot, sub, dep, cls, temp, mid, tr, sems
+):
     me_y = lax.axis_index("gy")
+    pairs = ((sub_in, sub), (dep_in, dep), (temp_in, temp), (cls_in, cls), (cot_in, cot))
+    copies = [pltpu.make_async_copy(a, b, sems.at[i]) for i, (a, b) in enumerate(pairs)]
+    for cp in copies:
+        cp.start()
+    for cp in copies[:4]:
+        cp.wait()
     sub_v, dep_v = sub[...], dep[...]
     top = film_top(cls[...])
     k, cap, s = [], [], []
@@ -156,6 +164,7 @@
             film = film + BOTTOM
         s.append(cap[z] + R * film)
     c = [R * jnp.minimum(k[z], k[z + 1]) for z in range(63)] + [None]
+    copies[4].wait()
     d = [cot[8 * z : 8 * z + 8] for z in range(64)]
     g, q, levels, _, _ = reduce_chain(c, s, d, False)
     u = expand_chain(q * recip(g), levels, None, None)
@@ -214,7 +223,7 @@
         ypack[n] = pack
 
 
-def second_kernel(gat, fac, ties, cond, sub, keep, send, xfac, xhfac, a2_out, kh_out, pick, flat, planes, xp):
+def second_kernel(gat, fac, ties, cond, sub, xpack, xfac, xhfac, a2_out, kh_out, pick, flat, planes):
     me_y = lax.axis_index("gy")
     me_x = lax.axis_index("gx")
     seg = [[gat[n, 4 * i : 4 * i + 4] for i in range(9)] for n in range(8)]
@@ -307,16 +316,11 @@
         levels, tie, port = x_chain(k, cap, d)
         store_x(xfac.at[chunk], levels, tie)
         for i in range(7):
-            xp[i, 8 * chunk : 8 * chunk + 8] = port[i]
+            xpack[64 * i + 8 * chunk : 64 * i + 8 * chunk + 8] = port[i]
     levels, tie, port = x_chain(kh, caph, dh)
     store_x(xhfac, levels, tie)
-    core = lax.rem(me_x, 2)
     for i in range(7):
-        keep[32 * i : 32 * i + 32] = xp[i, pl.ds(pl.multiple_of(32 * core, 32), 32), :]
-        send[32 * i : 32 * i + 32] = xp[i, pl.ds(pl.multiple_of(32 - 32 * core, 32), 32), :]
-    tile = jnp.concatenate(list(port) + [jnp.zeros((1, 128), F32)], axis=0)
-    keep[224:232] = tile
-    send[224:232] = tile
+        xpack[448 + i : 449 + i] = port[i]
 
 
 def store_x(ref, levels, tie):
@@ -336,16 +340,16 @@
 
 
 def read_pack(ref, n):
-    main = tuple(ref[32 * i : 32 * i + 32] for i in range(n))
-    edge = tuple(ref[32 * n + i : 32 * n + i + 1] for i in range(n))
+    main = tuple(ref[64 * i : 64 * i + 64] for i in range(n))
+    edge = tuple(ref[64 * n + i : 64 * n + i + 1] for i in range(n))
     return main, edge
 
 
 def write_pack(ref, main, edge):
     n = len(main)
     for i in range(n):
-        ref[32 * i : 32 * i + 32] = main[i]
-        ref[32 * n + i : 32 * n + i + 1] = edge[i]
+        ref[64 * i : 64 * i + 64] = main[i]
+        ref[64 * n + i : 64 * n + i + 1] = edge[i]
 
 
 def order(right, mine, theirs):
@@ -402,34 +406,32 @@
             flux = jnp.where(right, fb, flux)
             u = jnp.where(right, u, ua)
         ua, fb = descend(saved[0][part], flux, u)
-        odd = lax.rem(me_x, 2) == 1
-        final.append((jnp.where(odd, fb, flux), jnp.where(odd, u, ua), jnp.where(odd, flux, fb), jnp.where(odd, ua, u)))
-    write_pack(own, final[0][:2], final[1][:2])
-    send[0:32] = final[0][2]
-    send[32:64] = final[0][3]
-
-
-def last_kernel(own, got, xfac, xhfac, kh, cond, a2, cot, sub, dep, cls, temp_out, src_out, s1, fu):
+        final.append(((fb, u), (flux, ua)))
+    write_pack(own, final[0][0], final[1][0])
+    write_pack(send, final[0][1], final[1][1])
+
+
+def last_kernel(
+    own, got, xfac, xhfac, kh, cond, a2, cot, sub, dep, cls, temp_out, src_out, s1, fu, t_buf, s_buf, sems
+):
     me_x = lax.axis_index("gx")
     me_y = lax.axis_index("gy")
-    core = lax.rem(me_x, 2)
-    for i in range(2):
-        fu[i, pl.ds(pl.multiple_of(32 * core, 32), 32), :] = own[32 * i : 32 * i + 32]
-        fu[i, pl.ds(pl.multiple_of(32 - 32 * core, 32), 32), :] = got[32 * i : 32 * i + 32]
+    odd = lax.rem(me_x, 2) == 1
+    fu[...] = jnp.where(odd, own[...], got[...])
     for chunk in range(8):
         levels, tie = load_x(xfac.at[chunk])
-        u = expand_chain(fu[1, 8 * chunk : 8 * chunk + 8], levels, tie, fu[0, 8 * chunk : 8 * chunk + 8])
+        u = expand_chain(fu[64 + 8 * chunk : 72 + 8 * chunk], levels, tie, fu[8 * chunk : 8 * chunk + 8])
         for x in range(8):
             s1[pl.ds(64 * chunk + x, 8, stride=8), :] = u[x]
     levels, tie = load_x(xhfac)
-    uh = jnp.concatenate(expand_chain(own[65:66], levels, tie, own[64:65]), axis=0)
+    uh = jnp.concatenate(expand_chain(fu[129:130], levels, tie, fu[128:129]), axis=0)
     kh_v = kh[...]
     sub_v, dep_v = sub[...], dep[...]
     top = film_top(cls[...])
     lane = lax.broadcasted_iota(jnp.int32, (8, 128), 1)
     first, final = lane == 0, lane == 127
     film_y = jnp.where(first & (me_y == 0), SIDE, 0.0) + jnp.where(final & (me_y == 7), SIDE, 0.0)
-    up = None
+    up, copies = None, []
     for z in range(64):
         rows = slice(8 * z, 8 * z + 8)
         s, k = s1[rows], cond[rows]
@@ -452,58 +454,78 @@
         up = f_z
         total = total - film * s
         src = jnp.where(z < sub_v, 1.0, 0.6) * s
-        src_out[rows] = src
-        temp_out[rows] = 2.0 * src - 2.0 * a2[rows] + cot[rows] + (2.0 * R) * total
-
-
-def call(kernel, outs, scratch, name, *args):
-    vmem = pl.BlockSpec(memory_space=pltpu.VMEM)
+        s_buf[rows] = src
+        t_buf[rows] = 2.0 * src - 2.0 * a2[rows] + cot[rows] + (2.0 * R) * total
+        if z & 7 == 7:
+            part = slice(8 * z - 56, 8 * z + 8)
+            for i, (buf, out) in enumerate(((s_buf, src_out), (t_buf, temp_out))):
+                cp = pltpu.make_async_copy(buf.at[part], out.at[part], sems.at[2 * (z // 8) + i])
+                cp.start()
+                copies.append(cp)
+    for cp in copies:
+        cp.wait()
+
+
+VMEM = pl.BlockSpec(memory_space=pltpu.VMEM)
+HBM = pl.BlockSpec(memory_space=pltpu.MemorySpace.HBM)
+
+
+def call(kernel, outs, scratch, name, *args, far_in=0, far_out=0, sems=0):
+    shapes = [s if isinstance(s, jax.ShapeDtypeStruct) else jax.ShapeDtypeStruct(s, F32) for s in outs]
+    scr = [pltpu.VMEM(s, F32) for s in scratch]
+    args = [pltpu.with_memory_space_constraint(a, pltpu.MemorySpace.HBM) if i < far_in else a for i, a in enumerate(args)]
+    if sems:
+        scr.append(pltpu.SemaphoreType.DMA((sems,)))
     return pl.pallas_call(
         kernel,
-        out_shape=[jax.ShapeDtypeStruct(s, F32) for s in outs],
-        in_specs=[vmem] * len(args),
-        out_specs=[vmem] * len(outs),
-        scratch_shapes=[pltpu.VMEM(s, F32) for s in scratch],
+        out_shape=shapes,
+        in_specs=[HBM if i < far_in else VMEM for i in range(len(args))],
+        out_specs=[HBM if i < far_out else VMEM for i in range(len(outs))],
+        scratch_shapes=scr,
         compiler_params=pltpu.CompilerParams(vmem_limit_bytes=40 * 1024 * 1024),
         name=name,
     )(*args)
 
 
 def swap(v, bit):
-    return lax.ppermute(v, "gx", [(i, i ^ bit) for i in range(16)])
+    return lax.ppermute(v, "gx", [(i, i ^ bit) for i in range(1, 16, 2)])
 
 
 def body(cotangent, saved_temp, substrate_top, deposit_top, top_class):
     cot = cotangent.reshape(512, 128)
     temp = saved_temp.reshape(512, 128)
-    ypack, cond, fac, ties = call(
+    small = jax.ShapeDtypeStruct((8, 128), jnp.int32)
+    ypack, cond, fac, ties, cot, sub, dep, cls = call(
         first_kernel,
-        [(8, 40, 128), (512, 128), (3, 63, 8, 128), (12, 8, 128)],
-        [(3, 512, 128), (512, 128)],
+        [(8, 40, 128), (512, 128), (3, 63, 8, 128), (12, 8, 128), (512, 128), small, small, small],
+        [(512, 128), (3, 512, 128), (512, 128)],
         "first",
         cot, temp, substrate_top, deposit_top, top_class,
+        far_in=5, sems=5,
     )
     gat = lax.all_to_all(ypack, "gy", split_axis=0, concat_axis=0, tiled=True)
-    keep, send, xfac, xhfac, a2, kh = call(
+    xpack, xfac, xhfac, a2, kh = call(
         second_kernel,
-        [(232, 128), (232, 128), (8, 24, 8, 128), (24, 1, 128), (512, 128), (8, 128)],
-        [(8, 32, 128), (512, 128), (8, 64, 128), (7, 64, 128)],
+        [(456, 128), (8, 24, 8, 128), (24, 1, 128), (512, 128), (8, 128)],
+        [(8, 32, 128), (512, 128), (8, 64, 128)],
         "second",
-        gat, fac, ties, cond, substrate_top,
+        gat, fac, ties, cond, sub,
     )
-    m1, sv1 = call(functools.partial(merge_kernel, 1, False), [(232, 128), (200, 128)], [], "merge_core", keep, swap(send, 1))
-    m2, sv2 = call(functools.partial(merge_kernel, 2, False), [(232, 128), (200, 128)], [], "merge_near", m1, swap(m1, 2))
+    other = lax.ppermute(xpack, "gx", [(i, i + 1) for i in range(0, 16, 2)])
+    m1, sv1 = call(functools.partial(merge_kernel, 1, False), [(456, 128), (392, 128)], [], "merge_core", xpack, other)
+    m2, sv2 = call(functools.partial(merge_kernel, 2, False), [(456, 128), (392, 128)], [], "merge_near", m1, swap(m1, 2))
     m3, sv3, near = call(
-        functools.partial(merge_kernel, 4, True), [(232, 128), (200, 128), (104, 128)], [], "merge_far", m2, swap(m2, 6)
+        functools.partial(merge_kernel, 4, True), [(456, 128), (392, 128), (200, 128)], [], "merge_far", m2, swap(m2, 6)
     )
-    own, out = call(top_kernel, [(72, 128), (64, 128)], [], "top", m3, near, swap(near, 8), sv1, sv2, sv3)
-    got = swap(out, 1)
+    own, out = call(top_kernel, [(136, 128), (136, 128)], [], "top", m3, near, swap(near, 8), sv1, sv2, sv3)
+    got = lax.ppermute(out, "gx", [(i + 1, i) for i in range(0, 16, 2)])
     grad_temp, grad_source = call(
         last_kernel,
         [(512, 128), (512, 128)],
-        [(512, 128), (2, 64, 128)],
+        [(512, 128), (136, 128), (512, 128), (512, 128)],
         "last",
-        own, got, xfac, xhfac, kh, cond, a2, cot, substrate_top, deposit_top, top_class,
+        own, got, xfac, xhfac, kh, cond, a2, cot, sub, dep, cls,
+        far_out=2, sems=16,
     )
     return grad_temp.reshape(cotangent.shape), grad_source.reshape(cotangent.shape)
 

time: 44.4 us -> 47.9 us (1.079)
  local copies, waits for them, and re-layouts: 4.65 us -> 0 us
  waiting for transfers between devices: 9.07 us -> 13.2 us
  starting transfers between devices: 13.4 us -> 16.1 us
  Pallas kernels: 5.25 us -> 6.5 us
    unnamed x18 -> x0, local copies, waits for them, and re-layouts: 4.65 us -> none
    ppermute x5, waiting for transfers between devices: 9.07 us -> 13.2 us  [the longest x3 9.25 us: swap(): return lax.ppermute(v, 'gx', [(i, i ^ bit) for i in range(1, 16, 2)])]
    ppermute x5, starting transfers between devices: 13.4 us -> 16.1 us  [the longest x3 13.6 us: swap(): return lax.ppermute(v, 'gx', [(i, i ^ bit) for i in range(1, 16, 2)])]
    pallas_call x7, Pallas kernels: 5.25 us -> 6.5 us  [call(): pl.pallas_call(kernel, out_shape=shapes, in_specs=[HBM if i < far_in else...]
where the time goes in v2:
time: 47.9 us; the launch traced here: 47.6 us
  starting transfers between devices  16.1 us (34%)
  waiting for transfers between devices  13.2 us (28%)
  blocking collectives  11.1 us (23%)
  Pallas kernels  6.5 us (14%)
  between operations  0.7 us (1%)
    ppermute x3, starting transfers between devices, swap(): return lax.ppermute(v, 'gx', [(i, i ^ bit) for i in range(1, 16, 2)])  13.6 us
    all_to_all x1, blocking collectives, body(): gat = lax.all_to_all(ypack, 'gy', split_axis=0, concat_axis=0, tiled=True)  11.1 us
    ppermute x3, waiting for transfers between devices, swap(): return lax.ppermute(v, 'gx', [(i, i ^ bit) for i in range(1, 16, 2)])  9.25 us
    pallas_call x7, Pallas kernels, call(): pl.pallas_call(kernel, out_shape=shapes, in_specs=[HBM if i < far_in else...  6.5 us
    ppermute x1, waiting for transfers between devices, body(): other = lax.ppermute(xpack, 'gx', [(i, i + 1) for i in range(0, 16, 2)])  3.05 us
    ppermute x1, starting transfers between devices, body(): other = lax.ppermute(xpack, 'gx', [(i, i + 1) for i in range(0, 16, 2)])  1.29 us
    ppermute x1, starting transfers between devices, body(): got = lax.ppermute(out, 'gx', [(i + 1, i) for i in range(0, 16, 2)])  1.29 us
  transfers between devices with their start and end apart: 5, of which 5 were waited for; matrix products, arithmetic and copies ran while one was open for 0% of the time, Pallas kernels for 0%

profile of v2, /device:TPU:1, one launch (start us, length us, event | category | flops | bytes accessed | tf_op | source)
XLA Modules:
  0.0 47.6 jit_solution(14975466290263213445)
XLA Ops:
  0.6 1.8 %first.1 = (f32[8,40,128]{2,1,0:T(8,128)S(1)}, f32[512,128]{1,0:T(8,128)S(1)}, f32[3,63,8,128]{3,2,1,0:T(8,128)S(1)}, f32[12,8,128]{2,1,0:T(8,128)S(1)}, f32[512...) custom-call(f32[512,128]{1,0:T(8,128)} %bitcast.4, f32[512,128]{1,0:T(8,128)} %bitcast.5, ...), custom_call_target="tpu_custom_call" | custom-call | tf_op jit(solution)/shard_map/first/pallas_call | solution.py:479
  2.4 11.1 %all_to_all.5.gat = f32[8,40,128]{2,1,0:T(8,128)S(1)} all-to-all(f32[8,40,128]{2,1,0:T(8,128)S(1)} %get-tuple-element.26), channel_id=1, replica_groups=mesh['gx'=16,'gy'=8] {'gy'}, dimensions={0} | all-to-all | bytes 327680 | tf_op jit(solution)/shard_map/all_to_all | solution.py:506
  13.5 0.4 second.1
  13.9 1.3 %collective-permute-start = (f32[456,128]{1,0:T(8,128)S(1)}, f32[456,128]{1,0:T(8,128)S(1)}, u32[]{:S(2)}, u32[]{:S(2)}) collective-permute-start(f32[456,128]{1,0:T(8,128)S(1)} %get-tuple-element.31.mine), channel_id=1, source_target_pairs={{0,8},{16,24},{32,40},{48,56},{64,72},{80,88},{96,104},{112,120},{... | collective-permute-start | bytes 700424 | tf_op jit(solution)/shard_map/ppermute | solution.py:514
  15.2 3.1 %collective-permute-done.theirs = f32[456,128]{1,0:T(8,128)S(1)} collective-permute-done((f32[456,128]{1,0:T(8,128)S(1)}, f32[456,128]{1,0:T(8,128)S(1)}, u32[]{:S(2)}, u32[]{:S(2)}) %collective-permute-start) | collective-permute-done | bytes 233504 | tf_op jit(solution)/shard_map/ppermute | solution.py:514
  18.3 0.1 merge_core.1
  18.3 3.5 %collective-permute-start.1 = (f32[456,128]{1,0:T(8,128)S(1)}, f32[456,128]{1,0:T(8,128)S(1)}, u32[]{:S(2)}, u32[]{:S(2)}) collective-permute-start(f32[456,128]{1,0:T(8,128)S(1)} %get-tuple-element.32.mine), channel_id=1, source_target_pairs={{8,24},{24,8},{40,56},{56,40},{72,88},{88,72},{104,120},{120,104},... | collective-permute-start | bytes 700424 | tf_op jit(solution)/shard_map/ppermute | solution.py:491
  21.9 3.4 %collective-permute-done.1.theirs = f32[456,128]{1,0:T(8,128)S(1)} collective-permute-done((f32[456,128]{1,0:T(8,128)S(1)}, f32[456,128]{1,0:T(8,128)S(1)}, u32[]{:S(2)}, u32[]{:S(2)}) %collective-permute-start.1) | collective-permute-done | bytes 233504 | tf_op jit(solution)/shard_map/ppermute | solution.py:491
  25.3 0.1 merge_near.1
  25.4 5.5 %collective-permute-start.2 = (f32[456,128]{1,0:T(8,128)S(1)}, f32[456,128]{1,0:T(8,128)S(1)}, u32[]{:S(2)}, u32[]{:S(2)}) collective-permute-start(f32[456,128]{1,0:T(8,128)S(1)} %get-tuple-element.33.mine), channel_id=1, source_target_pairs={{8,56},{24,40},{40,24},{56,8},{72,120},{88,104},{104,88},{120,72},... | collective-permute-start | bytes 700424 | tf_op jit(solution)/shard_map/ppermute | solution.py:491
  30.9 3.4 %collective-permute-done.2.theirs = f32[456,128]{1,0:T(8,128)S(1)} collective-permute-done((f32[456,128]{1,0:T(8,128)S(1)}, f32[456,128]{1,0:T(8,128)S(1)}, u32[]{:S(2)}, u32[]{:S(2)}) %collective-permute-start.2) | collective-permute-done | bytes 233504 | tf_op jit(solution)/shard_map/ppermute | solution.py:491
  34.3 0.1 merge_far.1
  34.4 4.5 %collective-permute-start.3 = (f32[200,128]{1,0:T(8,128)S(1)}, f32[200,128]{1,0:T(8,128)S(1)}, u32[]{:S(2)}, u32[]{:S(2)}) collective-permute-start(f32[200,128]{1,0:T(8,128)S(1)} %get-tuple-element.35.near), channel_id=1, source_target_pairs={{8,72},{24,88},{40,104},{56,120},{72,8},{88,24},{104,40},{120,56},... | collective-permute-start | bytes 307208 | tf_op jit(solution)/shard_map/ppermute | solution.py:491
  39.0 2.4 %collective-permute-done.3.theirs = f32[200,128]{1,0:T(8,128)S(1)} collective-permute-done((f32[200,128]{1,0:T(8,128)S(1)}, f32[200,128]{1,0:T(8,128)S(1)}, u32[]{:S(2)}, u32[]{:S(2)}) %collective-permute-start.3) | collective-permute-done | bytes 102432 | tf_op jit(solution)/shard_map/ppermute | solution.py:491
  41.3 0.1 top.1
  41.4 1.3 %collective-permute-start.4 = (f32[136,128]{1,0:T(8,128)S(1)}, f32[136,128]{1,0:T(8,128)S(1)}, u32[]{:S(2)}, u32[]{:S(2)}) collective-permute-start(f32[136,128]{1,0:T(8,128)S(1)} %get-tuple-element.40), channel_id=1, source_target_pairs={{8,0},{24,16},{40,32},{56,48},{72,64},{88,80},{104,96},{120,112},{... | collective-permute-start | bytes 208904 | tf_op jit(solution)/shard_map/ppermute | solution.py:521
  42.7 0.9 %collective-permute-done.4.got = f32[136,128]{1,0:T(8,128)S(1)} collective-permute-done((f32[136,128]{1,0:T(8,128)S(1)}, f32[136,128]{1,0:T(8,128)S(1)}, u32[]{:S(2)}, u32[]{:S(2)}) %collective-permute-start.4) | collective-permute-done | bytes 69664 | tf_op jit(solution)/shard_map/ppermute | solution.py:521
  43.6 4.0 %last.1 = (f32[512,128]{1,0:T(8,128)}, f32[512,128]{1,0:T(8,128)}) custom-call(f32[136,128]{1,0:T(8,128)S(1)} %get-tuple-element.39.own, f32[136,128]{1,0:T(8,128)S(1)} %collective-permute-done.4.got, f32[8,24,8,128]{3,2,1,0:T(8,128)S(1)} %get-tuple-element.41.xfac, f32[24,1,128]{2,1,0:T(1,128)S(1)} %get-tuple-element.42.xhfac, ...), custom_call_target="tpu_custom_call" | custom-call | tf_op jit(solution)/shard_map/last/pallas_call | solution.py:479
Async XLA Ops:
  13.9 4.4 %collective-permute-start = (f32[456,128]{1,0:T(8,128)S(1)}, f32[456,128]{1,0:T(8,128)S(1)}, u32[]{:S(2)}, u32[]{:S(2)}) collective-permute-start(f32[456,128]{1,0:T(8,128)S(1)} %get-tuple-element.31.mine), channel_id=1, source_target_pairs={{0,8},{16,24},{32,40},{48,56},{64,72},{80,88},{96,104},{112,120},{... | collective-permute-start | bytes 700424 | tf_op jit(solution)/shard_map/ppermute | solution.py:514
  18.3 7.0 %collective-permute-start.1 = (f32[456,128]{1,0:T(8,128)S(1)}, f32[456,128]{1,0:T(8,128)S(1)}, u32[]{:S(2)}, u32[]{:S(2)}) collective-permute-start(f32[456,128]{1,0:T(8,128)S(1)} %get-tuple-element.32.mine), channel_id=1, source_target_pairs={{8,24},{24,8},{40,56},{56,40},{72,88},{88,72},{104,120},{120,104},... | collective-permute-start | bytes 700424 | tf_op jit(solution)/shard_map/ppermute | solution.py:491
  25.4 8.9 %collective-permute-start.2 = (f32[456,128]{1,0:T(8,128)S(1)}, f32[456,128]{1,0:T(8,128)S(1)}, u32[]{:S(2)}, u32[]{:S(2)}) collective-permute-start(f32[456,128]{1,0:T(8,128)S(1)} %get-tuple-element.33.mine), channel_id=1, source_target_pairs={{8,56},{24,40},{40,24},{56,8},{72,120},{88,104},{104,88},{120,72},... | collective-permute-start | bytes 700424 | tf_op jit(solution)/shard_map/ppermute | solution.py:491
  34.4 6.9 %collective-permute-start.3 = (f32[200,128]{1,0:T(8,128)S(1)}, f32[200,128]{1,0:T(8,128)S(1)}, u32[]{:S(2)}, u32[]{:S(2)}) collective-permute-start(f32[200,128]{1,0:T(8,128)S(1)} %get-tuple-element.35.near), channel_id=1, source_target_pairs={{8,72},{24,88},{40,104},{56,120},{72,8},{88,24},{104,40},{120,56},... | collective-permute-start | bytes 307208 | tf_op jit(solution)/shard_map/ppermute | solution.py:491
  41.4 2.2 %collective-permute-start.4 = (f32[136,128]{1,0:T(8,128)S(1)}, f32[136,128]{1,0:T(8,128)S(1)}, u32[]{:S(2)}, u32[]{:S(2)}) collective-permute-start(f32[136,128]{1,0:T(8,128)S(1)} %get-tuple-element.40), channel_id=1, source_target_pairs={{8,0},{24,16},{40,32},{56,48},{72,64},{88,80},{104,96},{120,112},{... | collective-permute-start | bytes 208904 | tf_op jit(solution)/shard_map/ppermute | solution.py:521

commit v3 on v2

--- a/solution.py
+++ b/solution.py
@@ -171,31 +171,18 @@
     for z in range(64):
         tr[8 * z : 8 * z + 8] = cap[z] * u[z]
 
-    def turned(src, dst):
-        for pair in range(4):
-            rows = jnp.concatenate(
-                [src[pl.ds(2 * pair, 64, stride=8), :], src[pl.ds(2 * pair + 1, 64, stride=8), :]], axis=0
-            )
-            block = jnp.transpose(rows)
-            for h in range(2):
-                dst[pl.ds(4 * h + pair, 64, stride=8), :] = block[64 * h : 64 * h + 64]
-
-    turned(cond, mid.at[0])
-    turned(tr, mid.at[1])
-
-    subf = sub_v.astype(F32)
-    for pair in range(4):
-        rows = jnp.concatenate(
-            [
-                jnp.broadcast_to(subf[2 * pair : 2 * pair + 1], (64, 128)),
-                jnp.broadcast_to(subf[2 * pair + 1 : 2 * pair + 2], (64, 128)),
-            ],
-            axis=0,
-        )
+    def turned(rows, dst, q):
         block = jnp.transpose(rows)
         for h in range(2):
-            mid[2, pl.ds(4 * h + pair, 64, stride=8), :] = block[64 * h : 64 * h + 64]
-    z_lane = (lax.broadcasted_iota(jnp.int32, (8, 128), 1) & 63).astype(F32)
+            dst[pl.ds(4 * h + q, 64, stride=8), :] = block[64 * h : 64 * h + 64]
+
+    subf = sub_v.astype(F32)
+    upper = (lax.broadcasted_iota(jnp.int32, (128, 128), 0) & 1) == 1
+    for q in range(4):
+        turned(cond[pl.ds(q, 128, stride=4), :], mid.at[0], q)
+        turned(tr[pl.ds(q, 128, stride=4), :], mid.at[1], q)
+        turned(jnp.where(upper, subf[q + 4 : q + 5], subf[q : q + 1]), mid.at[2], q)
+    z_lane = (lax.broadcasted_iota(jnp.int32, (8, 128), 1) >> 1).astype(F32)
     row = lax.broadcasted_iota(jnp.int32, (8, 128), 0)
     ky, sy, dy = [], [], []
     for y in range(64):
@@ -223,7 +210,7 @@
         ypack[n] = pack
 
 
-def second_kernel(gat, fac, ties, cond, sub, xpack, xfac, xhfac, a2_out, kh_out, pick, flat, planes):
+def second_kernel(gat, fac, ties, cond, sub, keep, send, xfac, xhfac, a2_out, kh_out, pick, flat, planes, xp):
     me_y = lax.axis_index("gy")
     me_x = lax.axis_index("gx")
     seg = [[gat[n, 4 * i : 4 * i + 4] for i in range(9)] for n in range(8)]
@@ -273,20 +260,17 @@
     for y in range(64):
         flat[8 * y : 8 * y + 8] = u_nodes[y]
     subf = sub[...]
-    for pair in range(4):
-        block = jnp.transpose(
-            jnp.concatenate([flat[pl.ds(pair, 64, stride=8), :], flat[pl.ds(4 + pair, 64, stride=8), :]], axis=0)
+    for q in range(4):
+        planes[pl.ds(q, 128, stride=4), :] = jnp.transpose(
+            jnp.concatenate([flat[pl.ds(q, 64, stride=8), :], flat[pl.ds(4 + q, 64, stride=8), :]], axis=0)
         )
-        for odd in range(2):
-            x = 2 * pair + odd
-            planes[x] = block[64 * odd : 64 * odd + 64]
-
-    lane = lax.broadcasted_iota(jnp.int32, (4, 128), 1)
+
+    even = (lax.broadcasted_iota(jnp.int32, (4, 128), 1) & 1) == 0
 
     def both(left, right):
-        even = jnp.where(lane < 64, left, pltpu.roll(right, 64, 1))
-        odd = jnp.where(lane < 64, pltpu.roll(left, 64, 1), right)
-        return [(odd if x & 1 else even)[x // 2 : x // 2 + 1] for x in range(8)]
+        low = jnp.where(even, left, pltpu.roll(right, 127, 1))
+        high = jnp.where(even, pltpu.roll(left, 127, 1), pltpu.roll(right, 126, 1))
+        return [low[x : x + 1] for x in range(4)] + [high[x : x + 1] for x in range(4)]
 
     dh, kh, caph = both(mine[2], mine[5]), both(mine[3], mine[6]), both(mine[4], mine[7])
     for x in range(8):
@@ -310,17 +294,21 @@
         for x in range(8):
             k.append(cond[pl.ds(64 * chunk + x, 8, stride=8), :])
             cap.append(jnp.where(zi < subf[x : x + 1], 1.0, 0.6))
-            dx = cap[x] * planes[x, 8 * chunk : 8 * chunk + 8]
+            dx = cap[x] * planes[pl.ds(64 * chunk + x, 8, stride=8), :]
             a2_out[pl.ds(64 * chunk + x, 8, stride=8), :] = dx
             d.append(dx)
         levels, tie, port = x_chain(k, cap, d)
         store_x(xfac.at[chunk], levels, tie)
         for i in range(7):
-            xpack[64 * i + 8 * chunk : 64 * i + 8 * chunk + 8] = port[i]
+            xp[i, 8 * chunk : 8 * chunk + 8] = port[i]
     levels, tie, port = x_chain(kh, caph, dh)
     store_x(xhfac, levels, tie)
+    core = lax.rem(me_x, 2)
     for i in range(7):
-        xpack[448 + i : 449 + i] = port[i]
+        keep[32 * i : 32 * i + 32] = xp[i, pl.ds(pl.multiple_of(32 * core, 32), 32), :]
+        send[32 * i : 32 * i + 32] = xp[i, pl.ds(pl.multiple_of(32 - 32 * core, 32), 32), :]
+        keep[224 + i : 225 + i] = port[i]
+        send[224 + i : 225 + i] = port[i]
 
 
 def store_x(ref, levels, tie):
@@ -340,16 +328,16 @@
 
 
 def read_pack(ref, n):
-    main = tuple(ref[64 * i : 64 * i + 64] for i in range(n))
-    edge = tuple(ref[64 * n + i : 64 * n + i + 1] for i in range(n))
+    main = tuple(ref[32 * i : 32 * i + 32] for i in range(n))
+    edge = tuple(ref[32 * n + i : 32 * n + i + 1] for i in range(n))
     return main, edge
 
 
 def write_pack(ref, main, edge):
     n = len(main)
     for i in range(n):
-        ref[64 * i : 64 * i + 64] = main[i]
-        ref[64 * n + i : 64 * n + i + 1] = edge[i]
+        ref[32 * i : 32 * i + 32] = main[i]
+        ref[32 * n + i : 32 * n + i + 1] = edge[i]
 
 
 def order(right, mine, theirs):
@@ -406,56 +394,74 @@
             flux = jnp.where(right, fb, flux)
             u = jnp.where(right, u, ua)
         ua, fb = descend(saved[0][part], flux, u)
-        final.append(((fb, u), (flux, ua)))
-    write_pack(own, final[0][0], final[1][0])
-    write_pack(send, final[0][1], final[1][1])
-
-
-def last_kernel(
-    own, got, xfac, xhfac, kh, cond, a2, cot, sub, dep, cls, temp_out, src_out, s1, fu, t_buf, s_buf, sems
-):
-    me_x = lax.axis_index("gx")
+        odd = lax.rem(me_x, 2) == 1
+        final.append((jnp.where(odd, fb, flux), jnp.where(odd, u, ua), jnp.where(odd, flux, fb), jnp.where(odd, ua, u)))
+    write_pack(own, final[0][:2], final[1][:2])
+    send[0:32] = final[0][2]
+    send[32:64] = final[0][3]
+
+
+def coef_kernel(cond, kh, a2, cot, sub, dep, cls, k_y, k_l, k_z, k_s, base):
     me_y = lax.axis_index("gy")
-    odd = lax.rem(me_x, 2) == 1
-    fu[...] = jnp.where(odd, own[...], got[...])
-    for chunk in range(8):
-        levels, tie = load_x(xfac.at[chunk])
-        u = expand_chain(fu[64 + 8 * chunk : 72 + 8 * chunk], levels, tie, fu[8 * chunk : 8 * chunk + 8])
-        for x in range(8):
-            s1[pl.ds(64 * chunk + x, 8, stride=8), :] = u[x]
-    levels, tie = load_x(xhfac)
-    uh = jnp.concatenate(expand_chain(fu[129:130], levels, tie, fu[128:129]), axis=0)
-    kh_v = kh[...]
-    sub_v, dep_v = sub[...], dep[...]
+    sub_v, dep_v, kh_v = sub[...], dep[...], kh[...]
     top = film_top(cls[...])
     lane = lax.broadcasted_iota(jnp.int32, (8, 128), 1)
     first, final = lane == 0, lane == 127
     film_y = jnp.where(first & (me_y == 0), SIDE, 0.0) + jnp.where(final & (me_y == 7), SIDE, 0.0)
-    up, copies = None, []
     for z in range(64):
         rows = slice(8 * z, 8 * z + 8)
-        s, k = s1[rows], cond[rows]
-        s_r = jnp.where(final, pltpu.roll(uh, 63 - z, 1), pltpu.roll(s, 127, 1))
-        k_r = jnp.where(final, pltpu.roll(kh_v, 63 - z, 1), pltpu.roll(k, 127, 1))
-        s_l = pltpu.roll(uh, (128 - z) % 128, 1) if z else uh
-        k_l = pltpu.roll(kh_v, (128 - z) % 128, 1) if z else kh_v
-        f_y = jnp.minimum(k, k_r) * (s_r - s)
-        f_l = jnp.minimum(k, k_l) * (s - s_l)
-        total = f_y - jnp.where(first, f_l, pltpu.roll(f_y, 1, 1))
+        k = cond[rows]
+        k_h = pltpu.roll(kh_v, 128 - 2 * z, 1) if z else kh_v
+        k_y[rows] = (2.0 * R) * jnp.minimum(k, jnp.where(final, k_h, pltpu.roll(k, 127, 1)))
+        k_l[rows] = (2.0 * R) * jnp.minimum(k, k_h)
+        if z < 63:
+            k_z[rows] = (2.0 * R) * jnp.minimum(k, cond[8 * z + 8 : 8 * z + 16])
         film = film_y + top * (dep_v - 1 == z).astype(F32)
         if z == 0:
             film = film + BOTTOM
+        k_s[rows] = 2.0 * jnp.where(z < sub_v, 1.0, 0.6) - (2.0 * R) * film
+        base[rows] = cot[rows] - 2.0 * a2[rows]
+
+
+def last_kernel(
+    own, got, xfac, xhfac, k_y, k_l, k_z, k_s, base, sub, temp_out, src_out, s1, fu, t_buf, s_buf, sems
+):
+    core = lax.rem(lax.axis_index("gx"), 2)
+    for i in range(2):
+        fu[i, pl.ds(pl.multiple_of(32 * core, 32), 32), :] = own[32 * i : 32 * i + 32]
+        fu[i, pl.ds(pl.multiple_of(32 - 32 * core, 32), 32), :] = got[32 * i : 32 * i + 32]
+    levels, tie = load_x(xhfac)
+    uh = jnp.concatenate(expand_chain(own[65:66], levels, tie, own[64:65]), axis=0)
+    sub_v = sub[...]
+    lane = lax.broadcasted_iota(jnp.int32, (8, 128), 1)
+    first, final = lane == 0, lane == 127
+    up, copies = None, []
+
+    def expand(chunk):
+        rows = slice(8 * chunk, 8 * chunk + 8)
+        levels, tie = load_x(xfac.at[chunk])
+        u = expand_chain(fu[1, rows], levels, tie, fu[0, rows])
+        for x in range(8):
+            s1[pl.ds(64 * chunk + x, 8, stride=8), :] = u[x]
+
+    expand(0)
+    for z in range(64):
+        if z & 7 == 0 and z < 56:
+            expand(z // 8 + 1)
+        rows = slice(8 * z, 8 * z + 8)
+        s = s1[rows]
+        s_h = pltpu.roll(uh, 128 - 2 * z, 1) if z else uh
+        f_y = k_y[rows] * (jnp.where(final, s_h, pltpu.roll(s, 127, 1)) - s)
+        f_l = k_l[rows] * (s - s_h)
+        total = f_y - jnp.where(first, f_l, pltpu.roll(f_y, 1, 1))
         if z < 63:
-            nxt = slice(8 * z + 8, 8 * z + 16)
-            f_z = jnp.minimum(k, cond[nxt]) * (s1[nxt] - s)
+            f_z = k_z[rows] * (s1[8 * z + 8 : 8 * z + 16] - s)
             total = total + f_z
         if z:
             total = total - up
         up = f_z
-        total = total - film * s
-        src = jnp.where(z < sub_v, 1.0, 0.6) * s
-        s_buf[rows] = src
-        t_buf[rows] = 2.0 * src - 2.0 * a2[rows] + cot[rows] + (2.0 * R) * total
+        s_buf[rows] = jnp.where(z < sub_v, 1.0, 0.6) * s
+        t_buf[rows] = base[rows] + k_s[rows] * s + total
         if z & 7 == 7:
             part = slice(8 * z - 56, 8 * z + 8)
             for i, (buf, out) in enumerate(((s_buf, src_out), (t_buf, temp_out))):
@@ -488,7 +494,7 @@
 
 
 def swap(v, bit):
-    return lax.ppermute(v, "gx", [(i, i ^ bit) for i in range(1, 16, 2)])
+    return lax.ppermute(v, "gx", [(i, i ^ bit) for i in range(16)])
 
 
 def body(cotangent, saved_temp, substrate_top, deposit_top, top_class):
@@ -504,27 +510,30 @@
         far_in=5, sems=5,
     )
     gat = lax.all_to_all(ypack, "gy", split_axis=0, concat_axis=0, tiled=True)
-    xpack, xfac, xhfac, a2, kh = call(
+    keep, send, xfac, xhfac, a2, kh = call(
         second_kernel,
-        [(456, 128), (8, 24, 8, 128), (24, 1, 128), (512, 128), (8, 128)],
-        [(8, 32, 128), (512, 128), (8, 64, 128)],
+        [(232, 128), (232, 128), (8, 24, 8, 128), (24, 1, 128), (512, 128), (8, 128)],
+        [(8, 32, 128), (512, 128), (512, 128), (7, 64, 128)],
         "second",
         gat, fac, ties, cond, sub,
     )
-    other = lax.ppermute(xpack, "gx", [(i, i + 1) for i in range(0, 16, 2)])
-    m1, sv1 = call(functools.partial(merge_kernel, 1, False), [(456, 128), (392, 128)], [], "merge_core", xpack, other)
-    m2, sv2 = call(functools.partial(merge_kernel, 2, False), [(456, 128), (392, 128)], [], "merge_near", m1, swap(m1, 2))
+    m1, sv1 = call(functools.partial(merge_kernel, 1, False), [(232, 128), (200, 128)], [], "merge_core", keep, swap(send, 1))
+    m2, sv2 = call(functools.partial(merge_kernel, 2, False), [(232, 128), (200, 128)], [], "merge_near", m1, swap(m1, 2))
     m3, sv3, near = call(
-        functools.partial(merge_kernel, 4, True), [(456, 128), (392, 128), (200, 128)], [], "merge_far", m2, swap(m2, 6)
+        functools.partial(merge_kernel, 4, True), [(232, 128), (200, 128), (104, 128)], [], "merge_far", m2, swap(m2, 6)
     )
-    own, out = call(top_kernel, [(136, 128), (136, 128)], [], "top", m3, near, swap(near, 8), sv1, sv2, sv3)
-    got = lax.ppermute(out, "gx", [(i + 1, i) for i in range(0, 16, 2)])
+    sv3, kh = lax.optimization_barrier((sv3, kh))
+    coefs = call(coef_kernel, [(512, 128)] * 5, [], "coef", cond, kh, a2, cot, sub, dep, cls)
+    opposite = swap(near, 8)
+    sv3, coefs = lax.optimization_barrier((sv3, coefs))
+    own, out = call(top_kernel, [(72, 128), (64, 128)], [], "top", m3, near, opposite, sv1, sv2, sv3)
+    got = swap(out, 1)
     grad_temp, grad_source = call(
         last_kernel,
         [(512, 128), (512, 128)],
-        [(512, 128), (136, 128), (512, 128), (512, 128)],
+        [(512, 128), (2, 64, 128), (512, 128), (512, 128)],
         "last",
-        own, got, xfac, xhfac, kh, cond, a2, cot, sub, dep, cls,
+        own, got, xfac, xhfac, *coefs, sub,
         far_out=2, sems=16,
     )
     return grad_temp.reshape(cotangent.shape), grad_source.reshape(cotangent.shape)

time: 47.9 us -> 38.3 us (0.80)
  waiting for transfers between devices: 13.2 us -> 8.82 us
  starting transfers between devices: 16.1 us -> 13.4 us
  Pallas kernels: 6.5 us -> 4.18 us
    ppermute x5, waiting for transfers between devices: 13.2 us -> 8.82 us  [swap(): return lax.ppermute(v, 'gx', [(i, i ^ bit) for i in range(16)])]
    ppermute x5, starting transfers between devices: 16.1 us -> 13.4 us  [swap(): return lax.ppermute(v, 'gx', [(i, i ^ bit) for i in range(16)])]
    pallas_call x7 -> x8, Pallas kernels: 6.5 us -> 4.18 us  [call(): pl.pallas_call(kernel, out_shape=shapes, in_specs=[HBM if i < far_in else...]
  transfers between devices with their start and end apart: 5 -> 5, of which waited for: 5 -> 5; matrix products, arithmetic and copies ran while one was open for 0% -> 0% of each run, Pallas kernels for 0% -> 1%
where the time goes in v3:
time: 38.3 us; the launch traced here: 38.1 us
  starting transfers between devices  13.4 us (35%)
  blocking collectives  11.1 us (29%)
  waiting for transfers between devices  8.82 us (23%)
  Pallas kernels  4.18 us (11%)
  between operations  0.67 us (2%)
    ppermute x5, starting transfers between devices, swap(): return lax.ppermute(v, 'gx', [(i, i ^ bit) for i in range(16)])  13.4 us
    all_to_all x1, blocking collectives, body(): gat = lax.all_to_all(ypack, 'gy', split_axis=0, concat_axis=0, tiled=True)  11.1 us
    ppermute x5, waiting for transfers between devices, swap(): return lax.ppermute(v, 'gx', [(i, i ^ bit) for i in range(16)])  8.82 us
    pallas_call x8, Pallas kernels, call(): pl.pallas_call(kernel, out_shape=shapes, in_specs=[HBM if i < far_in else...  4.18 us
  transfers between devices with their start and end apart: 5, of which 5 were waited for; matrix products, arithmetic and copies ran while one was open for 0% of the time, Pallas kernels for 1%

profile of v3, /device:TPU:1, one launch (start us, length us, event | category | flops | bytes accessed | tf_op | source)
XLA Modules:
  0.0 38.1 jit_solution(16283103741413332593)
XLA Ops:
  0.6 1.8 %first.1 = (f32[8,40,128]{2,1,0:T(8,128)S(1)}, f32[512,128]{1,0:T(8,128)S(1)}, f32[3,63,8,128]{3,2,1,0:T(8,128)S(1)}, f32[12,8,128]{2,1,0:T(8,128)S(1)}, f32[512...) custom-call(f32[512,128]{1,0:T(8,128)} %bitcast.4, f32[512,128]{1,0:T(8,128)} %bitcast.5, ...), custom_call_target="tpu_custom_call" | custom-call | tf_op jit(solution)/shard_map/first/pallas_call | solution.py:485
  2.4 11.1 %all_to_all.5.gat = f32[8,40,128]{2,1,0:T(8,128)S(1)} all-to-all(f32[8,40,128]{2,1,0:T(8,128)S(1)} %get-tuple-element.40), channel_id=1, replica_groups=mesh['gx'=16,'gy'=8] {'gy'}, dimensions={0} | all-to-all | bytes 327680 | tf_op jit(solution)/shard_map/all_to_all | solution.py:512
  13.4 0.5 %second.1 = (f32[232,128]{1,0:T(8,128)S(1)}, f32[232,128]{1,0:T(8,128)S(1)}, f32[8,24,8,128]{3,2,1,0:T(8,128)S(1)}, f32[24,1,128]{2,1,0:T(1,128)S(1)}, f32[512,128]{1,0:T(8,128)S(1)}, /*index=5*/f32[8,128]{1,0:T(8,128)S(1)}) custom-call(f32[8,40,128]{2,1,0:T(8,128)S(1)} %all_to_all.5.gat, f32[3,63,8,128]{3,2,1,0:T(8,128)S(1)} %get-tuple-element.41.fac, ...), custom_call_target="tpu_custom_call" | custom-call | tf_op jit(solution)/shard_map/second/pallas_call | solution.py:485
  13.9 2.2 %collective-permute-start = (f32[232,128]{1,0:T(8,128)S(1)}, f32[232,128]{1,0:T(8,128)S(1)}, u32[]{:S(2)}, u32[]{:S(2)}) collective-permute-start(f32[232,128]{1,0:T(8,128)S(1)} %get-tuple-element.46), channel_id=1, source_target_pairs={{0,8},{8,0},{16,24},{24,16},{32,40},{40,32},{48,56},{56,48},{64,72... | collective-permute-start | bytes 356360 | tf_op jit(solution)/shard_map/ppermute | solution.py:497
  16.1 1.0 %collective-permute-done.theirs = f32[232,128]{1,0:T(8,128)S(1)} collective-permute-done((f32[232,128]{1,0:T(8,128)S(1)}, f32[232,128]{1,0:T(8,128)S(1)}, u32[]{:S(2)}, u32[]{:S(2)}) %collective-permute-start) | collective-permute-done | bytes 118816 | tf_op jit(solution)/shard_map/ppermute | solution.py:497
  17.1 1.7 %collective-permute-start.1 = (f32[232,128]{1,0:T(8,128)S(1)}, f32[232,128]{1,0:T(8,128)S(1)}, u32[]{:S(2)}, u32[]{:S(2)}) collective-permute-start(f32[232,128]{1,0:T(8,128)S(1)} %get-tuple-element.47.mine), channel_id=1, source_target_pairs={{0,16},{8,24},{16,0},{24,8},{32,48},{40,56},{48,32},{56,40},{64,80... | collective-permute-start | bytes 356360 | tf_op jit(solution)/shard_map/ppermute | solution.py:497
  18.8 3.1 %collective-permute-done.1.theirs = f32[232,128]{1,0:T(8,128)S(1)} collective-permute-done((f32[232,128]{1,0:T(8,128)S(1)}, f32[232,128]{1,0:T(8,128)S(1)}, u32[]{:S(2)}, u32[]{:S(2)}) %collective-permute-start.1) | collective-permute-done | bytes 118816 | tf_op jit(solution)/shard_map/ppermute | solution.py:497
  22.0 3.5 %collective-permute-start.2 = (f32[232,128]{1,0:T(8,128)S(1)}, f32[232,128]{1,0:T(8,128)S(1)}, u32[]{:S(2)}, u32[]{:S(2)}) collective-permute-start(f32[232,128]{1,0:T(8,128)S(1)} %get-tuple-element.48.mine), channel_id=1, source_target_pairs={{0,48},{8,56},{16,32},{24,40},{32,16},{40,24},{48,0},{56,8},{64,11... | collective-permute-start | bytes 356360 | tf_op jit(solution)/shard_map/ppermute | solution.py:497
  25.5 2.2 %collective-permute-done.2.theirs = f32[232,128]{1,0:T(8,128)S(1)} collective-permute-done((f32[232,128]{1,0:T(8,128)S(1)}, f32[232,128]{1,0:T(8,128)S(1)}, u32[]{:S(2)}, u32[]{:S(2)}) %collective-permute-start.2) | collective-permute-done | bytes 118816 | tf_op jit(solution)/shard_map/ppermute | solution.py:497
  27.7 0.1 merge_far.1
  27.8 2.7 %collective-permute-start.3 = (f32[104,128]{1,0:T(8,128)S(1)}, f32[104,128]{1,0:T(8,128)S(1)}, u32[]{:S(2)}, u32[]{:S(2)}) collective-permute-start(f32[104,128]{1,0:T(8,128)S(1)} %get-tuple-element.50.near), channel_id=1, source_target_pairs={{0,64},{8,72},{16,80},{24,88},{32,96},{40,104},{48,112},{56,120},{... | collective-permute-start | bytes 159752 | tf_op jit(solution)/shard_map/ppermute | solution.py:497
  30.5 0.2 coef.1
  30.7 1.6 %collective-permute-done.3.theirs = f32[104,128]{1,0:T(8,128)S(1)} collective-permute-done((f32[104,128]{1,0:T(8,128)S(1)}, f32[104,128]{1,0:T(8,128)S(1)}, u32[]{:S(2)}, u32[]{:S(2)}) %collective-permute-start.3) | collective-permute-done | bytes 53280 | tf_op jit(solution)/shard_map/ppermute | solution.py:497
  32.3 0.1 top.1
  32.4 3.3 %collective-permute-start.4 = (f32[64,128]{1,0:T(8,128)S(1)}, f32[64,128]{1,0:T(8,128)S(1)}, u32[]{:S(2)}, u32[]{:S(2)}) collective-permute-start(f32[64,128]{1,0:T(8,128)S(1)} %get-tuple-element.68), channel_id=1, source_target_pairs={{0,8},{8,0},{16,24},{24,16},{32,40},{40,32},{48,56},{56,48},{64,72... | collective-permute-start | bytes 98312 | tf_op jit(solution)/shard_map/ppermute | solution.py:497
  35.7 0.9 %collective-permute-done.4.got = f32[64,128]{1,0:T(8,128)S(1)} collective-permute-done((f32[64,128]{1,0:T(8,128)S(1)}, f32[64,128]{1,0:T(8,128)S(1)}, u32[]{:S(2)}, u32[]{:S(2)}) %collective-permute-start.4) | collective-permute-done | bytes 32800 | tf_op jit(solution)/shard_map/ppermute | solution.py:497
  36.6 1.5 %last.1 = (f32[512,128]{1,0:T(8,128)}, f32[512,128]{1,0:T(8,128)}) custom-call(f32[72,128]{1,0:T(8,128)S(1)} %get-tuple-element.67.own, f32[64,128]{1,0:T(8,128)S(1)} %collective-permute-done.4.got, f32[8,24,8,128]{3,2,1,0:T(8,128)S(1)} %get-tuple-element.69.xfac, f32[24,1,128]{2,1,0:T(1,128)S(1)} %get-tuple-element.70.xhfac, ...), custom_call_target="tpu_custom_call" | custom-call | tf_op jit(solution)/shard_map/last/pallas_call | solution.py:485
  (2 shorter events, 0.1 us)
Async XLA Ops:
  13.9 3.1 %collective-permute-start = (f32[232,128]{1,0:T(8,128)S(1)}, f32[232,128]{1,0:T(8,128)S(1)}, u32[]{:S(2)}, u32[]{:S(2)}) collective-permute-start(f32[232,128]{1,0:T(8,128)S(1)} %get-tuple-element.46), channel_id=1, source_target_pairs={{0,8},{8,0},{16,24},{24,16},{32,40},{40,32},{48,56},{56,48},{64,72... | collective-permute-start | bytes 356360 | tf_op jit(solution)/shard_map/ppermute | solution.py:497
  17.1 4.9 %collective-permute-start.1 = (f32[232,128]{1,0:T(8,128)S(1)}, f32[232,128]{1,0:T(8,128)S(1)}, u32[]{:S(2)}, u32[]{:S(2)}) collective-permute-start(f32[232,128]{1,0:T(8,128)S(1)} %get-tuple-element.47.mine), channel_id=1, source_target_pairs={{0,16},{8,24},{16,0},{24,8},{32,48},{40,56},{48,32},{56,40},{64,80... | collective-permute-start | bytes 356360 | tf_op jit(solution)/shard_map/ppermute | solution.py:497
  22.0 5.7 %collective-permute-start.2 = (f32[232,128]{1,0:T(8,128)S(1)}, f32[232,128]{1,0:T(8,128)S(1)}, u32[]{:S(2)}, u32[]{:S(2)}) collective-permute-start(f32[232,128]{1,0:T(8,128)S(1)} %get-tuple-element.48.mine), channel_id=1, source_target_pairs={{0,48},{8,56},{16,32},{24,40},{32,16},{40,24},{48,0},{56,8},{64,11... | collective-permute-start | bytes 356360 | tf_op jit(solution)/shard_map/ppermute | solution.py:497
  27.8 4.6 %collective-permute-start.3 = (f32[104,128]{1,0:T(8,128)S(1)}, f32[104,128]{1,0:T(8,128)S(1)}, u32[]{:S(2)}, u32[]{:S(2)}) collective-permute-start(f32[104,128]{1,0:T(8,128)S(1)} %get-tuple-element.50.near), channel_id=1, source_target_pairs={{0,64},{8,72},{16,80},{24,88},{32,96},{40,104},{48,112},{56,120},{... | collective-permute-start | bytes 159752 | tf_op jit(solution)/shard_map/ppermute | solution.py:497
  32.4 4.2 %collective-permute-start.4 = (f32[64,128]{1,0:T(8,128)S(1)}, f32[64,128]{1,0:T(8,128)S(1)}, u32[]{:S(2)}, u32[]{:S(2)}) collective-permute-start(f32[64,128]{1,0:T(8,128)S(1)} %get-tuple-element.68), channel_id=1, source_target_pairs={{0,8},{8,0},{16,24},{24,16},{32,40},{40,32},{48,56},{56,48},{64,72... | collective-permute-start | bytes 98312 | tf_op jit(solution)/shard_map/ppermute | solution.py:497

commit v4 on v3

--- a/solution.py
+++ b/solution.py
@@ -1,5 +1,3 @@
-import functools
-
 import jax
 import jax.numpy as jnp
 from jax import lax
@@ -346,31 +344,35 @@
     return a, b
 
 
-def merge_kernel(bit, last, mine, theirs, merged_out, saved_out, *rest):
-    me_x = lax.axis_index("gx")
-    right = lax.rem(lax.div(me_x, bit), 2) == 1
+def core_kernel(mine, theirs, merged_out, saved_out):
+    right = lax.rem(lax.axis_index("gx"), 2) == 1
     m, t = read_pack(mine, 7), read_pack(theirs, 7)
-    done = []
-    for part in range(2):
-        a, b = order(right, m[part], t[part])
-        done.append(merge_ports(a, b))
+    done = [merge_ports(*order(right, m[part], t[part])) for part in range(2)]
     write_pack(merged_out, done[0][0], done[1][0])
     write_pack(saved_out, done[0][1], done[1][1])
-    if last:
-        far = lax.div(me_x, 8) == 1
-        outs = []
-        for part in range(2):
-            kf, kl, z, tt, g, p, q = done[part][0]
-            gi = recip(g)
-            tg = tt * gi
-            outs.append(
-                (
-                    jnp.where(far, z + tt * tg, g),
-                    jnp.where(far, p + tg * q, q),
-                    jnp.where(far, kf, kl),
-                )
-            )
-        write_pack(rest[0], outs[0], outs[1])
+
+
+def ring_kernel(own, near, far, mid, merged_out, pair_out, saved_out, top_out):
+    me_x = lax.axis_index("gx")
+    right = lax.rem(lax.div(me_x, 2), 2) == 1
+    upper = lax.rem(lax.div(me_x, 4), 2) == 1
+    last = lax.div(me_x, 8) == 1
+    packs = [read_pack(r, 7) for r in (own, near, mid, far)]
+    pairs, saves, outs, tops = [], [], [], []
+    for part in range(2):
+        mine, keep = merge_ports(*order(right, packs[0][part], packs[1][part]))
+        other, _ = merge_ports(*order(right, packs[2][part], packs[3][part]))
+        merged, saved = merge_ports(*order(upper, mine, other))
+        pairs.append(keep)
+        saves.append(saved)
+        outs.append(merged)
+        kf, kl, z, tt, g, p, q = merged
+        tg = tt * recip(g)
+        tops.append((jnp.where(last, z + tt * tg, g), jnp.where(last, p + tg * q, q), jnp.where(last, kf, kl)))
+    write_pack(merged_out, *outs)
+    write_pack(pair_out, *pairs)
+    write_pack(saved_out, *saves)
+    write_pack(top_out, *tops)
 
 
 def top_kernel(merged, near, theirs, sv1, sv2, sv3, own, send):
@@ -517,10 +519,16 @@
         "second",
         gat, fac, ties, cond, sub,
     )
-    m1, sv1 = call(functools.partial(merge_kernel, 1, False), [(232, 128), (200, 128)], [], "merge_core", keep, swap(send, 1))
-    m2, sv2 = call(functools.partial(merge_kernel, 2, False), [(232, 128), (200, 128)], [], "merge_near", m1, swap(m1, 2))
-    m3, sv3, near = call(
-        functools.partial(merge_kernel, 4, True), [(232, 128), (200, 128), (104, 128)], [], "merge_far", m2, swap(m2, 6)
+    m1, sv1 = call(core_kernel, [(232, 128), (200, 128)], [], "merge_core", keep, swap(send, 1))
+    near_z = swap(m1, 2)
+    far = swap(m1, 6)
+    mid = swap(m1, 4)
+    m3, sv2, sv3, near = call(
+        ring_kernel,
+        [(232, 128), (200, 128), (200, 128), (104, 128)],
+        [],
+        "merge_ring",
+        m1, near_z, far, mid,
     )
     sv3, kh = lax.optimization_barrier((sv3, kh))
     coefs = call(coef_kernel, [(512, 128)] * 5, [], "coef", cond, kh, a2, cot, sub, dep, cls)

time: 38.3 us -> 37.4 us (0.977)
  starting transfers between devices: 13.4 us -> 12.3 us
    ppermute x5 -> x6, starting transfers between devices: 13.4 us -> 12.3 us  [swap(): return lax.ppermute(v, 'gx', [(i, i ^ bit) for i in range(16)])]
    ppermute x5 -> x6, waiting for transfers between devices: 8.82 us -> 9.03 us  [swap(): return lax.ppermute(v, 'gx', [(i, i ^ bit) for i in range(16)])]
    pallas_call x8 -> x7, Pallas kernels: 4.18 us -> 4.2 us  [call(): pl.pallas_call(kernel, out_shape=shapes, in_specs=[HBM if i < far_in else...]
  transfers between devices with their start and end apart: 5 -> 6, of which waited for: 5 -> 5; matrix products, arithmetic and copies ran while one was open for 0% -> 0% of each run, Pallas kernels for 1% -> 1%
where the time goes in v4:
time: 37.4 us; the launch traced here: 37.2 us
  starting transfers between devices  12.3 us (33%)
  blocking collectives  11.1 us (30%)
  waiting for transfers between devices  9.03 us (24%)
  Pallas kernels  4.2 us (11%)
  between operations  0.67 us (2%)
    ppermute x6, starting transfers between devices, swap(): return lax.ppermute(v, 'gx', [(i, i ^ bit) for i in range(16)])  12.3 us
    all_to_all x1, blocking collectives, body(): gat = lax.all_to_all(ypack, 'gy', split_axis=0, concat_axis=0, tiled=True)  11.1 us
    ppermute x6, waiting for transfers between devices, swap(): return lax.ppermute(v, 'gx', [(i, i ^ bit) for i in range(16)])  9.03 us
    pallas_call x7, Pallas kernels, call(): pl.pallas_call(kernel, out_shape=shapes, in_specs=[HBM if i < far_in else...  4.2 us
  transfers between devices with their start and end apart: 6, of which 5 were waited for; matrix products, arithmetic and copies ran while one was open for 0% of the time, Pallas kernels for 1%

profile of v4, /device:TPU:1, one launch (start us, length us, event | category | flops | bytes accessed | tf_op | source)
XLA Modules:
  0.0 37.2 jit_solution(12805380591238699231)
XLA Ops:
  0.6 1.8 %first.1 = (f32[8,40,128]{2,1,0:T(8,128)S(1)}, f32[512,128]{1,0:T(8,128)S(1)}, f32[3,63,8,128]{3,2,1,0:T(8,128)S(1)}, f32[12,8,128]{2,1,0:T(8,128)S(1)}, f32[512...) custom-call(f32[512,128]{1,0:T(8,128)} %bitcast.4, f32[512,128]{1,0:T(8,128)} %bitcast.5, ...), custom_call_target="tpu_custom_call" | custom-call | tf_op jit(solution)/shard_map/first/pallas_call | solution.py:487
  2.4 11.1 %all_to_all.5.gat = f32[8,40,128]{2,1,0:T(8,128)S(1)} all-to-all(f32[8,40,128]{2,1,0:T(8,128)S(1)} %get-tuple-element.39), channel_id=1, replica_groups=mesh['gx'=16,'gy'=8] {'gy'}, dimensions={0} | all-to-all | bytes 327680 | tf_op jit(solution)/shard_map/all_to_all | solution.py:514
  13.4 0.5 %second.1 = (f32[232,128]{1,0:T(8,128)S(1)}, f32[232,128]{1,0:T(8,128)S(1)}, f32[8,24,8,128]{3,2,1,0:T(8,128)S(1)}, f32[24,1,128]{2,1,0:T(1,128)S(1)}, f32[512,128]{1,0:T(8,128)S(1)}, /*index=5*/f32[8,128]{1,0:T(8,128)S(1)}) custom-call(f32[8,40,128]{2,1,0:T(8,128)S(1)} %all_to_all.5.gat, f32[3,63,8,128]{3,2,1,0:T(8,128)S(1)} %get-tuple-element.40.fac, ...), custom_call_target="tpu_custom_call" | custom-call | tf_op jit(solution)/shard_map/second/pallas_call | solution.py:487
  13.9 2.2 %collective-permute-start = (f32[232,128]{1,0:T(8,128)S(1)}, f32[232,128]{1,0:T(8,128)S(1)}, u32[]{:S(2)}, u32[]{:S(2)}) collective-permute-start(f32[232,128]{1,0:T(8,128)S(1)} %get-tuple-element.45), channel_id=1, source_target_pairs={{0,8},{8,0},{16,24},{24,16},{32,40},{40,32},{48,56},{56,48},{64,72... | collective-permute-start | bytes 356360 | tf_op jit(solution)/shard_map/ppermute | solution.py:499
  16.1 1.0 %collective-permute-done.theirs = f32[232,128]{1,0:T(8,128)S(1)} collective-permute-done((f32[232,128]{1,0:T(8,128)S(1)}, f32[232,128]{1,0:T(8,128)S(1)}, u32[]{:S(2)}, u32[]{:S(2)}) %collective-permute-start) | collective-permute-done | bytes 118816 | tf_op jit(solution)/shard_map/ppermute | solution.py:499
  17.1 1.7 %collective-permute-start.1 = (f32[232,128]{1,0:T(8,128)S(1)}, f32[232,128]{1,0:T(8,128)S(1)}, u32[]{:S(2)}, u32[]{:S(2)}) collective-permute-start(f32[232,128]{1,0:T(8,128)S(1)} %get-tuple-element.46.own), channel_id=1, source_target_pairs={{0,16},{8,24},{16,0},{24,8},{32,48},{40,56},{48,32},{56,40},{64,80... | collective-permute-start | bytes 356360 | tf_op jit(solution)/shard_map/ppermute | solution.py:499
  18.8 2.2 %collective-permute-start.2 = (f32[232,128]{1,0:T(8,128)S(1)}, f32[232,128]{1,0:T(8,128)S(1)}, u32[]{:S(2)}, u32[]{:S(2)}) collective-permute-start(f32[232,128]{1,0:T(8,128)S(1)} %get-tuple-element.46.own), channel_id=1, source_target_pairs={{0,48},{8,56},{16,32},{24,40},{32,16},{40,24},{48,0},{56,8},{64,11... | collective-permute-start | bytes 356360 | tf_op jit(solution)/shard_map/ppermute | solution.py:499
  21.1 1.1 %collective-permute-start.3 = (f32[232,128]{1,0:T(8,128)S(1)}, f32[232,128]{1,0:T(8,128)S(1)}, u32[]{:S(2)}, u32[]{:S(2)}) collective-permute-start(f32[232,128]{1,0:T(8,128)S(1)} %get-tuple-element.46.own), channel_id=1, source_target_pairs={{0,32},{8,40},{16,48},{24,56},{32,0},{40,8},{48,16},{56,24},{64,96... | collective-permute-start | bytes 356360 | tf_op jit(solution)/shard_map/ppermute | solution.py:499
  22.1 0.0 collective-permute-done.1.near
  22.1 3.6 %collective-permute-done.2.far = f32[232,128]{1,0:T(8,128)S(1)} collective-permute-done((f32[232,128]{1,0:T(8,128)S(1)}, f32[232,128]{1,0:T(8,128)S(1)}, u32[]{:S(2)}, u32[]{:S(2)}) %collective-permute-start.2) | collective-permute-done | bytes 118816 | tf_op jit(solution)/shard_map/ppermute | solution.py:499
  25.7 2.0 %collective-permute-done.3.mid = f32[232,128]{1,0:T(8,128)S(1)} collective-permute-done((f32[232,128]{1,0:T(8,128)S(1)}, f32[232,128]{1,0:T(8,128)S(1)}, u32[]{:S(2)}, u32[]{:S(2)}) %collective-permute-start.3) | collective-permute-done | bytes 118816 | tf_op jit(solution)/shard_map/ppermute | solution.py:499
  27.7 0.1 merge_ring.1
  27.8 2.7 %collective-permute-start.4 = (f32[104,128]{1,0:T(8,128)S(1)}, f32[104,128]{1,0:T(8,128)S(1)}, u32[]{:S(2)}, u32[]{:S(2)}) collective-permute-start(f32[104,128]{1,0:T(8,128)S(1)} %get-tuple-element.48.near), channel_id=1, source_target_pairs={{0,64},{8,72},{16,80},{24,88},{32,96},{40,104},{48,112},{56,120},{... | collective-permute-start | bytes 159752 | tf_op jit(solution)/shard_map/ppermute | solution.py:499
  30.5 0.2 coef.1
  30.8 1.6 %collective-permute-done.4.theirs = f32[104,128]{1,0:T(8,128)S(1)} collective-permute-done((f32[104,128]{1,0:T(8,128)S(1)}, f32[104,128]{1,0:T(8,128)S(1)}, u32[]{:S(2)}, u32[]{:S(2)}) %collective-permute-start.4) | collective-permute-done | bytes 53280 | tf_op jit(solution)/shard_map/ppermute | solution.py:499
  32.4 0.1 top.1
  32.5 2.4 %collective-permute-start.5 = (f32[64,128]{1,0:T(8,128)S(1)}, f32[64,128]{1,0:T(8,128)S(1)}, u32[]{:S(2)}, u32[]{:S(2)}) collective-permute-start(f32[64,128]{1,0:T(8,128)S(1)} %get-tuple-element.66), channel_id=1, source_target_pairs={{0,8},{8,0},{16,24},{24,16},{32,40},{40,32},{48,56},{56,48},{64,72... | collective-permute-start | bytes 98312 | tf_op jit(solution)/shard_map/ppermute | solution.py:499
  34.8 0.9 %collective-permute-done.5.got = f32[64,128]{1,0:T(8,128)S(1)} collective-permute-done((f32[64,128]{1,0:T(8,128)S(1)}, f32[64,128]{1,0:T(8,128)S(1)}, u32[]{:S(2)}, u32[]{:S(2)}) %collective-permute-start.5) | collective-permute-done | bytes 32800 | tf_op jit(solution)/shard_map/ppermute | solution.py:499
  35.7 1.5 %last.1 = (f32[512,128]{1,0:T(8,128)}, f32[512,128]{1,0:T(8,128)}) custom-call(f32[72,128]{1,0:T(8,128)S(1)} %get-tuple-element.65.own, f32[64,128]{1,0:T(8,128)S(1)} %collective-permute-done.5.got, f32[8,24,8,128]{3,2,1,0:T(8,128)S(1)} %get-tuple-element.67.xfac, f32[24,1,128]{2,1,0:T(1,128)S(1)} %get-tuple-element.68.xhfac, ...), custom_call_target="tpu_custom_call" | custom-call | tf_op jit(solution)/shard_map/last/pallas_call | solution.py:487
  (1 shorter events, 0.0 us)
Async XLA Ops:
  13.9 3.1 %collective-permute-start = (f32[232,128]{1,0:T(8,128)S(1)}, f32[232,128]{1,0:T(8,128)S(1)}, u32[]{:S(2)}, u32[]{:S(2)}) collective-permute-start(f32[232,128]{1,0:T(8,128)S(1)} %get-tuple-element.45), channel_id=1, source_target_pairs={{0,8},{8,0},{16,24},{24,16},{32,40},{40,32},{48,56},{56,48},{64,72... | collective-permute-start | bytes 356360 | tf_op jit(solution)/shard_map/ppermute | solution.py:499
  17.1 5.0 %collective-permute-start.1 = (f32[232,128]{1,0:T(8,128)S(1)}, f32[232,128]{1,0:T(8,128)S(1)}, u32[]{:S(2)}, u32[]{:S(2)}) collective-permute-start(f32[232,128]{1,0:T(8,128)S(1)} %get-tuple-element.46.own), channel_id=1, source_target_pairs={{0,16},{8,24},{16,0},{24,8},{32,48},{40,56},{48,32},{56,40},{64,80... | collective-permute-start | bytes 356360 | tf_op jit(solution)/shard_map/ppermute | solution.py:499
  18.8 6.9 %collective-permute-start.2 = (f32[232,128]{1,0:T(8,128)S(1)}, f32[232,128]{1,0:T(8,128)S(1)}, u32[]{:S(2)}, u32[]{:S(2)}) collective-permute-start(f32[232,128]{1,0:T(8,128)S(1)} %get-tuple-element.46.own), channel_id=1, source_target_pairs={{0,48},{8,56},{16,32},{24,40},{32,16},{40,24},{48,0},{56,8},{64,11... | collective-permute-start | bytes 356360 | tf_op jit(solution)/shard_map/ppermute | solution.py:499
  21.1 6.6 %collective-permute-start.3 = (f32[232,128]{1,0:T(8,128)S(1)}, f32[232,128]{1,0:T(8,128)S(1)}, u32[]{:S(2)}, u32[]{:S(2)}) collective-permute-start(f32[232,128]{1,0:T(8,128)S(1)} %get-tuple-element.46.own), channel_id=1, source_target_pairs={{0,32},{8,40},{16,48},{24,56},{32,0},{40,8},{48,16},{56,24},{64,96... | collective-permute-start | bytes 356360 | tf_op jit(solution)/shard_map/ppermute | solution.py:499
  27.8 4.6 %collective-permute-start.4 = (f32[104,128]{1,0:T(8,128)S(1)}, f32[104,128]{1,0:T(8,128)S(1)}, u32[]{:S(2)}, u32[]{:S(2)}) collective-permute-start(f32[104,128]{1,0:T(8,128)S(1)} %get-tuple-element.48.near), channel_id=1, source_target_pairs={{0,64},{8,72},{16,80},{24,88},{32,96},{40,104},{48,112},{56,120},{... | collective-permute-start | bytes 159752 | tf_op jit(solution)/shard_map/ppermute | solution.py:499
  32.5 3.2 %collective-permute-start.5 = (f32[64,128]{1,0:T(8,128)S(1)}, f32[64,128]{1,0:T(8,128)S(1)}, u32[]{:S(2)}, u32[]{:S(2)}) collective-permute-start(f32[64,128]{1,0:T(8,128)S(1)} %get-tuple-element.66), channel_id=1, source_target_pairs={{0,8},{8,0},{16,24},{24,16},{32,40},{40,32},{48,56},{56,48},{64,72... | collective-permute-start | bytes 98312 | tf_op jit(solution)/shard_map/ppermute | solution.py:499

commit v5 on v4

--- a/solution.py
+++ b/solution.py
@@ -72,26 +72,31 @@
     return u
 
 
-def merge_ports(a, b):
-    kfa, kla, za, ta, ga, pa, qa = a
-    kfb, klb, zb, tb, gb, pb, qb = b
+def port_coefs(a, b):
+    kfa, kla, za, ta, ga = a
+    kfb, klb, zb, tb, gb = b
     link = R * jnp.minimum(kla, kfb)
     lk = link * recip(1.0 + link * zb)
     inv = recip(ga + lk)
-    h = inv * (qa + lk * pb)
     ti = ta * inv
     lt = lk * tb
     w = lt * inv
-    merged = (
-        kfa,
-        klb,
-        za + ta * ti,
-        ta * w,
-        gb + lt * tb * (ga * inv),
-        pa + ta * h,
-        qb + lt * (h - pb),
-    )
-    return merged, (h, ti, w, lk, pb, tb)
+    merged = (kfa, klb, za + ta * ti, ta * w, gb + lt * tb * (ga * inv))
+    return merged, (inv, lk, ta, lt, ti, w, tb)
+
+
+def port_values(coefs, a, b):
+    inv, lk, ta, lt, ti, w, tb = coefs
+    pa, qa = a
+    pb, qb = b
+    h = inv * (qa + lk * pb)
+    return (pa + ta * h, qb + lt * (h - pb)), (h, ti, w, lk, pb, tb)
+
+
+def merge_ports(a, b):
+    matrix, coefs = port_coefs(a[:5], b[:5])
+    values, saved = port_values(coefs, a[5:], b[5:])
+    return matrix + values, saved
 
 
 def descend(saved, flux, u_b):
@@ -137,32 +142,86 @@
     return levels
 
 
-def first_kernel(
-    cot_in, temp_in, sub_in, dep_in, cls_in, ypack, cond, fac, tie_out, cot, sub, dep, cls, temp, mid, tr, sems
-):
-    me_y = lax.axis_index("gy")
+def chain_matrix(c, s):
+    z = t = None
+    while len(s) > 1:
+        half = len(s) // 2
+        ml, mr = [None] * half, [None] * half
+        for j in range(half):
+            i = 2 * j
+            inv = recip(s[i] + c[i] + c[i - 1] if j else s[i] + c[i])
+            mr[j] = c[i] * inv
+            if j:
+                ml[j] = c[i - 1] * inv
+            elif z is None:
+                z, t = inv, mr[0]
+            else:
+                z, t = z + t * (t * inv), t * mr[0]
+        ns, nc = [], []
+        for j in range(half):
+            e = 2 * j
+            sv = s[e + 1] + mr[j] * s[e]
+            if j + 1 < half:
+                sv = sv + ml[j + 1] * s[e + 2]
+                nc.append(ml[j + 1] * c[e + 2])
+            ns.append(sv)
+        c, s = nc, ns
+    return z, t, s[0]
+
+
+def wall_terms():
+    me_x = lax.axis_index("gx")
+    return jnp.where(me_x == 0, R * SIDE, 0.0), jnp.where(me_x == 15, R * SIDE, 0.0)
+
+
+def split_halves(planes, keep, send):
+    core = lax.rem(lax.axis_index("gx"), 2)
+    for i in range(planes.shape[0]):
+        keep[32 * i : 32 * i + 32] = planes[i, pl.ds(pl.multiple_of(32 * core, 32), 32), :]
+        send[32 * i : 32 * i + 32] = planes[i, pl.ds(pl.multiple_of(32 - 32 * core, 32), 32), :]
+
+
+def fields_kernel(cot_in, temp_in, sub_in, dep_in, cls_in, cond, keep, send, cot, sub, dep, cls, temp, planes, sems):
     pairs = ((sub_in, sub), (dep_in, dep), (temp_in, temp), (cls_in, cls), (cot_in, cot))
     copies = [pltpu.make_async_copy(a, b, sems.at[i]) for i, (a, b) in enumerate(pairs)]
     for cp in copies:
         cp.start()
-    for cp in copies[:4]:
+    for cp in copies[:3]:
         cp.wait()
+    sub_v, dep_v = sub[...], dep[...]
+    for z in range(64):
+        base = jnp.where(z < sub_v, 1.0, 0.45)
+        sg = 0.5 + jax.nn.sigmoid(temp[8 * z : 8 * z + 8])
+        cond[8 * z : 8 * z + 8] = jnp.where(z < dep_v, base * sg, 0.0)
+    low, high = wall_terms()
+    base_z = lax.broadcasted_iota(jnp.int32, (8, 128), 0)
+    for chunk in range(8):
+        zi = base_z + 8 * chunk
+        k = [cond[pl.ds(64 * chunk + x, 8, stride=8), :] for x in range(8)]
+        s = [jnp.where(zi < sub_v[x : x + 1], 1.0, 0.6) for x in range(8)]
+        s[0] = s[0] + low
+        s[7] = s[7] + high
+        c = [R * jnp.minimum(k[x], k[x + 1]) for x in range(7)] + [None]
+        for i, v in enumerate((k[0], k[7]) + chain_matrix(c, s)):
+            planes[i, 8 * chunk : 8 * chunk + 8] = v
+    split_halves(planes, keep, send)
+    for cp in copies[3:]:
+        cp.wait()
+
+
+def first_kernel(cot, sub, dep, cls, cond, ypack, fac, tie_out, mid, tr):
+    me_y = lax.axis_index("gy")
     sub_v, dep_v = sub[...], dep[...]
     top = film_top(cls[...])
     k, cap, s = [], [], []
     for z in range(64):
-        under = z < sub_v
-        sg = 0.5 + jax.nn.sigmoid(temp[8 * z : 8 * z + 8])
-        kz = jnp.where(z < dep_v, jnp.where(under, 1.0, 0.45) * sg, 0.0)
-        cond[8 * z : 8 * z + 8] = kz
-        k.append(kz)
-        cap.append(jnp.where(under, 1.0, 0.6))
+        k.append(cond[8 * z : 8 * z + 8])
+        cap.append(jnp.where(z < sub_v, 1.0, 0.6))
         film = top * (dep_v - 1 == z).astype(F32)
         if z == 0:
             film = film + BOTTOM
         s.append(cap[z] + R * film)
     c = [R * jnp.minimum(k[z], k[z + 1]) for z in range(63)] + [None]
-    copies[4].wait()
     d = [cot[8 * z : 8 * z + 8] for z in range(64)]
     g, q, levels, _, _ = reduce_chain(c, s, d, False)
     u = expand_chain(q * recip(g), levels, None, None)
@@ -210,7 +269,6 @@
 
 def second_kernel(gat, fac, ties, cond, sub, keep, send, xfac, xhfac, a2_out, kh_out, pick, flat, planes, xp):
     me_y = lax.axis_index("gy")
-    me_x = lax.axis_index("gx")
     seg = [[gat[n, 4 * i : 4 * i + 4] for i in range(9)] for n in range(8)]
     gam, rhs = seg[0][4], seg[0][6]
     down, links = [None], [None]
@@ -274,8 +332,7 @@
     for x in range(8):
         kh_out[x : x + 1] = kh[x]
 
-    low = jnp.where(me_x == 0, R * SIDE, 0.0)
-    high = jnp.where(me_x == 15, R * SIDE, 0.0)
+    low, high = wall_terms()
 
     def x_chain(k, cap, d):
         s = list(cap)
@@ -297,16 +354,14 @@
             d.append(dx)
         levels, tie, port = x_chain(k, cap, d)
         store_x(xfac.at[chunk], levels, tie)
-        for i in range(7):
-            xp[i, 8 * chunk : 8 * chunk + 8] = port[i]
+        for i in range(2):
+            xp[i, 8 * chunk : 8 * chunk + 8] = port[5 + i]
     levels, tie, port = x_chain(kh, caph, dh)
     store_x(xhfac, levels, tie)
-    core = lax.rem(me_x, 2)
+    split_halves(xp, keep, send)
     for i in range(7):
-        keep[32 * i : 32 * i + 32] = xp[i, pl.ds(pl.multiple_of(32 * core, 32), 32), :]
-        send[32 * i : 32 * i + 32] = xp[i, pl.ds(pl.multiple_of(32 - 32 * core, 32), 32), :]
-        keep[224 + i : 225 + i] = port[i]
-        send[224 + i : 225 + i] = port[i]
+        keep[64 + i : 65 + i] = port[i]
+        send[64 + i : 65 + i] = port[i]
 
 
 def store_x(ref, levels, tie):
@@ -344,34 +399,74 @@
     return a, b
 
 
-def core_kernel(mine, theirs, merged_out, saved_out):
-    right = lax.rem(lax.axis_index("gx"), 2) == 1
-    m, t = read_pack(mine, 7), read_pack(theirs, 7)
-    done = [merge_ports(*order(right, m[part], t[part])) for part in range(2)]
-    write_pack(merged_out, done[0][0], done[1][0])
-    write_pack(saved_out, done[0][1], done[1][1])
-
-
-def ring_kernel(own, near, far, mid, merged_out, pair_out, saved_out, top_out):
+def planes_of(ref, n):
+    return tuple(ref[32 * i : 32 * i + 32] for i in range(n))
+
+
+def put_planes(ref, values):
+    for i, v in enumerate(values):
+        ref[32 * i : 32 * i + 32] = v
+
+
+def spots():
     me_x = lax.axis_index("gx")
-    right = lax.rem(lax.div(me_x, 2), 2) == 1
-    upper = lax.rem(lax.div(me_x, 4), 2) == 1
-    last = lax.div(me_x, 8) == 1
-    packs = [read_pack(r, 7) for r in (own, near, mid, far)]
-    pairs, saves, outs, tops = [], [], [], []
-    for part in range(2):
-        mine, keep = merge_ports(*order(right, packs[0][part], packs[1][part]))
-        other, _ = merge_ports(*order(right, packs[2][part], packs[3][part]))
-        merged, saved = merge_ports(*order(upper, mine, other))
-        pairs.append(keep)
-        saves.append(saved)
-        outs.append(merged)
-        kf, kl, z, tt, g, p, q = merged
+    return [lax.rem(lax.div(me_x, bit), 2) == 1 for bit in (1, 2, 4)]
+
+
+def core_matrix_kernel(mine, theirs, merged_out, coef_out):
+    odd, _, _ = spots()
+    merged, coefs = port_coefs(*order(odd, planes_of(mine, 5), planes_of(theirs, 5)))
+    put_planes(merged_out, merged)
+    put_planes(coef_out, coefs)
+
+
+def ring_matrix_kernel(own, near, far, mid, merged_out, mine_out, other_out, ring_out):
+    _, right, upper = spots()
+    packs = [planes_of(r, 5) for r in (own, near, mid, far)]
+    mine, mine_c = port_coefs(*order(right, packs[0], packs[1]))
+    other, other_c = port_coefs(*order(right, packs[2], packs[3]))
+    merged, ring_c = port_coefs(*order(upper, mine, other))
+    put_planes(merged_out, merged)
+    put_planes(mine_out, mine_c)
+    put_planes(other_out, other_c)
+    put_planes(ring_out, ring_c)
+
+
+def read_sides(ref):
+    main = (ref[0:32], ref[32:64])
+    edge = tuple(ref[64 + i : 65 + i] for i in range(7))
+    return main, edge
+
+
+def core_kernel(mine, theirs, coefs, merged_out, saved_out):
+    odd, _, _ = spots()
+    m, t = read_sides(mine), read_sides(theirs)
+    values, saved = port_values(planes_of(coefs, 7), *order(odd, m[0], t[0]))
+    edge, edge_saved = merge_ports(*order(odd, m[1], t[1]))
+    put_planes(merged_out, values)
+    for i in range(7):
+        merged_out[64 + i : 65 + i] = edge[i]
+    write_pack(saved_out, saved, edge_saved)
+
+
+def ring_kernel(own, near, far, mid, matrix, mine_c, other_c, ring_c, merged_out, pair_out, saved_out, top_out):
+    _, right, upper = spots()
+    last = lax.div(lax.axis_index("gx"), 8) == 1
+    main, edge = zip(*[read_sides(r) for r in (own, near, mid, far)])
+    mine, pair = port_values(planes_of(mine_c, 7), *order(right, main[0], main[1]))
+    other, _ = port_values(planes_of(other_c, 7), *order(right, main[2], main[3]))
+    values, saved = port_values(planes_of(ring_c, 7), *order(upper, mine, other))
+    e_mine, e_pair = merge_ports(*order(right, edge[0], edge[1]))
+    e_other, _ = merge_ports(*order(right, edge[2], edge[3]))
+    e_merged, e_saved = merge_ports(*order(upper, e_mine, e_other))
+    outs = [planes_of(matrix, 5) + values, e_merged]
+    tops = []
+    for kf, kl, z, tt, g, p, q in outs:
         tg = tt * recip(g)
         tops.append((jnp.where(last, z + tt * tg, g), jnp.where(last, p + tg * q, q), jnp.where(last, kf, kl)))
     write_pack(merged_out, *outs)
-    write_pack(pair_out, *pairs)
-    write_pack(saved_out, *saves)
+    write_pack(pair_out, pair, e_pair)
+    write_pack(saved_out, saved, e_saved)
     write_pack(top_out, *tops)
 
 
@@ -503,32 +598,43 @@
     cot = cotangent.reshape(512, 128)
     temp = saved_temp.reshape(512, 128)
     small = jax.ShapeDtypeStruct((8, 128), jnp.int32)
-    ypack, cond, fac, ties, cot, sub, dep, cls = call(
-        first_kernel,
-        [(8, 40, 128), (512, 128), (3, 63, 8, 128), (12, 8, 128), (512, 128), small, small, small],
-        [(512, 128), (3, 512, 128), (512, 128)],
-        "first",
+    cond, keep_m, send_m, cot, sub, dep, cls = call(
+        fields_kernel,
+        [(512, 128), (160, 128), (160, 128), (512, 128), small, small, small],
+        [(512, 128), (5, 64, 128)],
+        "fields",
         cot, temp, substrate_top, deposit_top, top_class,
         far_in=5, sems=5,
     )
+    other_m = swap(send_m, 1)
+    ypack, fac, ties = call(
+        first_kernel,
+        [(8, 40, 128), (3, 63, 8, 128), (12, 8, 128)],
+        [(3, 512, 128), (512, 128)],
+        "first",
+        cot, sub, dep, cls, cond,
+    )
     gat = lax.all_to_all(ypack, "gy", split_axis=0, concat_axis=0, tiled=True)
+    mm, core_c = call(core_matrix_kernel, [(160, 128), (224, 128)], [], "matrix_core", keep_m, other_m)
+    ring_m = [swap(mm, bit) for bit in (2, 6, 4)]
     keep, send, xfac, xhfac, a2, kh = call(
         second_kernel,
-        [(232, 128), (232, 128), (8, 24, 8, 128), (24, 1, 128), (512, 128), (8, 128)],
-        [(8, 32, 128), (512, 128), (512, 128), (7, 64, 128)],
+        [(72, 128), (72, 128), (8, 24, 8, 128), (24, 1, 128), (512, 128), (8, 128)],
+        [(8, 32, 128), (512, 128), (512, 128), (2, 64, 128)],
         "second",
         gat, fac, ties, cond, sub,
     )
-    m1, sv1 = call(core_kernel, [(232, 128), (200, 128)], [], "merge_core", keep, swap(send, 1))
-    near_z = swap(m1, 2)
-    far = swap(m1, 6)
-    mid = swap(m1, 4)
+    m1, sv1 = call(core_kernel, [(72, 128), (200, 128)], [], "merge_core", keep, swap(send, 1), core_c)
+    ring_v = [swap(m1, bit) for bit in (2, 6, 4)]
+    matrix, mine_c, other_c, ring_c = call(
+        ring_matrix_kernel, [(160, 128)] + [(224, 128)] * 3, [], "matrix_ring", mm, *ring_m
+    )
     m3, sv2, sv3, near = call(
         ring_kernel,
         [(232, 128), (200, 128), (200, 128), (104, 128)],
         [],
         "merge_ring",
-        m1, near_z, far, mid,
+        m1, *ring_v, matrix, mine_c, other_c, ring_c,
     )
     sv3, kh = lax.optimization_barrier((sv3, kh))
     coefs = call(coef_kernel, [(512, 128)] * 5, [], "coef", cond, kh, a2, cot, sub, dep, cls)

time: 37.4 us -> 36.8 us (0.984)
  starting transfers between devices: 12.3 us -> 23.5 us
  blocking collectives: 11.1 us -> 0 us
  waiting for transfers between devices: 9.03 us -> 7.43 us
  Pallas kernels: 4.2 us -> 5.03 us
    all_to_all x1 -> x0, blocking collectives: 11.1 us -> none  [body(): gat = lax.all_to_all(ypack, 'gy', split_axis=0, concat_axis=0, tiled=True)]
    all_to_all x0 -> x1, starting transfers between devices: none -> 5.85 us  [body(): gat = lax.all_to_all(ypack, 'gy', split_axis=0, concat_axis=0, tiled=True)]
    ppermute x6 -> x10, starting transfers between devices: 12.3 us -> 17.6 us  [swap(): return lax.ppermute(v, 'gx', [(i, i ^ bit) for i in range(16)])]
    ppermute x6 -> x10, waiting for transfers between devices: 9.03 us -> 7.43 us  [swap(): return lax.ppermute(v, 'gx', [(i, i ^ bit) for i in range(16)])]
    pallas_call x7 -> x10, Pallas kernels: 4.2 us -> 5.03 us  [call(): pl.pallas_call(kernel, out_shape=shapes, in_specs=[HBM if i < far_in else...]
  transfers between devices with their start and end apart: 6 -> 11, of which waited for: 5 -> 6; matrix products, arithmetic and copies ran while one was open for 0% -> 0% of each run, Pallas kernels for 1% -> 2%
where the time goes in v5:
time: 36.8 us; the launch traced here: 36.6 us
  starting transfers between devices  23.5 us (64%)
  waiting for transfers between devices  7.43 us (20%)
  Pallas kernels  5.03 us (14%)
  between operations  0.68 us (2%)
    ppermute x10, starting transfers between devices, swap(): return lax.ppermute(v, 'gx', [(i, i ^ bit) for i in range(16)])  17.6 us
    ppermute x10, waiting for transfers between devices, swap(): return lax.ppermute(v, 'gx', [(i, i ^ bit) for i in range(16)])  7.43 us
    all_to_all x1, starting transfers between devices, body(): gat = lax.all_to_all(ypack, 'gy', split_axis=0, concat_axis=0, tiled=True)  5.85 us
    pallas_call x10, Pallas kernels, call(): pl.pallas_call(kernel, out_shape=shapes, in_specs=[HBM if i < far_in else...  5.03 us
  transfers between devices with their start and end apart: 11, of which 6 were waited for; matrix products, arithmetic and copies ran while one was open for 0% of the time, Pallas kernels for 2%

profile of v5, /device:TPU:1, one launch (start us, length us, event | category | flops | bytes accessed | tf_op | source)
XLA Modules:
  0.0 36.6 jit_solution(13050597681606745402)
XLA Ops:
  0.6 1.2 %fields.1 = (f32[512,128]{1,0:T(8,128)S(1)}, f32[160,128]{1,0:T(8,128)S(1)}, f32[160,128]{1,0:T(8,128)S(1)}, f32[512,128]{1,0:T(8,128)S(1)}, s32[8,128]{1,0:T(8,...) custom-call(f32[512,128]{1,0:T(8,128)} %bitcast.4, f32[512,128]{1,0:T(8,128)} %bitcast.5, s32[8,128]{1,0:T(8,128)} %sub_in.1, ...), custom_call_target="tpu_custom_call" | custom-call | tf_op jit(solution)/shard_map/fields/pallas_call | solution.py:582
  1.9 1.3 %first.1 = (f32[8,40,128]{2,1,0:T(8,128)}, f32[3,63,8,128]{3,2,1,0:T(8,128)S(1)}, f32[12,8,128]{2,1,0:T(8,128)S(1)}) custom-call(f32[512,128]{1,0:T(8,128)S(1)} %get-tuple-element.47.cot, s32[8,128]{1,0:T(8,128)S(1)} %get-tuple-element.48.sub, s32[8,128]{1,0:T(8,128)S(1)} %get-tuple-element.49.dep, s32[8,128]{1,0:T(8,128)S(1)} %get-tuple-element.50.cls, ...), custom_call_target="tpu_custom_call" | custom-call | tf_op jit(solution)/shard_map/first/pallas_call | solution.py:582
  3.2 5.9 %all-to-all-start = ((f32[8,40,128]{2,1,0:T(8,128)}), f32[8,40,128]{2,1,0:T(8,128)S(1)}, u32[]{:S(2)}, u32[]{:S(2)}) async-start(f32[8,40,128]{2,1,0:T(8,128)} %get-tuple-element.52), calls=%async_computation | async-start | bytes 327680 | tf_op jit(solution)/shard_map/all_to_all | solution.py:617
  9.0 1.0 %collective-permute-start.1 = (f32[160,128]{1,0:T(8,128)S(1)}, f32[160,128]{1,0:T(8,128)S(1)}, u32[]{:S(2)}, u32[]{:S(2)}) collective-permute-start(f32[160,128]{1,0:T(8,128)S(1)} %get-tuple-element.58), channel_id=1, source_target_pairs={{0,8},{8,0},{16,24},{24,16},{32,40},{40,32},{48,56},{56,48},{64,72... | collective-permute-start | bytes 245768 | tf_op jit(solution)/shard_map/ppermute | solution.py:594
  10.0 0.9 %collective-permute-done.1.theirs = f32[160,128]{1,0:T(8,128)S(1)} collective-permute-done((f32[160,128]{1,0:T(8,128)S(1)}, f32[160,128]{1,0:T(8,128)S(1)}, u32[]{:S(2)}, u32[]{:S(2)}) %collective-permute-start.1) | collective-permute-done | bytes 81952 | tf_op jit(solution)/shard_map/ppermute | solution.py:594
  10.9 1.7 %collective-permute-start.5 = (f32[160,128]{1,0:T(8,128)S(1)}, f32[160,128]{1,0:T(8,128)S(1)}, u32[]{:S(2)}, u32[]{:S(2)}) collective-permute-start(f32[160,128]{1,0:T(8,128)S(1)} %get-tuple-element.61.own), channel_id=1, source_target_pairs={{0,16},{8,24},{16,0},{24,8},{32,48},{40,56},{48,32},{56,40},{64,80... | collective-permute-start | bytes 245768 | tf_op jit(solution)/shard_map/ppermute | solution.py:594
  12.7 2.2 %collective-permute-start.6 = (f32[160,128]{1,0:T(8,128)S(1)}, f32[160,128]{1,0:T(8,128)S(1)}, u32[]{:S(2)}, u32[]{:S(2)}) collective-permute-start(f32[160,128]{1,0:T(8,128)S(1)} %get-tuple-element.61.own), channel_id=1, source_target_pairs={{0,48},{8,56},{16,32},{24,40},{32,16},{40,24},{48,0},{56,8},{64,11... | collective-permute-start | bytes 245768 | tf_op jit(solution)/shard_map/ppermute | solution.py:594
  14.9 1.1 %collective-permute-start.7 = (f32[160,128]{1,0:T(8,128)S(1)}, f32[160,128]{1,0:T(8,128)S(1)}, u32[]{:S(2)}, u32[]{:S(2)}) collective-permute-start(f32[160,128]{1,0:T(8,128)S(1)} %get-tuple-element.61.own), channel_id=1, source_target_pairs={{0,32},{8,40},{16,48},{24,56},{32,0},{40,8},{48,16},{56,24},{64,96... | collective-permute-start | bytes 245768 | tf_op jit(solution)/shard_map/ppermute | solution.py:594
  16.0 0.0 all-to-all-done.gat
  16.0 0.4 %second.1 = (f32[72,128]{1,0:T(8,128)S(1)}, f32[72,128]{1,0:T(8,128)S(1)}, f32[8,24,8,128]{3,2,1,0:T(8,128)S(1)}, f32[24,1,128]{2,1,0:T(1,128)S(1)}, f32[512,128]{1,0:T(8,128)S(1)}, /*index=5*/f32[8,128]{1,0:T(8,128)S(1)}) custom-call(f32[8,40,128]{2,1,0:T(8,128)S(1)} %all-to-all-done.gat, f32[3,63,8,128]{3,2,1,0:T(8,128)S(1)} %get-tuple-element.53.fac, ...), custom_call_target="tpu_custom_call" | custom-call | tf_op jit(solution)/shard_map/second/pallas_call | solution.py:582
  16.4 1.0 %collective-permute-start = (f32[72,128]{1,0:T(8,128)S(1)}, f32[72,128]{1,0:T(8,128)S(1)}, u32[]{:S(2)}, u32[]{:S(2)}) collective-permute-start(f32[72,128]{1,0:T(8,128)S(1)} %get-tuple-element.56), channel_id=1, source_target_pairs={{0,8},{8,0},{16,24},{24,16},{32,40},{40,32},{48,56},{56,48},{64,72... | collective-permute-start | bytes 110600 | tf_op jit(solution)/shard_map/ppermute | solution.py:594
  17.4 0.9 %collective-permute-done.theirs = f32[72,128]{1,0:T(8,128)S(1)} collective-permute-done((f32[72,128]{1,0:T(8,128)S(1)}, f32[72,128]{1,0:T(8,128)S(1)}, u32[]{:S(2)}, u32[]{:S(2)}) %collective-permute-start) | collective-permute-done | bytes 36896 | tf_op jit(solution)/shard_map/ppermute | solution.py:594
  18.3 1.4 %collective-permute-start.2 = (f32[72,128]{1,0:T(8,128)S(1)}, f32[72,128]{1,0:T(8,128)S(1)}, u32[]{:S(2)}, u32[]{:S(2)}) collective-permute-start(f32[72,128]{1,0:T(8,128)S(1)} %get-tuple-element.60.own), channel_id=1, source_target_pairs={{0,16},{8,24},{16,0},{24,8},{32,48},{40,56},{48,32},{56,40},{64,80... | collective-permute-start | bytes 110600 | tf_op jit(solution)/shard_map/ppermute | solution.py:594
  19.7 2.2 %collective-permute-start.3 = (f32[72,128]{1,0:T(8,128)S(1)}, f32[72,128]{1,0:T(8,128)S(1)}, u32[]{:S(2)}, u32[]{:S(2)}) collective-permute-start(f32[72,128]{1,0:T(8,128)S(1)} %get-tuple-element.60.own), channel_id=1, source_target_pairs={{0,48},{8,56},{16,32},{24,40},{32,16},{40,24},{48,0},{56,8},{64,11... | collective-permute-start | bytes 110600 | tf_op jit(solution)/shard_map/ppermute | solution.py:594
  21.9 0.0 collective-permute-done.5.near
  21.9 1.1 %collective-permute-start.4 = (f32[72,128]{1,0:T(8,128)S(1)}, f32[72,128]{1,0:T(8,128)S(1)}, u32[]{:S(2)}, u32[]{:S(2)}) collective-permute-start(f32[72,128]{1,0:T(8,128)S(1)} %get-tuple-element.60.own), channel_id=1, source_target_pairs={{0,32},{8,40},{16,48},{24,56},{32,0},{40,8},{48,16},{56,24},{64,96... | collective-permute-start | bytes 110600 | tf_op jit(solution)/shard_map/ppermute | solution.py:594
  23.0 0.0 collective-permute-done.6.far
  23.0 0.0 collective-permute-done.7.mid
  23.0 0.1 matrix_ring.1
  23.1 0.0 collective-permute-done.2.near
  23.1 0.6 %collective-permute-done.3.far = f32[72,128]{1,0:T(8,128)S(1)} collective-permute-done((f32[72,128]{1,0:T(8,128)S(1)}, f32[72,128]{1,0:T(8,128)S(1)}, u32[]{:S(2)}, u32[]{:S(2)}) %collective-permute-start.3) | collective-permute-done | bytes 36896 | tf_op jit(solution)/shard_map/ppermute | solution.py:594
  23.7 2.5 %collective-permute-done.4.mid = f32[72,128]{1,0:T(8,128)S(1)} collective-permute-done((f32[72,128]{1,0:T(8,128)S(1)}, f32[72,128]{1,0:T(8,128)S(1)}, u32[]{:S(2)}, u32[]{:S(2)}) %collective-permute-start.4) | collective-permute-done | bytes 36896 | tf_op jit(solution)/shard_map/ppermute | solution.py:594
  26.2 0.1 merge_ring.1
  26.3 2.7 %collective-permute-start.8 = (f32[104,128]{1,0:T(8,128)S(1)}, f32[104,128]{1,0:T(8,128)S(1)}, u32[]{:S(2)}, u32[]{:S(2)}) collective-permute-start(f32[104,128]{1,0:T(8,128)S(1)} %get-tuple-element.67.near), channel_id=1, source_target_pairs={{0,64},{8,72},{16,80},{24,88},{32,96},{40,104},{48,112},{56,120},{... | collective-permute-start | bytes 159752 | tf_op jit(solution)/shard_map/ppermute | solution.py:594
  29.0 0.2 coef.1
  29.3 1.6 %collective-permute-done.8.theirs = f32[104,128]{1,0:T(8,128)S(1)} collective-permute-done((f32[104,128]{1,0:T(8,128)S(1)}, f32[104,128]{1,0:T(8,128)S(1)}, u32[]{:S(2)}, u32[]{:S(2)}) %collective-permute-start.8) | collective-permute-done | bytes 53280 | tf_op jit(solution)/shard_map/ppermute | solution.py:594
  30.9 0.1 top.1
  30.9 3.3 %collective-permute-start.9 = (f32[64,128]{1,0:T(8,128)S(1)}, f32[64,128]{1,0:T(8,128)S(1)}, u32[]{:S(2)}, u32[]{:S(2)}) collective-permute-start(f32[64,128]{1,0:T(8,128)S(1)} %get-tuple-element.82), channel_id=1, source_target_pairs={{0,8},{8,0},{16,24},{24,16},{32,40},{40,32},{48,56},{56,48},{64,72... | collective-permute-start | bytes 98312 | tf_op jit(solution)/shard_map/ppermute | solution.py:594
  34.2 0.9 %collective-permute-done.9.got = f32[64,128]{1,0:T(8,128)S(1)} collective-permute-done((f32[64,128]{1,0:T(8,128)S(1)}, f32[64,128]{1,0:T(8,128)S(1)}, u32[]{:S(2)}, u32[]{:S(2)}) %collective-permute-start.9) | collective-permute-done | bytes 32800 | tf_op jit(solution)/shard_map/ppermute | solution.py:594
  35.1 1.5 %last.1 = (f32[512,128]{1,0:T(8,128)}, f32[512,128]{1,0:T(8,128)}) custom-call(f32[72,128]{1,0:T(8,128)S(1)} %get-tuple-element.81.own, f32[64,128]{1,0:T(8,128)S(1)} %collective-permute-done.9.got, f32[8,24,8,128]{3,2,1,0:T(8,128)S(1)} %get-tuple-element.83.xfac, f32[24,1,128]{2,1,0:T(1,128)S(1)} %get-tuple-element.84.xhfac, ...), custom_call_target="tpu_custom_call" | custom-call | tf_op jit(solution)/shard_map/last/pallas_call | solution.py:582
  (2 shorter events, 0.1 us)
Async XLA Ops:
  3.2 12.8 %all-to-all-start = ((f32[8,40,128]{2,1,0:T(8,128)}), f32[8,40,128]{2,1,0:T(8,128)S(1)}, u32[]{:S(2)}, u32[]{:S(2)}) async-start(f32[8,40,128]{2,1,0:T(8,128)} %get-tuple-element.52), calls=%async_computation | async-start | bytes 327680 | tf_op jit(solution)/shard_map/all_to_all | solution.py:617
  9.0 1.9 %collective-permute-start.1 = (f32[160,128]{1,0:T(8,128)S(1)}, f32[160,128]{1,0:T(8,128)S(1)}, u32[]{:S(2)}, u32[]{:S(2)}) collective-permute-start(f32[160,128]{1,0:T(8,128)S(1)} %get-tuple-element.58), channel_id=1, source_target_pairs={{0,8},{8,0},{16,24},{24,16},{32,40},{40,32},{48,56},{56,48},{64,72... | collective-permute-start | bytes 245768 | tf_op jit(solution)/shard_map/ppermute | solution.py:594
  10.9 11.0 %collective-permute-start.5 = (f32[160,128]{1,0:T(8,128)S(1)}, f32[160,128]{1,0:T(8,128)S(1)}, u32[]{:S(2)}, u32[]{:S(2)}) collective-permute-start(f32[160,128]{1,0:T(8,128)S(1)} %get-tuple-element.61.own), channel_id=1, source_target_pairs={{0,16},{8,24},{16,0},{24,8},{32,48},{40,56},{48,32},{56,40},{64,80... | collective-permute-start | bytes 245768 | tf_op jit(solution)/shard_map/ppermute | solution.py:594
  12.7 10.3 %collective-permute-start.6 = (f32[160,128]{1,0:T(8,128)S(1)}, f32[160,128]{1,0:T(8,128)S(1)}, u32[]{:S(2)}, u32[]{:S(2)}) collective-permute-start(f32[160,128]{1,0:T(8,128)S(1)} %get-tuple-element.61.own), channel_id=1, source_target_pairs={{0,48},{8,56},{16,32},{24,40},{32,16},{40,24},{48,0},{56,8},{64,11... | collective-permute-start | bytes 245768 | tf_op jit(solution)/shard_map/ppermute | solution.py:594
  14.9 8.1 %collective-permute-start.7 = (f32[160,128]{1,0:T(8,128)S(1)}, f32[160,128]{1,0:T(8,128)S(1)}, u32[]{:S(2)}, u32[]{:S(2)}) collective-permute-start(f32[160,128]{1,0:T(8,128)S(1)} %get-tuple-element.61.own), channel_id=1, source_target_pairs={{0,32},{8,40},{16,48},{24,56},{32,0},{40,8},{48,16},{56,24},{64,96... | collective-permute-start | bytes 245768 | tf_op jit(solution)/shard_map/ppermute | solution.py:594
  16.4 1.9 %collective-permute-start = (f32[72,128]{1,0:T(8,128)S(1)}, f32[72,128]{1,0:T(8,128)S(1)}, u32[]{:S(2)}, u32[]{:S(2)}) collective-permute-start(f32[72,128]{1,0:T(8,128)S(1)} %get-tuple-element.56), channel_id=1, source_target_pairs={{0,8},{8,0},{16,24},{24,16},{32,40},{40,32},{48,56},{56,48},{64,72... | collective-permute-start | bytes 110600 | tf_op jit(solution)/shard_map/ppermute | solution.py:594
  18.3 4.8 %collective-permute-start.2 = (f32[72,128]{1,0:T(8,128)S(1)}, f32[72,128]{1,0:T(8,128)S(1)}, u32[]{:S(2)}, u32[]{:S(2)}) collective-permute-start(f32[72,128]{1,0:T(8,128)S(1)} %get-tuple-element.60.own), channel_id=1, source_target_pairs={{0,16},{8,24},{16,0},{24,8},{32,48},{40,56},{48,32},{56,40},{64,80... | collective-permute-start | bytes 110600 | tf_op jit(solution)/shard_map/ppermute | solution.py:594
  19.7 4.0 %collective-permute-start.3 = (f32[72,128]{1,0:T(8,128)S(1)}, f32[72,128]{1,0:T(8,128)S(1)}, u32[]{:S(2)}, u32[]{:S(2)}) collective-permute-start(f32[72,128]{1,0:T(8,128)S(1)} %get-tuple-element.60.own), channel_id=1, source_target_pairs={{0,48},{8,56},{16,32},{24,40},{32,16},{40,24},{48,0},{56,8},{64,11... | collective-permute-start | bytes 110600 | tf_op jit(solution)/shard_map/ppermute | solution.py:594
  21.9 4.3 %collective-permute-start.4 = (f32[72,128]{1,0:T(8,128)S(1)}, f32[72,128]{1,0:T(8,128)S(1)}, u32[]{:S(2)}, u32[]{:S(2)}) collective-permute-start(f32[72,128]{1,0:T(8,128)S(1)} %get-tuple-element.60.own), channel_id=1, source_target_pairs={{0,32},{8,40},{16,48},{24,56},{32,0},{40,8},{48,16},{56,24},{64,96... | collective-permute-start | bytes 110600 | tf_op jit(solution)/shard_map/ppermute | solution.py:594
  26.3 4.6 %collective-permute-start.8 = (f32[104,128]{1,0:T(8,128)S(1)}, f32[104,128]{1,0:T(8,128)S(1)}, u32[]{:S(2)}, u32[]{:S(2)}) collective-permute-start(f32[104,128]{1,0:T(8,128)S(1)} %get-tuple-element.67.near), channel_id=1, source_target_pairs={{0,64},{8,72},{16,80},{24,88},{32,96},{40,104},{48,112},{56,120},{... | collective-permute-start | bytes 159752 | tf_op jit(solution)/shard_map/ppermute | solution.py:594
  30.9 4.1 %collective-permute-start.9 = (f32[64,128]{1,0:T(8,128)S(1)}, f32[64,128]{1,0:T(8,128)S(1)}, u32[]{:S(2)}, u32[]{:S(2)}) collective-permute-start(f32[64,128]{1,0:T(8,128)S(1)} %get-tuple-element.82), channel_id=1, source_target_pairs={{0,8},{8,0},{16,24},{24,16},{32,40},{40,32},{48,56},{56,48},{64,72... | collective-permute-start | bytes 98312 | tf_op jit(solution)/shard_map/ppermute | solution.py:594

commit v6 on v5

--- a/solution.py
+++ b/solution.py
@@ -174,8 +174,13 @@
     return jnp.where(me_x == 0, R * SIDE, 0.0), jnp.where(me_x == 15, R * SIDE, 0.0)
 
 
+def own_half():
+    me_x = lax.axis_index("gx")
+    return lax.rem(me_x + lax.div(me_x, 2) + lax.div(me_x, 8), 2)
+
+
 def split_halves(planes, keep, send):
-    core = lax.rem(lax.axis_index("gx"), 2)
+    core = own_half()
     for i in range(planes.shape[0]):
         keep[32 * i : 32 * i + 32] = planes[i, pl.ds(pl.multiple_of(32 * core, 32), 32), :]
         send[32 * i : 32 * i + 32] = planes[i, pl.ds(pl.multiple_of(32 - 32 * core, 32), 32), :]
@@ -523,7 +528,7 @@
 def last_kernel(
     own, got, xfac, xhfac, k_y, k_l, k_z, k_s, base, sub, temp_out, src_out, s1, fu, t_buf, s_buf, sems
 ):
-    core = lax.rem(lax.axis_index("gx"), 2)
+    core = own_half()
     for i in range(2):
         fu[i, pl.ds(pl.multiple_of(32 * core, 32), 32), :] = own[32 * i : 32 * i + 32]
         fu[i, pl.ds(pl.multiple_of(32 - 32 * core, 32), 32), :] = got[32 * i : 32 * i + 32]
@@ -614,9 +619,10 @@
         "first",
         cot, sub, dep, cls, cond,
     )
+    mm, core_c = call(core_matrix_kernel, [(160, 128), (224, 128)], [], "matrix_core", keep_m, other_m)
+    mm, ypack = lax.optimization_barrier((mm, ypack))
     gat = lax.all_to_all(ypack, "gy", split_axis=0, concat_axis=0, tiled=True)
-    mm, core_c = call(core_matrix_kernel, [(160, 128), (224, 128)], [], "matrix_core", keep_m, other_m)
-    ring_m = [swap(mm, bit) for bit in (2, 6, 4)]
+    ring_m = [swap(mm, bit) for bit in (3, 7, 4)]
     keep, send, xfac, xhfac, a2, kh = call(
         second_kernel,
         [(72, 128), (72, 128), (8, 24, 8, 128), (24, 1, 128), (512, 128), (8, 128)],
@@ -625,7 +631,7 @@
         gat, fac, ties, cond, sub,
     )
     m1, sv1 = call(core_kernel, [(72, 128), (200, 128)], [], "merge_core", keep, swap(send, 1), core_c)
-    ring_v = [swap(m1, bit) for bit in (2, 6, 4)]
+    ring_v = [swap(m1, bit) for bit in (3, 7, 4)]
     matrix, mine_c, other_c, ring_c = call(
         ring_matrix_kernel, [(160, 128)] + [(224, 128)] * 3, [], "matrix_ring", mm, *ring_m
     )
@@ -638,7 +644,7 @@
     )
     sv3, kh = lax.optimization_barrier((sv3, kh))
     coefs = call(coef_kernel, [(512, 128)] * 5, [], "coef", cond, kh, a2, cot, sub, dep, cls)
-    opposite = swap(near, 8)
+    opposite = swap(near, 9)
     sv3, coefs = lax.optimization_barrier((sv3, coefs))
     own, out = call(top_kernel, [(72, 128), (64, 128)], [], "top", m3, near, opposite, sv1, sv2, sv3)
     got = swap(out, 1)

time: 36.8 us -> 36.8 us (level)
    all_to_all x1, starting transfers between devices: 5.85 us -> 5.16 us  [body(): gat = lax.all_to_all(ypack, 'gy', split_axis=0, concat_axis=0, tiled=True)]
    ppermute x10, starting transfers between devices: 17.6 us -> 18.1 us  [swap(): return lax.ppermute(v, 'gx', [(i, i ^ bit) for i in range(16)])]
  transfers between devices with their start and end apart: 11 -> 11, of which waited for: 6 -> 6; matrix products, arithmetic and copies ran while one was open for 0% -> 0% of each run, Pallas kernels for 2% -> 6%
where the time goes in v6:
time: 36.8 us; the launch traced here: 36.6 us
  starting transfers between devices  23.2 us (63%)
  waiting for transfers between devices  7.68 us (21%)
  Pallas kernels  4.96 us (13%)
  between operations  0.68 us (2%)
    ppermute x10, starting transfers between devices, swap(): return lax.ppermute(v, 'gx', [(i, i ^ bit) for i in range(16)])  18.1 us
    ppermute x10, waiting for transfers between devices, swap(): return lax.ppermute(v, 'gx', [(i, i ^ bit) for i in range(16)])  7.32 us
    all_to_all x1, starting transfers between devices, body(): gat = lax.all_to_all(ypack, 'gy', split_axis=0, concat_axis=0, tiled=True)  5.16 us
    pallas_call x10, Pallas kernels, call(): pl.pallas_call(kernel, out_shape=shapes, in_specs=[HBM if i < far_in else...  4.96 us
  transfers between devices with their start and end apart: 11, of which 6 were waited for; matrix products, arithmetic and copies ran while one was open for 0% of the time, Pallas kernels for 6%

profile of v6, /device:TPU:1, one launch (start us, length us, event | category | flops | bytes accessed | tf_op | source)
XLA Modules:
  0.0 36.6 jit_solution(5169994313157676542)
XLA Ops:
  0.6 1.2 %fields.1 = (f32[512,128]{1,0:T(8,128)S(1)}, f32[160,128]{1,0:T(8,128)S(1)}, f32[160,128]{1,0:T(8,128)S(1)}, f32[512,128]{1,0:T(8,128)S(1)}, s32[8,128]{1,0:T(8,...) custom-call(f32[512,128]{1,0:T(8,128)} %bitcast.4, f32[512,128]{1,0:T(8,128)} %bitcast.5, s32[8,128]{1,0:T(8,128)} %sub_in.1, ...), custom_call_target="tpu_custom_call" | custom-call | tf_op jit(solution)/shard_map/fields/pallas_call | solution.py:587
  1.9 1.5 %collective-permute-start = (f32[160,128]{1,0:T(8,128)S(1)}, f32[160,128]{1,0:T(8,128)S(1)}, u32[]{:S(2)}, u32[]{:S(2)}) collective-permute-start(f32[160,128]{1,0:T(8,128)S(1)} %get-tuple-element.50), channel_id=1, source_target_pairs={{0,8},{8,0},{16,24},{24,16},{32,40},{40,32},{48,56},{56,48},{64,72... | collective-permute-start | bytes 245768 | tf_op jit(solution)/shard_map/ppermute | solution.py:599
  3.3 1.3 %first.1 = (f32[8,40,128]{2,1,0:T(8,128)}, f32[3,63,8,128]{3,2,1,0:T(8,128)S(1)}, f32[12,8,128]{2,1,0:T(8,128)S(1)}) custom-call(f32[512,128]{1,0:T(8,128)S(1)} %get-tuple-element.52.cot, s32[8,128]{1,0:T(8,128)S(1)} %get-tuple-element.53.sub, s32[8,128]{1,0:T(8,128)S(1)} %get-tuple-element.54.dep, s32[8,128]{1,0:T(8,128)S(1)} %get-tuple-element.55.cls, ...), custom_call_target="tpu_custom_call" | custom-call | tf_op jit(solution)/shard_map/first/pallas_call | solution.py:587
  4.6 0.0 collective-permute-done.theirs
  4.7 5.2 %all-to-all-start = ((f32[8,40,128]{2,1,0:T(8,128)}), f32[8,40,128]{2,1,0:T(8,128)S(1)}, u32[]{:S(2)}, u32[]{:S(2)}) async-start(f32[8,40,128]{2,1,0:T(8,128)} %get-tuple-element.58), calls=%async_computation | async-start | bytes 327680 | tf_op jit(solution)/shard_map/all_to_all | solution.py:624
  9.8 1.8 %collective-permute-start.5 = (f32[160,128]{1,0:T(8,128)S(1)}, f32[160,128]{1,0:T(8,128)S(1)}, u32[]{:S(2)}, u32[]{:S(2)}) collective-permute-start(f32[160,128]{1,0:T(8,128)S(1)} %get-tuple-element.65.own), channel_id=1, source_target_pairs={{0,24},{8,16},{16,8},{24,0},{32,56},{40,48},{48,40},{56,32},{64,88... | collective-permute-start | bytes 245768 | tf_op jit(solution)/shard_map/ppermute | solution.py:599
  11.7 2.3 %collective-permute-start.6 = (f32[160,128]{1,0:T(8,128)S(1)}, f32[160,128]{1,0:T(8,128)S(1)}, u32[]{:S(2)}, u32[]{:S(2)}) collective-permute-start(f32[160,128]{1,0:T(8,128)S(1)} %get-tuple-element.65.own), channel_id=1, source_target_pairs={{0,56},{8,48},{16,40},{24,32},{32,24},{40,16},{48,8},{56,0},{64,12... | collective-permute-start | bytes 245768 | tf_op jit(solution)/shard_map/ppermute | solution.py:599
  14.0 1.0 %collective-permute-start.7 = (f32[160,128]{1,0:T(8,128)S(1)}, f32[160,128]{1,0:T(8,128)S(1)}, u32[]{:S(2)}, u32[]{:S(2)}) collective-permute-start(f32[160,128]{1,0:T(8,128)S(1)} %get-tuple-element.65.own), channel_id=1, source_target_pairs={{0,32},{8,40},{16,48},{24,56},{32,0},{40,8},{48,16},{56,24},{64,96... | collective-permute-start | bytes 245768 | tf_op jit(solution)/shard_map/ppermute | solution.py:599
  15.0 0.4 %all-to-all-done.gat = f32[8,40,128]{2,1,0:T(8,128)S(1)} async-done(((f32[8,40,128]{2,1,0:T(8,128)}), f32[8,40,128]{2,1,0:T(8,128)S(1)}, u32[]{:S(2)}, u32[]{:S(2)}) %all-to-all-start) | async-done | bytes 163872 | tf_op jit(solution)/shard_map/all_to_all | solution.py:624
  15.3 0.4 %second.1 = (f32[72,128]{1,0:T(8,128)S(1)}, f32[72,128]{1,0:T(8,128)S(1)}, f32[8,24,8,128]{3,2,1,0:T(8,128)S(1)}, f32[24,1,128]{2,1,0:T(1,128)S(1)}, f32[512,128]{1,0:T(8,128)S(1)}, /*index=5*/f32[8,128]{1,0:T(8,128)S(1)}) custom-call(f32[8,40,128]{2,1,0:T(8,128)S(1)} %all-to-all-done.gat, f32[3,63,8,128]{3,2,1,0:T(8,128)S(1)} %get-tuple-element.59.fac, ...), custom_call_target="tpu_custom_call" | custom-call | tf_op jit(solution)/shard_map/second/pallas_call | solution.py:587
  15.8 1.6 %collective-permute-start.1 = (f32[72,128]{1,0:T(8,128)S(1)}, f32[72,128]{1,0:T(8,128)S(1)}, u32[]{:S(2)}, u32[]{:S(2)}) collective-permute-start(f32[72,128]{1,0:T(8,128)S(1)} %get-tuple-element.62), channel_id=1, source_target_pairs={{0,8},{8,0},{16,24},{24,16},{32,40},{40,32},{48,56},{56,48},{64,72... | collective-permute-start | bytes 110600 | tf_op jit(solution)/shard_map/ppermute | solution.py:599
  17.4 0.9 %collective-permute-done.1.theirs = f32[72,128]{1,0:T(8,128)S(1)} collective-permute-done((f32[72,128]{1,0:T(8,128)S(1)}, f32[72,128]{1,0:T(8,128)S(1)}, u32[]{:S(2)}, u32[]{:S(2)}) %collective-permute-start.1) | collective-permute-done | bytes 36896 | tf_op jit(solution)/shard_map/ppermute | solution.py:599
  18.3 2.0 %collective-permute-start.2 = (f32[72,128]{1,0:T(8,128)S(1)}, f32[72,128]{1,0:T(8,128)S(1)}, u32[]{:S(2)}, u32[]{:S(2)}) collective-permute-start(f32[72,128]{1,0:T(8,128)S(1)} %get-tuple-element.64.own), channel_id=1, source_target_pairs={{0,24},{8,16},{16,8},{24,0},{32,56},{40,48},{48,40},{56,32},{64,88... | collective-permute-start | bytes 110600 | tf_op jit(solution)/shard_map/ppermute | solution.py:599
  20.3 2.3 %collective-permute-start.3 = (f32[72,128]{1,0:T(8,128)S(1)}, f32[72,128]{1,0:T(8,128)S(1)}, u32[]{:S(2)}, u32[]{:S(2)}) collective-permute-start(f32[72,128]{1,0:T(8,128)S(1)} %get-tuple-element.64.own), channel_id=1, source_target_pairs={{0,56},{8,48},{16,40},{24,32},{32,24},{40,16},{48,8},{56,0},{64,12... | collective-permute-start | bytes 110600 | tf_op jit(solution)/shard_map/ppermute | solution.py:599
  22.6 0.0 collective-permute-done.5.near
  22.6 1.0 %collective-permute-start.4 = (f32[72,128]{1,0:T(8,128)S(1)}, f32[72,128]{1,0:T(8,128)S(1)}, u32[]{:S(2)}, u32[]{:S(2)}) collective-permute-start(f32[72,128]{1,0:T(8,128)S(1)} %get-tuple-element.64.own), channel_id=1, source_target_pairs={{0,32},{8,40},{16,48},{24,56},{32,0},{40,8},{48,16},{56,24},{64,96... | collective-permute-start | bytes 110600 | tf_op jit(solution)/shard_map/ppermute | solution.py:599
  23.6 0.0 collective-permute-done.6.far
  23.6 0.0 collective-permute-done.7.mid
  23.6 0.1 matrix_ring.1
  23.7 0.0 collective-permute-done.2.near
  23.7 1.2 %collective-permute-done.3.far = f32[72,128]{1,0:T(8,128)S(1)} collective-permute-done((f32[72,128]{1,0:T(8,128)S(1)}, f32[72,128]{1,0:T(8,128)S(1)}, u32[]{:S(2)}, u32[]{:S(2)}) %collective-permute-start.3) | collective-permute-done | bytes 36896 | tf_op jit(solution)/shard_map/ppermute | solution.py:599
  24.9 2.0 %collective-permute-done.4.mid = f32[72,128]{1,0:T(8,128)S(1)} collective-permute-done((f32[72,128]{1,0:T(8,128)S(1)}, f32[72,128]{1,0:T(8,128)S(1)}, u32[]{:S(2)}, u32[]{:S(2)}) %collective-permute-start.4) | collective-permute-done | bytes 36896 | tf_op jit(solution)/shard_map/ppermute | solution.py:599
  26.9 0.1 merge_ring.1
  27.0 4.1 %collective-permute-start.8 = (f32[104,128]{1,0:T(8,128)S(1)}, f32[104,128]{1,0:T(8,128)S(1)}, u32[]{:S(2)}, u32[]{:S(2)}) collective-permute-start(f32[104,128]{1,0:T(8,128)S(1)} %get-tuple-element.71.near), channel_id=1, source_target_pairs={{0,72},{8,64},{16,88},{24,80},{32,104},{40,96},{48,120},{56,112},{... | collective-permute-start | bytes 159752 | tf_op jit(solution)/shard_map/ppermute | solution.py:599
  31.0 0.2 coef.1
  31.3 2.4 %collective-permute-done.8.theirs = f32[104,128]{1,0:T(8,128)S(1)} collective-permute-done((f32[104,128]{1,0:T(8,128)S(1)}, f32[104,128]{1,0:T(8,128)S(1)}, u32[]{:S(2)}, u32[]{:S(2)}) %collective-permute-start.8) | collective-permute-done | bytes 53280 | tf_op jit(solution)/shard_map/ppermute | solution.py:599
  33.7 0.1 top.1
  33.7 0.5 %collective-permute-start.9 = (f32[64,128]{1,0:T(8,128)S(1)}, f32[64,128]{1,0:T(8,128)S(1)}, u32[]{:S(2)}, u32[]{:S(2)}) collective-permute-start(f32[64,128]{1,0:T(8,128)S(1)} %get-tuple-element.86), channel_id=1, source_target_pairs={{0,8},{8,0},{16,24},{24,16},{32,40},{40,32},{48,56},{56,48},{64,72... | collective-permute-start | bytes 98312 | tf_op jit(solution)/shard_map/ppermute | solution.py:599
  34.3 0.9 %collective-permute-done.9.got = f32[64,128]{1,0:T(8,128)S(1)} collective-permute-done((f32[64,128]{1,0:T(8,128)S(1)}, f32[64,128]{1,0:T(8,128)S(1)}, u32[]{:S(2)}, u32[]{:S(2)}) %collective-permute-start.9) | collective-permute-done | bytes 32800 | tf_op jit(solution)/shard_map/ppermute | solution.py:599
  35.1 1.5 %last.1 = (f32[512,128]{1,0:T(8,128)}, f32[512,128]{1,0:T(8,128)}) custom-call(f32[72,128]{1,0:T(8,128)S(1)} %get-tuple-element.85.own, f32[64,128]{1,0:T(8,128)S(1)} %collective-permute-done.9.got, f32[8,24,8,128]{3,2,1,0:T(8,128)S(1)} %get-tuple-element.87.xfac, f32[24,1,128]{2,1,0:T(1,128)S(1)} %get-tuple-element.88.xhfac, ...), custom_call_target="tpu_custom_call" | custom-call | tf_op jit(solution)/shard_map/last/pallas_call | solution.py:587
  (2 shorter events, 0.1 us)
Async XLA Ops:
  1.9 2.8 %collective-permute-start = (f32[160,128]{1,0:T(8,128)S(1)}, f32[160,128]{1,0:T(8,128)S(1)}, u32[]{:S(2)}, u32[]{:S(2)}) collective-permute-start(f32[160,128]{1,0:T(8,128)S(1)} %get-tuple-element.50), channel_id=1, source_target_pairs={{0,8},{8,0},{16,24},{24,16},{32,40},{40,32},{48,56},{56,48},{64,72... | collective-permute-start | bytes 245768 | tf_op jit(solution)/shard_map/ppermute | solution.py:599
  4.7 10.6 %all-to-all-start = ((f32[8,40,128]{2,1,0:T(8,128)}), f32[8,40,128]{2,1,0:T(8,128)S(1)}, u32[]{:S(2)}, u32[]{:S(2)}) async-start(f32[8,40,128]{2,1,0:T(8,128)} %get-tuple-element.58), calls=%async_computation | async-start | bytes 327680 | tf_op jit(solution)/shard_map/all_to_all | solution.py:624
  9.8 12.7 %collective-permute-start.5 = (f32[160,128]{1,0:T(8,128)S(1)}, f32[160,128]{1,0:T(8,128)S(1)}, u32[]{:S(2)}, u32[]{:S(2)}) collective-permute-start(f32[160,128]{1,0:T(8,128)S(1)} %get-tuple-element.65.own), channel_id=1, source_target_pairs={{0,24},{8,16},{16,8},{24,0},{32,56},{40,48},{48,40},{56,32},{64,88... | collective-permute-start | bytes 245768 | tf_op jit(solution)/shard_map/ppermute | solution.py:599
  11.7 11.9 %collective-permute-start.6 = (f32[160,128]{1,0:T(8,128)S(1)}, f32[160,128]{1,0:T(8,128)S(1)}, u32[]{:S(2)}, u32[]{:S(2)}) collective-permute-start(f32[160,128]{1,0:T(8,128)S(1)} %get-tuple-element.65.own), channel_id=1, source_target_pairs={{0,56},{8,48},{16,40},{24,32},{32,24},{40,16},{48,8},{56,0},{64,12... | collective-permute-start | bytes 245768 | tf_op jit(solution)/shard_map/ppermute | solution.py:599
  14.0 9.6 %collective-permute-start.7 = (f32[160,128]{1,0:T(8,128)S(1)}, f32[160,128]{1,0:T(8,128)S(1)}, u32[]{:S(2)}, u32[]{:S(2)}) collective-permute-start(f32[160,128]{1,0:T(8,128)S(1)} %get-tuple-element.65.own), channel_id=1, source_target_pairs={{0,32},{8,40},{16,48},{24,56},{32,0},{40,8},{48,16},{56,24},{64,96... | collective-permute-start | bytes 245768 | tf_op jit(solution)/shard_map/ppermute | solution.py:599
  15.8 2.5 %collective-permute-start.1 = (f32[72,128]{1,0:T(8,128)S(1)}, f32[72,128]{1,0:T(8,128)S(1)}, u32[]{:S(2)}, u32[]{:S(2)}) collective-permute-start(f32[72,128]{1,0:T(8,128)S(1)} %get-tuple-element.62), channel_id=1, source_target_pairs={{0,8},{8,0},{16,24},{24,16},{32,40},{40,32},{48,56},{56,48},{64,72... | collective-permute-start | bytes 110600 | tf_op jit(solution)/shard_map/ppermute | solution.py:599
  18.3 5.4 %collective-permute-start.2 = (f32[72,128]{1,0:T(8,128)S(1)}, f32[72,128]{1,0:T(8,128)S(1)}, u32[]{:S(2)}, u32[]{:S(2)}) collective-permute-start(f32[72,128]{1,0:T(8,128)S(1)} %get-tuple-element.64.own), channel_id=1, source_target_pairs={{0,24},{8,16},{16,8},{24,0},{32,56},{40,48},{48,40},{56,32},{64,88... | collective-permute-start | bytes 110600 | tf_op jit(solution)/shard_map/ppermute | solution.py:599
  20.3 4.6 %collective-permute-start.3 = (f32[72,128]{1,0:T(8,128)S(1)}, f32[72,128]{1,0:T(8,128)S(1)}, u32[]{:S(2)}, u32[]{:S(2)}) collective-permute-start(f32[72,128]{1,0:T(8,128)S(1)} %get-tuple-element.64.own), channel_id=1, source_target_pairs={{0,56},{8,48},{16,40},{24,32},{32,24},{40,16},{48,8},{56,0},{64,12... | collective-permute-start | bytes 110600 | tf_op jit(solution)/shard_map/ppermute | solution.py:599
  22.6 4.3 %collective-permute-start.4 = (f32[72,128]{1,0:T(8,128)S(1)}, f32[72,128]{1,0:T(8,128)S(1)}, u32[]{:S(2)}, u32[]{:S(2)}) collective-permute-start(f32[72,128]{1,0:T(8,128)S(1)} %get-tuple-element.64.own), channel_id=1, source_target_pairs={{0,32},{8,40},{16,48},{24,56},{32,0},{40,8},{48,16},{56,24},{64,96... | collective-permute-start | bytes 110600 | tf_op jit(solution)/shard_map/ppermute | solution.py:599
  27.0 6.7 %collective-permute-start.8 = (f32[104,128]{1,0:T(8,128)S(1)}, f32[104,128]{1,0:T(8,128)S(1)}, u32[]{:S(2)}, u32[]{:S(2)}) collective-permute-start(f32[104,128]{1,0:T(8,128)S(1)} %get-tuple-element.71.near), channel_id=1, source_target_pairs={{0,72},{8,64},{16,88},{24,80},{32,104},{40,96},{48,120},{56,112},{... | collective-permute-start | bytes 159752 | tf_op jit(solution)/shard_map/ppermute | solution.py:599
  33.7 1.4 %collective-permute-start.9 = (f32[64,128]{1,0:T(8,128)S(1)}, f32[64,128]{1,0:T(8,128)S(1)}, u32[]{:S(2)}, u32[]{:S(2)}) collective-permute-start(f32[64,128]{1,0:T(8,128)S(1)} %get-tuple-element.86), channel_id=1, source_target_pairs={{0,8},{8,0},{16,24},{24,16},{32,40},{40,32},{48,56},{56,48},{64,72... | collective-permute-start | bytes 98312 | tf_op jit(solution)/shard_map/ppermute | solution.py:599

commit v7 on v4

--- a/solution.py
+++ b/solution.py
@@ -206,6 +206,11 @@
     pack = jnp.concatenate(list(merged) + [cap_first, cap_last, jnp.zeros((4, 128), F32)], axis=0)
     for n in range(8):
         ypack[n] = pack
+
+
+def own_half():
+    me_x = lax.axis_index("gx")
+    return lax.rem(me_x + lax.div(me_x, 2) + lax.div(me_x, 8), 2)
 
 
 def second_kernel(gat, fac, ties, cond, sub, keep, send, xfac, xhfac, a2_out, kh_out, pick, flat, planes, xp):
@@ -301,7 +306,7 @@
             xp[i, 8 * chunk : 8 * chunk + 8] = port[i]
     levels, tie, port = x_chain(kh, caph, dh)
     store_x(xhfac, levels, tie)
-    core = lax.rem(me_x, 2)
+    core = own_half()
     for i in range(7):
         keep[32 * i : 32 * i + 32] = xp[i, pl.ds(pl.multiple_of(32 * core, 32), 32), :]
         send[32 * i : 32 * i + 32] = xp[i, pl.ds(pl.multiple_of(32 - 32 * core, 32), 32), :]
@@ -428,7 +433,7 @@
 def last_kernel(
     own, got, xfac, xhfac, k_y, k_l, k_z, k_s, base, sub, temp_out, src_out, s1, fu, t_buf, s_buf, sems
 ):
-    core = lax.rem(lax.axis_index("gx"), 2)
+    core = own_half()
     for i in range(2):
         fu[i, pl.ds(pl.multiple_of(32 * core, 32), 32), :] = own[32 * i : 32 * i + 32]
         fu[i, pl.ds(pl.multiple_of(32 - 32 * core, 32), 32), :] = got[32 * i : 32 * i + 32]
@@ -520,8 +525,8 @@
         gat, fac, ties, cond, sub,
     )
     m1, sv1 = call(core_kernel, [(232, 128), (200, 128)], [], "merge_core", keep, swap(send, 1))
-    near_z = swap(m1, 2)
-    far = swap(m1, 6)
+    near_z = swap(m1, 3)
+    far = swap(m1, 7)
     mid = swap(m1, 4)
     m3, sv2, sv3, near = call(
         ring_kernel,
@@ -532,7 +537,7 @@
     )
     sv3, kh = lax.optimization_barrier((sv3, kh))
     coefs = call(coef_kernel, [(512, 128)] * 5, [], "coef", cond, kh, a2, cot, sub, dep, cls)
-    opposite = swap(near, 8)
+    opposite = swap(near, 9)
     sv3, coefs = lax.optimization_barrier((sv3, coefs))
     own, out = call(top_kernel, [(72, 128), (64, 128)], [], "top", m3, near, opposite, sv1, sv2, sv3)
     got = swap(out, 1)

time: 37.4 us -> 37.5 us (level)
  waiting for transfers between devices: 9.03 us -> 10.2 us
  starting transfers between devices: 12.3 us -> 11.3 us
    ppermute x6, waiting for transfers between devices: 9.03 us -> 10.2 us  [swap(): return lax.ppermute(v, 'gx', [(i, i ^ bit) for i in range(16)])]
    ppermute x6, starting transfers between devices: 12.3 us -> 11.3 us  [swap(): return lax.ppermute(v, 'gx', [(i, i ^ bit) for i in range(16)])]
where the time goes in v7:
time: 37.5 us; the launch traced here: 37.4 us
  starting transfers between devices  11.3 us (30%)
  blocking collectives  11.1 us (30%)
  waiting for transfers between devices  10.2 us (27%)
  Pallas kernels  4.14 us (11%)
  between operations  0.67 us (2%)
    ppermute x6, starting transfers between devices, swap(): return lax.ppermute(v, 'gx', [(i, i ^ bit) for i in range(16)])  11.3 us
    all_to_all x1, blocking collectives, body(): gat = lax.all_to_all(ypack, 'gy', split_axis=0, concat_axis=0, tiled=True)  11.1 us
    ppermute x6, waiting for transfers between devices, swap(): return lax.ppermute(v, 'gx', [(i, i ^ bit) for i in range(16)])  10.2 us
    pallas_call x7, Pallas kernels, call(): pl.pallas_call(kernel, out_shape=shapes, in_specs=[HBM if i < far_in else...  4.14 us
  transfers between devices with their start and end apart: 6, of which 5 were waited for; matrix products, arithmetic and copies ran while one was open for 0% of the time, Pallas kernels for 1%

profile of v7, /device:TPU:1, one launch (start us, length us, event | category | flops | bytes accessed | tf_op | source)
XLA Modules:
  0.0 37.4 jit_solution(14319527440638419774)
XLA Ops:
  0.6 1.8 %first.1 = (f32[8,40,128]{2,1,0:T(8,128)S(1)}, f32[512,128]{1,0:T(8,128)S(1)}, f32[3,63,8,128]{3,2,1,0:T(8,128)S(1)}, f32[12,8,128]{2,1,0:T(8,128)S(1)}, f32[512...) custom-call(f32[512,128]{1,0:T(8,128)} %bitcast.4, f32[512,128]{1,0:T(8,128)} %bitcast.5, ...), custom_call_target="tpu_custom_call" | custom-call | tf_op jit(solution)/shard_map/first/pallas_call | solution.py:492
  2.4 11.1 %all_to_all.5.gat = f32[8,40,128]{2,1,0:T(8,128)S(1)} all-to-all(f32[8,40,128]{2,1,0:T(8,128)S(1)} %get-tuple-element.39), channel_id=1, replica_groups=mesh['gx'=16,'gy'=8] {'gy'}, dimensions={0} | all-to-all | bytes 327680 | tf_op jit(solution)/shard_map/all_to_all | solution.py:519
  13.4 0.5 %second.1 = (f32[232,128]{1,0:T(8,128)S(1)}, f32[232,128]{1,0:T(8,128)S(1)}, f32[8,24,8,128]{3,2,1,0:T(8,128)S(1)}, f32[24,1,128]{2,1,0:T(1,128)S(1)}, f32[512,128]{1,0:T(8,128)S(1)}, /*index=5*/f32[8,128]{1,0:T(8,128)S(1)}) custom-call(f32[8,40,128]{2,1,0:T(8,128)S(1)} %all_to_all.5.gat, f32[3,63,8,128]{3,2,1,0:T(8,128)S(1)} %get-tuple-element.40.fac, ...), custom_call_target="tpu_custom_call" | custom-call | tf_op jit(solution)/shard_map/second/pallas_call | solution.py:492
  13.9 2.2 %collective-permute-start = (f32[232,128]{1,0:T(8,128)S(1)}, f32[232,128]{1,0:T(8,128)S(1)}, u32[]{:S(2)}, u32[]{:S(2)}) collective-permute-start(f32[232,128]{1,0:T(8,128)S(1)} %get-tuple-element.45), channel_id=1, source_target_pairs={{0,8},{8,0},{16,24},{24,16},{32,40},{40,32},{48,56},{56,48},{64,72... | collective-permute-start | bytes 356360 | tf_op jit(solution)/shard_map/ppermute | solution.py:504
  16.1 1.0 %collective-permute-done.theirs = f32[232,128]{1,0:T(8,128)S(1)} collective-permute-done((f32[232,128]{1,0:T(8,128)S(1)}, f32[232,128]{1,0:T(8,128)S(1)}, u32[]{:S(2)}, u32[]{:S(2)}) %collective-permute-start) | collective-permute-done | bytes 118816 | tf_op jit(solution)/shard_map/ppermute | solution.py:504
  17.1 2.0 %collective-permute-start.1 = (f32[232,128]{1,0:T(8,128)S(1)}, f32[232,128]{1,0:T(8,128)S(1)}, u32[]{:S(2)}, u32[]{:S(2)}) collective-permute-start(f32[232,128]{1,0:T(8,128)S(1)} %get-tuple-element.46.own), channel_id=1, source_target_pairs={{0,24},{8,16},{16,8},{24,0},{32,56},{40,48},{48,40},{56,32},{64,88... | collective-permute-start | bytes 356360 | tf_op jit(solution)/shard_map/ppermute | solution.py:504
  19.1 2.3 %collective-permute-start.2 = (f32[232,128]{1,0:T(8,128)S(1)}, f32[232,128]{1,0:T(8,128)S(1)}, u32[]{:S(2)}, u32[]{:S(2)}) collective-permute-start(f32[232,128]{1,0:T(8,128)S(1)} %get-tuple-element.46.own), channel_id=1, source_target_pairs={{0,56},{8,48},{16,40},{24,32},{32,24},{40,16},{48,8},{56,0},{64,12... | collective-permute-start | bytes 356360 | tf_op jit(solution)/shard_map/ppermute | solution.py:504
  21.3 1.0 %collective-permute-start.3 = (f32[232,128]{1,0:T(8,128)S(1)}, f32[232,128]{1,0:T(8,128)S(1)}, u32[]{:S(2)}, u32[]{:S(2)}) collective-permute-start(f32[232,128]{1,0:T(8,128)S(1)} %get-tuple-element.46.own), channel_id=1, source_target_pairs={{0,32},{8,40},{16,48},{24,56},{32,0},{40,8},{48,16},{56,24},{64,96... | collective-permute-start | bytes 356360 | tf_op jit(solution)/shard_map/ppermute | solution.py:504
  22.4 0.0 collective-permute-done.1.near
  22.4 3.9 %collective-permute-done.2.far = f32[232,128]{1,0:T(8,128)S(1)} collective-permute-done((f32[232,128]{1,0:T(8,128)S(1)}, f32[232,128]{1,0:T(8,128)S(1)}, u32[]{:S(2)}, u32[]{:S(2)}) %collective-permute-start.2) | collective-permute-done | bytes 118816 | tf_op jit(solution)/shard_map/ppermute | solution.py:504
  26.3 2.1 %collective-permute-done.3.mid = f32[232,128]{1,0:T(8,128)S(1)} collective-permute-done((f32[232,128]{1,0:T(8,128)S(1)}, f32[232,128]{1,0:T(8,128)S(1)}, u32[]{:S(2)}, u32[]{:S(2)}) %collective-permute-start.3) | collective-permute-done | bytes 118816 | tf_op jit(solution)/shard_map/ppermute | solution.py:504
  28.4 0.1 merge_ring.1
  28.5 3.3 %collective-permute-start.4 = (f32[104,128]{1,0:T(8,128)S(1)}, f32[104,128]{1,0:T(8,128)S(1)}, u32[]{:S(2)}, u32[]{:S(2)}) collective-permute-start(f32[104,128]{1,0:T(8,128)S(1)} %get-tuple-element.48.near), channel_id=1, source_target_pairs={{0,72},{8,64},{16,88},{24,80},{32,104},{40,96},{48,120},{56,112},{... | collective-permute-start | bytes 159752 | tf_op jit(solution)/shard_map/ppermute | solution.py:504
  31.8 0.2 coef.1
  32.1 2.4 %collective-permute-done.4.theirs = f32[104,128]{1,0:T(8,128)S(1)} collective-permute-done((f32[104,128]{1,0:T(8,128)S(1)}, f32[104,128]{1,0:T(8,128)S(1)}, u32[]{:S(2)}, u32[]{:S(2)}) %collective-permute-start.4) | collective-permute-done | bytes 53280 | tf_op jit(solution)/shard_map/ppermute | solution.py:504
  34.5 0.1 top.1
  34.5 0.5 %collective-permute-start.5 = (f32[64,128]{1,0:T(8,128)S(1)}, f32[64,128]{1,0:T(8,128)S(1)}, u32[]{:S(2)}, u32[]{:S(2)}) collective-permute-start(f32[64,128]{1,0:T(8,128)S(1)} %get-tuple-element.66), channel_id=1, source_target_pairs={{0,8},{8,0},{16,24},{24,16},{32,40},{40,32},{48,56},{56,48},{64,72... | collective-permute-start | bytes 98312 | tf_op jit(solution)/shard_map/ppermute | solution.py:504
  35.0 0.9 %collective-permute-done.5.got = f32[64,128]{1,0:T(8,128)S(1)} collective-permute-done((f32[64,128]{1,0:T(8,128)S(1)}, f32[64,128]{1,0:T(8,128)S(1)}, u32[]{:S(2)}, u32[]{:S(2)}) %collective-permute-start.5) | collective-permute-done | bytes 32800 | tf_op jit(solution)/shard_map/ppermute | solution.py:504
  35.9 1.5 %last.1 = (f32[512,128]{1,0:T(8,128)}, f32[512,128]{1,0:T(8,128)}) custom-call(f32[72,128]{1,0:T(8,128)S(1)} %get-tuple-element.65.own, f32[64,128]{1,0:T(8,128)S(1)} %collective-permute-done.5.got, f32[8,24,8,128]{3,2,1,0:T(8,128)S(1)} %get-tuple-element.67.xfac, f32[24,1,128]{2,1,0:T(1,128)S(1)} %get-tuple-element.68.xhfac, ...), custom_call_target="tpu_custom_call" | custom-call | tf_op jit(solution)/shard_map/last/pallas_call | solution.py:492
  (1 shorter events, 0.0 us)
Async XLA Ops:
  13.9 3.1 %collective-permute-start = (f32[232,128]{1,0:T(8,128)S(1)}, f32[232,128]{1,0:T(8,128)S(1)}, u32[]{:S(2)}, u32[]{:S(2)}) collective-permute-start(f32[232,128]{1,0:T(8,128)S(1)} %get-tuple-element.45), channel_id=1, source_target_pairs={{0,8},{8,0},{16,24},{24,16},{32,40},{40,32},{48,56},{56,48},{64,72... | collective-permute-start | bytes 356360 | tf_op jit(solution)/shard_map/ppermute | solution.py:504
  17.1 5.3 %collective-permute-start.1 = (f32[232,128]{1,0:T(8,128)S(1)}, f32[232,128]{1,0:T(8,128)S(1)}, u32[]{:S(2)}, u32[]{:S(2)}) collective-permute-start(f32[232,128]{1,0:T(8,128)S(1)} %get-tuple-element.46.own), channel_id=1, source_target_pairs={{0,24},{8,16},{16,8},{24,0},{32,56},{40,48},{48,40},{56,32},{64,88... | collective-permute-start | bytes 356360 | tf_op jit(solution)/shard_map/ppermute | solution.py:504
  19.1 7.2 %collective-permute-start.2 = (f32[232,128]{1,0:T(8,128)S(1)}, f32[232,128]{1,0:T(8,128)S(1)}, u32[]{:S(2)}, u32[]{:S(2)}) collective-permute-start(f32[232,128]{1,0:T(8,128)S(1)} %get-tuple-element.46.own), channel_id=1, source_target_pairs={{0,56},{8,48},{16,40},{24,32},{32,24},{40,16},{48,8},{56,0},{64,12... | collective-permute-start | bytes 356360 | tf_op jit(solution)/shard_map/ppermute | solution.py:504
  21.3 7.0 %collective-permute-start.3 = (f32[232,128]{1,0:T(8,128)S(1)}, f32[232,128]{1,0:T(8,128)S(1)}, u32[]{:S(2)}, u32[]{:S(2)}) collective-permute-start(f32[232,128]{1,0:T(8,128)S(1)} %get-tuple-element.46.own), channel_id=1, source_target_pairs={{0,32},{8,40},{16,48},{24,56},{32,0},{40,8},{48,16},{56,24},{64,96... | collective-permute-start | bytes 356360 | tf_op jit(solution)/shard_map/ppermute | solution.py:504
  28.5 6.0 %collective-permute-start.4 = (f32[104,128]{1,0:T(8,128)S(1)}, f32[104,128]{1,0:T(8,128)S(1)}, u32[]{:S(2)}, u32[]{:S(2)}) collective-permute-start(f32[104,128]{1,0:T(8,128)S(1)} %get-tuple-element.48.near), channel_id=1, source_target_pairs={{0,72},{8,64},{16,88},{24,80},{32,104},{40,96},{48,120},{56,112},{... | collective-permute-start | bytes 159752 | tf_op jit(solution)/shard_map/ppermute | solution.py:504
  34.5 1.4 %collective-permute-start.5 = (f32[64,128]{1,0:T(8,128)S(1)}, f32[64,128]{1,0:T(8,128)S(1)}, u32[]{:S(2)}, u32[]{:S(2)}) collective-permute-start(f32[64,128]{1,0:T(8,128)S(1)} %get-tuple-element.66), channel_id=1, source_target_pairs={{0,8},{8,0},{16,24},{24,16},{32,40},{40,32},{48,56},{56,48},{64,72... | collective-permute-start | bytes 98312 | tf_op jit(solution)/shard_map/ppermute | solution.py:504

commit v8 on v6

--- a/solution.py
+++ b/solution.py
@@ -425,7 +425,7 @@
     put_planes(coef_out, coefs)
 
 
-def ring_matrix_kernel(own, near, far, mid, merged_out, mine_out, other_out, ring_out):
+def ring_matrix_kernel(own, mid, far, near, merged_out, mine_out, other_out, ring_out):
     _, right, upper = spots()
     packs = [planes_of(r, 5) for r in (own, near, mid, far)]
     mine, mine_c = port_coefs(*order(right, packs[0], packs[1]))
@@ -454,7 +454,7 @@
     write_pack(saved_out, saved, edge_saved)
 
 
-def ring_kernel(own, near, far, mid, matrix, mine_c, other_c, ring_c, merged_out, pair_out, saved_out, top_out):
+def ring_kernel(own, mid, far, near, matrix, mine_c, other_c, ring_c, merged_out, pair_out, saved_out, top_out):
     _, right, upper = spots()
     last = lax.div(lax.axis_index("gx"), 8) == 1
     main, edge = zip(*[read_sides(r) for r in (own, near, mid, far)])
@@ -622,7 +622,7 @@
     mm, core_c = call(core_matrix_kernel, [(160, 128), (224, 128)], [], "matrix_core", keep_m, other_m)
     mm, ypack = lax.optimization_barrier((mm, ypack))
     gat = lax.all_to_all(ypack, "gy", split_axis=0, concat_axis=0, tiled=True)
-    ring_m = [swap(mm, bit) for bit in (3, 7, 4)]
+    ring_m = [swap(mm, bit) for bit in (4, 7, 3)]
     keep, send, xfac, xhfac, a2, kh = call(
         second_kernel,
         [(72, 128), (72, 128), (8, 24, 8, 128), (24, 1, 128), (512, 128), (8, 128)],
@@ -631,7 +631,7 @@
         gat, fac, ties, cond, sub,
     )
     m1, sv1 = call(core_kernel, [(72, 128), (200, 128)], [], "merge_core", keep, swap(send, 1), core_c)
-    ring_v = [swap(m1, bit) for bit in (3, 7, 4)]
+    ring_v = [swap(m1, bit) for bit in (4, 7, 3)]
     matrix, mine_c, other_c, ring_c = call(
         ring_matrix_kernel, [(160, 128)] + [(224, 128)] * 3, [], "matrix_ring", mm, *ring_m
     )

time: 36.8 us -> 35.7 us (0.970)
  starting transfers between devices: 23.2 us -> 21.2 us
  waiting for transfers between devices: 7.68 us -> 8.61 us
    ppermute x10, starting transfers between devices: 18.1 us -> 16.1 us  [swap(): return lax.ppermute(v, 'gx', [(i, i ^ bit) for i in range(16)])]
    all_to_all x1, waiting for transfers between devices: 0.37 us -> 0.88 us  [body(): gat = lax.all_to_all(ypack, 'gy', split_axis=0, concat_axis=0, tiled=True)]
    ppermute x10, waiting for transfers between devices: 7.32 us -> 7.72 us  [swap(): return lax.ppermute(v, 'gx', [(i, i ^ bit) for i in range(16)])]
  transfers between devices with their start and end apart: 11 -> 11, of which waited for: 6 -> 5; matrix products, arithmetic and copies ran while one was open for 0% -> 0% of each run, Pallas kernels for 6% -> 6%
where the time goes in v8:
time: 35.7 us; the launch traced here: 35.5 us
  starting transfers between devices  21.2 us (59%)
  waiting for transfers between devices  8.61 us (24%)
  Pallas kernels  4.96 us (14%)
  between operations  0.69 us (2%)
    ppermute x10, starting transfers between devices, swap(): return lax.ppermute(v, 'gx', [(i, i ^ bit) for i in range(16)])  16.1 us
    ppermute x10, waiting for transfers between devices, swap(): return lax.ppermute(v, 'gx', [(i, i ^ bit) for i in range(16)])  7.72 us
    all_to_all x1, starting transfers between devices, body(): gat = lax.all_to_all(ypack, 'gy', split_axis=0, concat_axis=0, tiled=True)  5.16 us
    pallas_call x10, Pallas kernels, call(): pl.pallas_call(kernel, out_shape=shapes, in_specs=[HBM if i < far_in else...  4.96 us
    all_to_all x1, waiting for transfers between devices, body(): gat = lax.all_to_all(ypack, 'gy', split_axis=0, concat_axis=0, tiled=True)  0.88 us
  transfers between devices with their start and end apart: 11, of which 5 were waited for; matrix products, arithmetic and copies ran while one was open for 0% of the time, Pallas kernels for 6%

profile of v8, /device:TPU:1, one launch (start us, length us, event | category | flops | bytes accessed | tf_op | source)
XLA Modules:
  0.0 35.5 jit_solution(14708038348133764837)
XLA Ops:
  0.6 1.2 %fields.1 = (f32[512,128]{1,0:T(8,128)S(1)}, f32[160,128]{1,0:T(8,128)S(1)}, f32[160,128]{1,0:T(8,128)S(1)}, f32[512,128]{1,0:T(8,128)S(1)}, s32[8,128]{1,0:T(8,...) custom-call(f32[512,128]{1,0:T(8,128)} %bitcast.4, f32[512,128]{1,0:T(8,128)} %bitcast.5, s32[8,128]{1,0:T(8,128)} %sub_in.1, ...), custom_call_target="tpu_custom_call" | custom-call | tf_op jit(solution)/shard_map/fields/pallas_call | solution.py:587
  1.9 1.5 %collective-permute-start = (f32[160,128]{1,0:T(8,128)S(1)}, f32[160,128]{1,0:T(8,128)S(1)}, u32[]{:S(2)}, u32[]{:S(2)}) collective-permute-start(f32[160,128]{1,0:T(8,128)S(1)} %get-tuple-element.50), channel_id=1, source_target_pairs={{0,8},{8,0},{16,24},{24,16},{32,40},{40,32},{48,56},{56,48},{64,72... | collective-permute-start | bytes 245768 | tf_op jit(solution)/shard_map/ppermute | solution.py:599
  3.3 1.3 %first.1 = (f32[8,40,128]{2,1,0:T(8,128)}, f32[3,63,8,128]{3,2,1,0:T(8,128)S(1)}, f32[12,8,128]{2,1,0:T(8,128)S(1)}) custom-call(f32[512,128]{1,0:T(8,128)S(1)} %get-tuple-element.52.cot, s32[8,128]{1,0:T(8,128)S(1)} %get-tuple-element.53.sub, s32[8,128]{1,0:T(8,128)S(1)} %get-tuple-element.54.dep, s32[8,128]{1,0:T(8,128)S(1)} %get-tuple-element.55.cls, ...), custom_call_target="tpu_custom_call" | custom-call | tf_op jit(solution)/shard_map/first/pallas_call | solution.py:587
  4.6 0.0 collective-permute-done.theirs
  4.7 5.2 %all-to-all-start = ((f32[8,40,128]{2,1,0:T(8,128)}), f32[8,40,128]{2,1,0:T(8,128)S(1)}, u32[]{:S(2)}, u32[]{:S(2)}) async-start(f32[8,40,128]{2,1,0:T(8,128)} %get-tuple-element.58), calls=%async_computation | async-start | bytes 327680 | tf_op jit(solution)/shard_map/all_to_all | solution.py:624
  9.8 3.6 %collective-permute-start.5 = (f32[160,128]{1,0:T(8,128)S(1)}, f32[160,128]{1,0:T(8,128)S(1)}, u32[]{:S(2)}, u32[]{:S(2)}) collective-permute-start(f32[160,128]{1,0:T(8,128)S(1)} %get-tuple-element.65.own), channel_id=1, source_target_pairs={{0,32},{8,40},{16,48},{24,56},{32,0},{40,8},{48,16},{56,24},{64,96... | collective-permute-start | bytes 245768 | tf_op jit(solution)/shard_map/ppermute | solution.py:599
  13.4 0.9 %collective-permute-start.6 = (f32[160,128]{1,0:T(8,128)S(1)}, f32[160,128]{1,0:T(8,128)S(1)}, u32[]{:S(2)}, u32[]{:S(2)}) collective-permute-start(f32[160,128]{1,0:T(8,128)S(1)} %get-tuple-element.65.own), channel_id=1, source_target_pairs={{0,56},{8,48},{16,40},{24,32},{32,24},{40,16},{48,8},{56,0},{64,12... | collective-permute-start | bytes 245768 | tf_op jit(solution)/shard_map/ppermute | solution.py:599
  14.3 0.3 collective-permute-start.7
  14.6 0.9 %all-to-all-done.gat = f32[8,40,128]{2,1,0:T(8,128)S(1)} async-done(((f32[8,40,128]{2,1,0:T(8,128)}), f32[8,40,128]{2,1,0:T(8,128)S(1)}, u32[]{:S(2)}, u32[]{:S(2)}) %all-to-all-start) | async-done | bytes 163872 | tf_op jit(solution)/shard_map/all_to_all | solution.py:624
  15.5 0.4 %second.1 = (f32[72,128]{1,0:T(8,128)S(1)}, f32[72,128]{1,0:T(8,128)S(1)}, f32[8,24,8,128]{3,2,1,0:T(8,128)S(1)}, f32[24,1,128]{2,1,0:T(1,128)S(1)}, f32[512,128]{1,0:T(8,128)S(1)}, /*index=5*/f32[8,128]{1,0:T(8,128)S(1)}) custom-call(f32[8,40,128]{2,1,0:T(8,128)S(1)} %all-to-all-done.gat, f32[3,63,8,128]{3,2,1,0:T(8,128)S(1)} %get-tuple-element.59.fac, ...), custom_call_target="tpu_custom_call" | custom-call | tf_op jit(solution)/shard_map/second/pallas_call | solution.py:587
  16.0 1.4 %collective-permute-start.1 = (f32[72,128]{1,0:T(8,128)S(1)}, f32[72,128]{1,0:T(8,128)S(1)}, u32[]{:S(2)}, u32[]{:S(2)}) collective-permute-start(f32[72,128]{1,0:T(8,128)S(1)} %get-tuple-element.62), channel_id=1, source_target_pairs={{0,8},{8,0},{16,24},{24,16},{32,40},{40,32},{48,56},{56,48},{64,72... | collective-permute-start | bytes 110600 | tf_op jit(solution)/shard_map/ppermute | solution.py:599
  17.4 0.9 %collective-permute-done.1.theirs = f32[72,128]{1,0:T(8,128)S(1)} collective-permute-done((f32[72,128]{1,0:T(8,128)S(1)}, f32[72,128]{1,0:T(8,128)S(1)}, u32[]{:S(2)}, u32[]{:S(2)}) %collective-permute-start.1) | collective-permute-done | bytes 36896 | tf_op jit(solution)/shard_map/ppermute | solution.py:599
  18.3 3.7 %collective-permute-start.2 = (f32[72,128]{1,0:T(8,128)S(1)}, f32[72,128]{1,0:T(8,128)S(1)}, u32[]{:S(2)}, u32[]{:S(2)}) collective-permute-start(f32[72,128]{1,0:T(8,128)S(1)} %get-tuple-element.64.own), channel_id=1, source_target_pairs={{0,32},{8,40},{16,48},{24,56},{32,0},{40,8},{48,16},{56,24},{64,96... | collective-permute-start | bytes 110600 | tf_op jit(solution)/shard_map/ppermute | solution.py:599
  22.0 0.9 %collective-permute-start.3 = (f32[72,128]{1,0:T(8,128)S(1)}, f32[72,128]{1,0:T(8,128)S(1)}, u32[]{:S(2)}, u32[]{:S(2)}) collective-permute-start(f32[72,128]{1,0:T(8,128)S(1)} %get-tuple-element.64.own), channel_id=1, source_target_pairs={{0,56},{8,48},{16,40},{24,32},{32,24},{40,16},{48,8},{56,0},{64,12... | collective-permute-start | bytes 110600 | tf_op jit(solution)/shard_map/ppermute | solution.py:599
  22.9 0.0 collective-permute-done.5.mid
  22.9 0.3 collective-permute-start.4
  23.3 0.0 collective-permute-done.6.far
  23.3 0.0 collective-permute-done.7.near
  23.3 0.1 matrix_ring.1
  23.3 0.0 collective-permute-done.2.mid
  23.4 3.8 %collective-permute-done.3.far = f32[72,128]{1,0:T(8,128)S(1)} collective-permute-done((f32[72,128]{1,0:T(8,128)S(1)}, f32[72,128]{1,0:T(8,128)S(1)}, u32[]{:S(2)}, u32[]{:S(2)}) %collective-permute-start.3) | collective-permute-done | bytes 36896 | tf_op jit(solution)/shard_map/ppermute | solution.py:599
  27.2 0.0 collective-permute-done.4.near
  27.2 0.1 merge_ring.1
  27.2 3.0 %collective-permute-start.8 = (f32[104,128]{1,0:T(8,128)S(1)}, f32[104,128]{1,0:T(8,128)S(1)}, u32[]{:S(2)}, u32[]{:S(2)}) collective-permute-start(f32[104,128]{1,0:T(8,128)S(1)} %get-tuple-element.71.near), channel_id=1, source_target_pairs={{0,72},{8,64},{16,88},{24,80},{32,104},{40,96},{48,120},{56,112},{... | collective-permute-start | bytes 159752 | tf_op jit(solution)/shard_map/ppermute | solution.py:599
  30.2 0.2 coef.1
  30.5 2.2 %collective-permute-done.8.theirs = f32[104,128]{1,0:T(8,128)S(1)} collective-permute-done((f32[104,128]{1,0:T(8,128)S(1)}, f32[104,128]{1,0:T(8,128)S(1)}, u32[]{:S(2)}, u32[]{:S(2)}) %collective-permute-start.8) | collective-permute-done | bytes 53280 | tf_op jit(solution)/shard_map/ppermute | solution.py:599
  32.7 0.1 top.1
  32.7 0.5 %collective-permute-start.9 = (f32[64,128]{1,0:T(8,128)S(1)}, f32[64,128]{1,0:T(8,128)S(1)}, u32[]{:S(2)}, u32[]{:S(2)}) collective-permute-start(f32[64,128]{1,0:T(8,128)S(1)} %get-tuple-element.86), channel_id=1, source_target_pairs={{0,8},{8,0},{16,24},{24,16},{32,40},{40,32},{48,56},{56,48},{64,72... | collective-permute-start | bytes 98312 | tf_op jit(solution)/shard_map/ppermute | solution.py:599
  33.2 0.9 %collective-permute-done.9.got = f32[64,128]{1,0:T(8,128)S(1)} collective-permute-done((f32[64,128]{1,0:T(8,128)S(1)}, f32[64,128]{1,0:T(8,128)S(1)}, u32[]{:S(2)}, u32[]{:S(2)}) %collective-permute-start.9) | collective-permute-done | bytes 32800 | tf_op jit(solution)/shard_map/ppermute | solution.py:599
  34.0 1.5 %last.1 = (f32[512,128]{1,0:T(8,128)}, f32[512,128]{1,0:T(8,128)}) custom-call(f32[72,128]{1,0:T(8,128)S(1)} %get-tuple-element.85.own, f32[64,128]{1,0:T(8,128)S(1)} %collective-permute-done.9.got, f32[8,24,8,128]{3,2,1,0:T(8,128)S(1)} %get-tuple-element.87.xfac, f32[24,1,128]{2,1,0:T(1,128)S(1)} %get-tuple-element.88.xhfac, ...), custom_call_target="tpu_custom_call" | custom-call | tf_op jit(solution)/shard_map/last/pallas_call | solution.py:587
  (2 shorter events, 0.1 us)
Async XLA Ops:
  1.9 2.8 %collective-permute-start = (f32[160,128]{1,0:T(8,128)S(1)}, f32[160,128]{1,0:T(8,128)S(1)}, u32[]{:S(2)}, u32[]{:S(2)}) collective-permute-start(f32[160,128]{1,0:T(8,128)S(1)} %get-tuple-element.50), channel_id=1, source_target_pairs={{0,8},{8,0},{16,24},{24,16},{32,40},{40,32},{48,56},{56,48},{64,72... | collective-permute-start | bytes 245768 | tf_op jit(solution)/shard_map/ppermute | solution.py:599
  4.7 10.8 %all-to-all-start = ((f32[8,40,128]{2,1,0:T(8,128)}), f32[8,40,128]{2,1,0:T(8,128)S(1)}, u32[]{:S(2)}, u32[]{:S(2)}) async-start(f32[8,40,128]{2,1,0:T(8,128)} %get-tuple-element.58), calls=%async_computation | async-start | bytes 327680 | tf_op jit(solution)/shard_map/all_to_all | solution.py:624
  9.8 13.1 %collective-permute-start.5 = (f32[160,128]{1,0:T(8,128)S(1)}, f32[160,128]{1,0:T(8,128)S(1)}, u32[]{:S(2)}, u32[]{:S(2)}) collective-permute-start(f32[160,128]{1,0:T(8,128)S(1)} %get-tuple-element.65.own), channel_id=1, source_target_pairs={{0,32},{8,40},{16,48},{24,56},{32,0},{40,8},{48,16},{56,24},{64,96... | collective-permute-start | bytes 245768 | tf_op jit(solution)/shard_map/ppermute | solution.py:599
  13.4 9.8 %collective-permute-start.6 = (f32[160,128]{1,0:T(8,128)S(1)}, f32[160,128]{1,0:T(8,128)S(1)}, u32[]{:S(2)}, u32[]{:S(2)}) collective-permute-start(f32[160,128]{1,0:T(8,128)S(1)} %get-tuple-element.65.own), channel_id=1, source_target_pairs={{0,56},{8,48},{16,40},{24,32},{32,24},{40,16},{48,8},{56,0},{64,12... | collective-permute-start | bytes 245768 | tf_op jit(solution)/shard_map/ppermute | solution.py:599
  14.3 8.9 %collective-permute-start.7 = (f32[160,128]{1,0:T(8,128)S(1)}, f32[160,128]{1,0:T(8,128)S(1)}, u32[]{:S(2)}, u32[]{:S(2)}) collective-permute-start(f32[160,128]{1,0:T(8,128)S(1)} %get-tuple-element.65.own), channel_id=1, source_target_pairs={{0,24},{8,16},{16,8},{24,0},{32,56},{40,48},{48,40},{56,32},{64,88... | collective-permute-start | bytes 245768 | tf_op jit(solution)/shard_map/ppermute | solution.py:599
  16.0 2.3 %collective-permute-start.1 = (f32[72,128]{1,0:T(8,128)S(1)}, f32[72,128]{1,0:T(8,128)S(1)}, u32[]{:S(2)}, u32[]{:S(2)}) collective-permute-start(f32[72,128]{1,0:T(8,128)S(1)} %get-tuple-element.62), channel_id=1, source_target_pairs={{0,8},{8,0},{16,24},{24,16},{32,40},{40,32},{48,56},{56,48},{64,72... | collective-permute-start | bytes 110600 | tf_op jit(solution)/shard_map/ppermute | solution.py:599
  18.3 5.0 %collective-permute-start.2 = (f32[72,128]{1,0:T(8,128)S(1)}, f32[72,128]{1,0:T(8,128)S(1)}, u32[]{:S(2)}, u32[]{:S(2)}) collective-permute-start(f32[72,128]{1,0:T(8,128)S(1)} %get-tuple-element.64.own), channel_id=1, source_target_pairs={{0,32},{8,40},{16,48},{24,56},{32,0},{40,8},{48,16},{56,24},{64,96... | collective-permute-start | bytes 110600 | tf_op jit(solution)/shard_map/ppermute | solution.py:599
  22.0 5.2 %collective-permute-start.3 = (f32[72,128]{1,0:T(8,128)S(1)}, f32[72,128]{1,0:T(8,128)S(1)}, u32[]{:S(2)}, u32[]{:S(2)}) collective-permute-start(f32[72,128]{1,0:T(8,128)S(1)} %get-tuple-element.64.own), channel_id=1, source_target_pairs={{0,56},{8,48},{16,40},{24,32},{32,24},{40,16},{48,8},{56,0},{64,12... | collective-permute-start | bytes 110600 | tf_op jit(solution)/shard_map/ppermute | solution.py:599
  22.9 4.2 %collective-permute-start.4 = (f32[72,128]{1,0:T(8,128)S(1)}, f32[72,128]{1,0:T(8,128)S(1)}, u32[]{:S(2)}, u32[]{:S(2)}) collective-permute-start(f32[72,128]{1,0:T(8,128)S(1)} %get-tuple-element.64.own), channel_id=1, source_target_pairs={{0,24},{8,16},{16,8},{24,0},{32,56},{40,48},{48,40},{56,32},{64,88... | collective-permute-start | bytes 110600 | tf_op jit(solution)/shard_map/ppermute | solution.py:599
  27.2 5.4 %collective-permute-start.8 = (f32[104,128]{1,0:T(8,128)S(1)}, f32[104,128]{1,0:T(8,128)S(1)}, u32[]{:S(2)}, u32[]{:S(2)}) collective-permute-start(f32[104,128]{1,0:T(8,128)S(1)} %get-tuple-element.71.near), channel_id=1, source_target_pairs={{0,72},{8,64},{16,88},{24,80},{32,104},{40,96},{48,120},{56,112},{... | collective-permute-start | bytes 159752 | tf_op jit(solution)/shard_map/ppermute | solution.py:599
  32.7 1.3 %collective-permute-start.9 = (f32[64,128]{1,0:T(8,128)S(1)}, f32[64,128]{1,0:T(8,128)S(1)}, u32[]{:S(2)}, u32[]{:S(2)}) collective-permute-start(f32[64,128]{1,0:T(8,128)S(1)} %get-tuple-element.86), channel_id=1, source_target_pairs={{0,8},{8,0},{16,24},{24,16},{32,40},{40,32},{48,56},{56,48},{64,72... | collective-permute-start | bytes 98312 | tf_op jit(solution)/shard_map/ppermute | solution.py:599

commit v9 on v8

--- a/solution.py
+++ b/solution.py
@@ -187,14 +187,18 @@
 
 
 def fields_kernel(cot_in, temp_in, sub_in, dep_in, cls_in, cond, keep, send, cot, sub, dep, cls, temp, planes, sems):
-    pairs = ((sub_in, sub), (dep_in, dep), (temp_in, temp), (cls_in, cls), (cot_in, cot))
+    pieces = [slice(128 * i, 128 * i + 128) for i in range(4)]
+    pairs = [(sub_in, sub), (dep_in, dep)] + [(temp_in.at[r], temp.at[r]) for r in pieces]
+    pairs += [(cls_in, cls), (cot_in, cot)]
     copies = [pltpu.make_async_copy(a, b, sems.at[i]) for i, (a, b) in enumerate(pairs)]
     for cp in copies:
         cp.start()
-    for cp in copies[:3]:
+    for cp in copies[:2]:
         cp.wait()
     sub_v, dep_v = sub[...], dep[...]
     for z in range(64):
+        if z % 16 == 0:
+            copies[2 + z // 16].wait()
         base = jnp.where(z < sub_v, 1.0, 0.45)
         sg = 0.5 + jax.nn.sigmoid(temp[8 * z : 8 * z + 8])
         cond[8 * z : 8 * z + 8] = jnp.where(z < dep_v, base * sg, 0.0)
@@ -210,7 +214,7 @@
         for i, v in enumerate((k[0], k[7]) + chain_matrix(c, s)):
             planes[i, 8 * chunk : 8 * chunk + 8] = v
     split_halves(planes, keep, send)
-    for cp in copies[3:]:
+    for cp in copies[6:]:
         cp.wait()
 
 
@@ -251,7 +255,6 @@
         ky.append(mid[0, 8 * y : 8 * y + 8])
         dy.append(mid[1, 8 * y : 8 * y + 8])
         sy.append(jnp.where(z_lane < mid[2, 8 * y : 8 * y + 8], 1.0, 0.6))
-    cap_first, cap_last = sy[0][0:4], sy[63][4:8]
     low = jnp.where(me_y == 0, R * SIDE, 0.0)
     high = jnp.where(me_y == 7, R * SIDE, 0.0)
     sy[0] = sy[0] + jnp.where(row < 4, low, 0.0)
@@ -267,14 +270,16 @@
     merged, saved = merge_ports(side_a, side_b)
     for i, v in enumerate(saved):
         tie_out[NLEV + i, 0:4] = v
-    pack = jnp.concatenate(list(merged) + [cap_first, cap_last, jnp.zeros((4, 128), F32)], axis=0)
+    lower = lax.broadcasted_iota(jnp.int32, (4, 128), 1) < 64
+    edges = jnp.where(lower, mid[2, 0:4], mid[2, 508:512])
+    pack = jnp.concatenate(list(merged) + [edges], axis=0)
     for n in range(8):
         ypack[n] = pack
 
 
 def second_kernel(gat, fac, ties, cond, sub, keep, send, xfac, xhfac, a2_out, kh_out, pick, flat, planes, xp):
     me_y = lax.axis_index("gy")
-    seg = [[gat[n, 4 * i : 4 * i + 4] for i in range(9)] for n in range(8)]
+    seg = [[gat[n, 4 * i : 4 * i + 4] for i in range(8)] for n in range(8)]
     gam, rhs = seg[0][4], seg[0][6]
     down, links = [None], [None]
     for n in range(1, 8):
@@ -301,13 +306,13 @@
     for n in range(8):
         rows = [fl[n], u[n]]
         if n:
-            rows += [seg[n - 1][8] * u[n - 1], seg[n - 1][1], seg[n - 1][8]]
+            rows += [u[n - 1], seg[n - 1][1], seg[n - 1][7]]
         else:
-            rows += [zero4, zero4, zero4 + 1.0]
+            rows += [zero4, zero4, zero4]
         if n < 7:
-            rows += [seg[n + 1][7] * uf[n + 1], seg[n + 1][0], seg[n + 1][7]]
+            rows += [uf[n + 1], seg[n + 1][0], seg[n + 1][7]]
         else:
-            rows += [zero4, zero4, zero4 + 1.0]
+            rows += [zero4, zero4, zero4]
         for i, v in enumerate(rows):
             pick[n, 4 * i : 4 * i + 4] = v
     mine = [pick[me_y, 4 * i : 4 * i + 4] for i in range(8)]
@@ -326,14 +331,18 @@
             jnp.concatenate([flat[pl.ds(q, 64, stride=8), :], flat[pl.ds(4 + q, 64, stride=8), :]], axis=0)
         )
 
-    even = (lax.broadcasted_iota(jnp.int32, (4, 128), 1) & 1) == 0
+    lane = lax.broadcasted_iota(jnp.int32, (4, 128), 1)
+    even = (lane & 1) == 0
+    z_of = (lane >> 1).astype(F32)
+    cap_l = jnp.where(z_of < jnp.where(lane < 64, pltpu.roll(mine[4], 64, 1), mine[4]), 1.0, 0.6)
+    cap_r = jnp.where(z_of < jnp.where(lane < 64, mine[7], pltpu.roll(mine[7], 64, 1)), 1.0, 0.6)
 
     def both(left, right):
         low = jnp.where(even, left, pltpu.roll(right, 127, 1))
         high = jnp.where(even, pltpu.roll(left, 127, 1), pltpu.roll(right, 126, 1))
         return [low[x : x + 1] for x in range(4)] + [high[x : x + 1] for x in range(4)]
 
-    dh, kh, caph = both(mine[2], mine[5]), both(mine[3], mine[6]), both(mine[4], mine[7])
+    dh, kh, caph = both(cap_l * mine[2], cap_r * mine[5]), both(mine[3], mine[6]), both(cap_l, cap_r)
     for x in range(8):
         kh_out[x : x + 1] = kh[x]
 
@@ -425,7 +434,7 @@
     put_planes(coef_out, coefs)
 
 
-def ring_matrix_kernel(own, mid, far, near, merged_out, mine_out, other_out, ring_out):
+def ring_matrix_kernel(own, mid, far, near, merged_out, mine_out, other_out, ring_out, top_out):
     _, right, upper = spots()
     packs = [planes_of(r, 5) for r in (own, near, mid, far)]
     mine, mine_c = port_coefs(*order(right, packs[0], packs[1]))
@@ -435,6 +444,9 @@
     put_planes(mine_out, mine_c)
     put_planes(other_out, other_c)
     put_planes(ring_out, ring_c)
+    last = lax.div(lax.axis_index("gx"), 8) == 1
+    kf, kl, z, tt, g = merged
+    put_planes(top_out, (jnp.where(last, z + tt * (tt * recip(g)), g), jnp.where(last, kf, kl)))
 
 
 def read_sides(ref):
@@ -465,21 +477,27 @@
     e_other, _ = merge_ports(*order(right, edge[2], edge[3]))
     e_merged, e_saved = merge_ports(*order(upper, e_mine, e_other))
     outs = [planes_of(matrix, 5) + values, e_merged]
-    tops = []
-    for kf, kl, z, tt, g, p, q in outs:
-        tg = tt * recip(g)
-        tops.append((jnp.where(last, z + tt * tg, g), jnp.where(last, p + tg * q, q), jnp.where(last, kf, kl)))
     write_pack(merged_out, *outs)
+    kf, kl, z, tt, g, p, q = outs[0]
+    top_out[0:32] = jnp.where(last, p + tt * recip(g) * q, q)
+    kf, kl, z, tt, g, p, q = e_merged
+    tg = tt * recip(g)
+    for i, (a, b) in enumerate(((z + tt * tg, g), (p + tg * q, q), (kf, kl))):
+        top_out[32 + i : 33 + i] = jnp.where(last, a, b)
     write_pack(pair_out, pair, e_pair)
     write_pack(saved_out, saved, e_saved)
-    write_pack(top_out, *tops)
-
-
-def top_kernel(merged, near, theirs, sv1, sv2, sv3, own, send):
+
+
+def read_top(matrix, values):
+    main = (matrix[0:32], values[0:32], matrix[32:64])
+    return main, tuple(values[32 + i : 33 + i] for i in range(3))
+
+
+def top_kernel(merged, near_m, near, theirs_m, theirs, sv1, sv2, sv3, own, send):
     me_x = lax.axis_index("gx")
     far = lax.div(me_x, 8) == 1
     mm = read_pack(merged, 7)
-    n, t = read_pack(near, 3), read_pack(theirs, 3)
+    n, t = read_top(near_m, near), read_top(theirs_m, theirs)
     saved = [read_pack(r, 6) for r in (sv1, sv2, sv3)]
     final = []
     for part in range(2):
@@ -609,12 +627,12 @@
         [(512, 128), (5, 64, 128)],
         "fields",
         cot, temp, substrate_top, deposit_top, top_class,
-        far_in=5, sems=5,
+        far_in=5, sems=8,
     )
     other_m = swap(send_m, 1)
     ypack, fac, ties = call(
         first_kernel,
-        [(8, 40, 128), (3, 63, 8, 128), (12, 8, 128)],
+        [(8, 32, 128), (3, 63, 8, 128), (12, 8, 128)],
         [(3, 512, 128), (512, 128)],
         "first",
         cot, sub, dep, cls, cond,
@@ -632,12 +650,13 @@
     )
     m1, sv1 = call(core_kernel, [(72, 128), (200, 128)], [], "merge_core", keep, swap(send, 1), core_c)
     ring_v = [swap(m1, bit) for bit in (4, 7, 3)]
-    matrix, mine_c, other_c, ring_c = call(
-        ring_matrix_kernel, [(160, 128)] + [(224, 128)] * 3, [], "matrix_ring", mm, *ring_m
+    matrix, mine_c, other_c, ring_c, near_m = call(
+        ring_matrix_kernel, [(160, 128)] + [(224, 128)] * 3 + [(64, 128)], [], "matrix_ring", mm, *ring_m
     )
+    opposite_m = swap(near_m, 9)
     m3, sv2, sv3, near = call(
         ring_kernel,
-        [(232, 128), (200, 128), (200, 128), (104, 128)],
+        [(232, 128), (200, 128), (200, 128), (40, 128)],
         [],
         "merge_ring",
         m1, *ring_v, matrix, mine_c, other_c, ring_c,
@@ -646,7 +665,7 @@
     coefs = call(coef_kernel, [(512, 128)] * 5, [], "coef", cond, kh, a2, cot, sub, dep, cls)
     opposite = swap(near, 9)
     sv3, coefs = lax.optimization_barrier((sv3, coefs))
-    own, out = call(top_kernel, [(72, 128), (64, 128)], [], "top", m3, near, opposite, sv1, sv2, sv3)
+    own, out = call(top_kernel, [(72, 128), (64, 128)], [], "top", m3, near_m, near, opposite_m, opposite, sv1, sv2, sv3)
     got = swap(out, 1)
     grad_temp, grad_source = call(
         last_kernel,

time: 35.7 us -> 34.9 us (0.978)
  waiting for transfers between devices: 8.61 us -> 5.21 us
  starting transfers between devices: 21.2 us -> 23.8 us
    ppermute x10 -> x11, waiting for transfers between devices: 7.72 us -> 4.62 us  [swap(): return lax.ppermute(v, 'gx', [(i, i ^ bit) for i in range(16)])]
    ppermute x10 -> x11, starting transfers between devices: 16.1 us -> 18.7 us  [swap(): return lax.ppermute(v, 'gx', [(i, i ^ bit) for i in range(16)])]
  transfers between devices with their start and end apart: 11 -> 12, of which waited for: 5 -> 5; matrix products, arithmetic and copies ran while one was open for 0% -> 0% of each run, Pallas kernels for 6% -> 6%
where the time goes in v9:
time: 34.9 us; the launch traced here: 34.7 us
  starting transfers between devices  23.8 us (68%)
  waiting for transfers between devices  5.21 us (15%)
  Pallas kernels  4.96 us (14%)
  between operations  0.69 us (2%)
    ppermute x11, starting transfers between devices, swap(): return lax.ppermute(v, 'gx', [(i, i ^ bit) for i in range(16)])  18.7 us
    all_to_all x1, starting transfers between devices, body(): gat = lax.all_to_all(ypack, 'gy', split_axis=0, concat_axis=0, tiled=True)  5.16 us
    pallas_call x10, Pallas kernels, call(): pl.pallas_call(kernel, out_shape=shapes, in_specs=[HBM if i < far_in else...  4.96 us
    ppermute x11, waiting for transfers between devices, swap(): return lax.ppermute(v, 'gx', [(i, i ^ bit) for i in range(16)])  4.62 us
  transfers between devices with their start and end apart: 12, of which 5 were waited for; matrix products, arithmetic and copies ran while one was open for 0% of the time, Pallas kernels for 6%

profile of v9, /device:TPU:1, one launch (start us, length us, event | category | flops | bytes accessed | tf_op | source)
XLA Modules:
  0.0 34.7 jit_solution(3903328898723912832)
XLA Ops:
  0.6 1.2 %fields.1 = (f32[512,128]{1,0:T(8,128)S(1)}, f32[160,128]{1,0:T(8,128)S(1)}, f32[160,128]{1,0:T(8,128)S(1)}, f32[512,128]{1,0:T(8,128)S(1)}, s32[8,128]{1,0:T(8,...) custom-call(f32[512,128]{1,0:T(8,128)} %bitcast.4, f32[512,128]{1,0:T(8,128)} %bitcast.5, s32[8,128]{1,0:T(8,128)} %sub_in.1, ...), custom_call_target="tpu_custom_call" | custom-call | tf_op jit(solution)/shard_map/fields/pallas_call | solution.py:605
  1.8 1.5 %collective-permute-start = (f32[160,128]{1,0:T(8,128)S(1)}, f32[160,128]{1,0:T(8,128)S(1)}, u32[]{:S(2)}, u32[]{:S(2)}) collective-permute-start(f32[160,128]{1,0:T(8,128)S(1)} %get-tuple-element.51), channel_id=1, source_target_pairs={{0,8},{8,0},{16,24},{24,16},{32,40},{40,32},{48,56},{56,48},{64,72... | collective-permute-start | bytes 245768 | tf_op jit(solution)/shard_map/ppermute | solution.py:617
  3.3 1.3 %first.1 = (f32[8,32,128]{2,1,0:T(8,128)}, f32[3,63,8,128]{3,2,1,0:T(8,128)S(1)}, f32[12,8,128]{2,1,0:T(8,128)S(1)}) custom-call(f32[512,128]{1,0:T(8,128)S(1)} %get-tuple-element.53.cot, s32[8,128]{1,0:T(8,128)S(1)} %get-tuple-element.54.sub, s32[8,128]{1,0:T(8,128)S(1)} %get-tuple-element.55.dep, s32[8,128]{1,0:T(8,128)S(1)} %get-tuple-element.56.cls, ...), custom_call_target="tpu_custom_call" | custom-call | tf_op jit(solution)/shard_map/first/pallas_call | solution.py:605
  4.6 0.0 collective-permute-done.theirs
  4.6 5.2 %all-to-all-start = ((f32[8,32,128]{2,1,0:T(8,128)}), f32[8,32,128]{2,1,0:T(8,128)S(1)}, u32[]{:S(2)}, u32[]{:S(2)}) async-start(f32[8,32,128]{2,1,0:T(8,128)} %get-tuple-element.59), calls=%async_computation | async-start | bytes 262144 | tf_op jit(solution)/shard_map/all_to_all | solution.py:642
  9.8 3.6 %collective-permute-start.5 = (f32[160,128]{1,0:T(8,128)S(1)}, f32[160,128]{1,0:T(8,128)S(1)}, u32[]{:S(2)}, u32[]{:S(2)}) collective-permute-start(f32[160,128]{1,0:T(8,128)S(1)} %get-tuple-element.66.own), channel_id=1, source_target_pairs={{0,32},{8,40},{16,48},{24,56},{32,0},{40,8},{48,16},{56,24},{64,96... | collective-permute-start | bytes 245768 | tf_op jit(solution)/shard_map/ppermute | solution.py:617
  13.4 0.9 %collective-permute-start.6 = (f32[160,128]{1,0:T(8,128)S(1)}, f32[160,128]{1,0:T(8,128)S(1)}, u32[]{:S(2)}, u32[]{:S(2)}) collective-permute-start(f32[160,128]{1,0:T(8,128)S(1)} %get-tuple-element.66.own), channel_id=1, source_target_pairs={{0,56},{8,48},{16,40},{24,32},{32,24},{40,16},{48,8},{56,0},{64,12... | collective-permute-start | bytes 245768 | tf_op jit(solution)/shard_map/ppermute | solution.py:617
  14.3 0.3 collective-permute-start.7
  14.6 0.6 %all-to-all-done.gat = f32[8,32,128]{2,1,0:T(8,128)S(1)} async-done(((f32[8,32,128]{2,1,0:T(8,128)}), f32[8,32,128]{2,1,0:T(8,128)S(1)}, u32[]{:S(2)}, u32[]{:S(2)}) %all-to-all-start) | async-done | bytes 131104 | tf_op jit(solution)/shard_map/all_to_all | solution.py:642
  15.2 0.5 %second.1 = (f32[72,128]{1,0:T(8,128)S(1)}, f32[72,128]{1,0:T(8,128)S(1)}, f32[8,24,8,128]{3,2,1,0:T(8,128)S(1)}, f32[24,1,128]{2,1,0:T(1,128)S(1)}, f32[512,128]{1,0:T(8,128)S(1)}, /*index=5*/f32[8,128]{1,0:T(8,128)S(1)}) custom-call(f32[8,32,128]{2,1,0:T(8,128)S(1)} %all-to-all-done.gat, f32[3,63,8,128]{3,2,1,0:T(8,128)S(1)} %get-tuple-element.60.fac, ...), custom_call_target="tpu_custom_call" | custom-call | tf_op jit(solution)/shard_map/second/pallas_call | solution.py:605
  15.7 1.6 %collective-permute-start.1 = (f32[72,128]{1,0:T(8,128)S(1)}, f32[72,128]{1,0:T(8,128)S(1)}, u32[]{:S(2)}, u32[]{:S(2)}) collective-permute-start(f32[72,128]{1,0:T(8,128)S(1)} %get-tuple-element.63), channel_id=1, source_target_pairs={{0,8},{8,0},{16,24},{24,16},{32,40},{40,32},{48,56},{56,48},{64,72... | collective-permute-start | bytes 110600 | tf_op jit(solution)/shard_map/ppermute | solution.py:617
  17.2 0.9 %collective-permute-done.1.theirs = f32[72,128]{1,0:T(8,128)S(1)} collective-permute-done((f32[72,128]{1,0:T(8,128)S(1)}, f32[72,128]{1,0:T(8,128)S(1)}, u32[]{:S(2)}, u32[]{:S(2)}) %collective-permute-start.1) | collective-permute-done | bytes 36896 | tf_op jit(solution)/shard_map/ppermute | solution.py:617
  18.1 3.7 %collective-permute-start.2 = (f32[72,128]{1,0:T(8,128)S(1)}, f32[72,128]{1,0:T(8,128)S(1)}, u32[]{:S(2)}, u32[]{:S(2)}) collective-permute-start(f32[72,128]{1,0:T(8,128)S(1)} %get-tuple-element.65.own), channel_id=1, source_target_pairs={{0,32},{8,40},{16,48},{24,56},{32,0},{40,8},{48,16},{56,24},{64,96... | collective-permute-start | bytes 110600 | tf_op jit(solution)/shard_map/ppermute | solution.py:617
  21.8 0.9 %collective-permute-start.3 = (f32[72,128]{1,0:T(8,128)S(1)}, f32[72,128]{1,0:T(8,128)S(1)}, u32[]{:S(2)}, u32[]{:S(2)}) collective-permute-start(f32[72,128]{1,0:T(8,128)S(1)} %get-tuple-element.65.own), channel_id=1, source_target_pairs={{0,56},{8,48},{16,40},{24,32},{32,24},{40,16},{48,8},{56,0},{64,12... | collective-permute-start | bytes 110600 | tf_op jit(solution)/shard_map/ppermute | solution.py:617
  22.8 0.0 collective-permute-done.5.mid
  22.8 0.3 collective-permute-start.4
  23.1 0.0 collective-permute-done.6.far
  23.1 0.0 collective-permute-done.7.near
  23.1 0.1 matrix_ring.1
  23.2 2.5 %collective-permute-start.8 = (f32[64,128]{1,0:T(8,128)S(1)}, f32[64,128]{1,0:T(8,128)S(1)}, u32[]{:S(2)}, u32[]{:S(2)}) collective-permute-start(f32[64,128]{1,0:T(8,128)S(1)} %get-tuple-element.72.near_m), channel_id=1, source_target_pairs={{0,72},{8,64},{16,88},{24,80},{32,104},{40,96},{48,120},{56,112},{... | collective-permute-start | bytes 98312 | tf_op jit(solution)/shard_map/ppermute | solution.py:617
  25.6 0.0 collective-permute-done.2.mid
  25.6 1.3 %collective-permute-done.3.far = f32[72,128]{1,0:T(8,128)S(1)} collective-permute-done((f32[72,128]{1,0:T(8,128)S(1)}, f32[72,128]{1,0:T(8,128)S(1)}, u32[]{:S(2)}, u32[]{:S(2)}) %collective-permute-start.3) | collective-permute-done | bytes 36896 | tf_op jit(solution)/shard_map/ppermute | solution.py:617
  27.0 0.0 collective-permute-done.4.near
  27.0 0.1 merge_ring.1
  27.0 3.0 %collective-permute-start.9 = (f32[40,128]{1,0:T(8,128)S(1)}, f32[40,128]{1,0:T(8,128)S(1)}, u32[]{:S(2)}, u32[]{:S(2)}) collective-permute-start(f32[40,128]{1,0:T(8,128)S(1)} %get-tuple-element.73.near), channel_id=1, source_target_pairs={{0,72},{8,64},{16,88},{24,80},{32,104},{40,96},{48,120},{56,112},{... | collective-permute-start | bytes 61448 | tf_op jit(solution)/shard_map/ppermute | solution.py:617
  30.0 0.2 coef.1
  30.3 0.0 collective-permute-done.8.theirs_m
  30.3 1.5 %collective-permute-done.9.theirs = f32[40,128]{1,0:T(8,128)S(1)} collective-permute-done((f32[40,128]{1,0:T(8,128)S(1)}, f32[40,128]{1,0:T(8,128)S(1)}, u32[]{:S(2)}, u32[]{:S(2)}) %collective-permute-start.9) | collective-permute-done | bytes 20512 | tf_op jit(solution)/shard_map/ppermute | solution.py:617
  31.8 0.1 top.1
  31.9 0.5 %collective-permute-start.10 = (f32[64,128]{1,0:T(8,128)S(1)}, f32[64,128]{1,0:T(8,128)S(1)}, u32[]{:S(2)}, u32[]{:S(2)}) collective-permute-start(f32[64,128]{1,0:T(8,128)S(1)} %get-tuple-element.88), channel_id=1, source_target_pairs={{0,8},{8,0},{16,24},{24,16},{32,40},{40,32},{48,56},{56,48},{64,72... | collective-permute-start | bytes 98312 | tf_op jit(solution)/shard_map/ppermute | solution.py:617
  32.4 0.9 %collective-permute-done.10.got = f32[64,128]{1,0:T(8,128)S(1)} collective-permute-done((f32[64,128]{1,0:T(8,128)S(1)}, f32[64,128]{1,0:T(8,128)S(1)}, u32[]{:S(2)}, u32[]{:S(2)}) %collective-permute-start.10) | collective-permute-done | bytes 32800 | tf_op jit(solution)/shard_map/ppermute | solution.py:617
  33.2 1.5 %last.1 = (f32[512,128]{1,0:T(8,128)}, f32[512,128]{1,0:T(8,128)}) custom-call(f32[72,128]{1,0:T(8,128)S(1)} %get-tuple-element.87.own, f32[64,128]{1,0:T(8,128)S(1)} %collective-permute-done.10.got, f32[8,24,8,128]{3,2,1,0:T(8,128)S(1)} %get-tuple-element.89.xfac, f32[24,1,128]{2,1,0:T(1,128)S(1)} %get-tuple-element.90.xhfac, ...), custom_call_target="tpu_custom_call" | custom-call | tf_op jit(solution)/shard_map/last/pallas_call | solution.py:605
  (2 shorter events, 0.1 us)
Async XLA Ops:
  1.8 2.8 %collective-permute-start = (f32[160,128]{1,0:T(8,128)S(1)}, f32[160,128]{1,0:T(8,128)S(1)}, u32[]{:S(2)}, u32[]{:S(2)}) collective-permute-start(f32[160,128]{1,0:T(8,128)S(1)} %get-tuple-element.51), channel_id=1, source_target_pairs={{0,8},{8,0},{16,24},{24,16},{32,40},{40,32},{48,56},{56,48},{64,72... | collective-permute-start | bytes 245768 | tf_op jit(solution)/shard_map/ppermute | solution.py:617
  4.6 10.5 %all-to-all-start = ((f32[8,32,128]{2,1,0:T(8,128)}), f32[8,32,128]{2,1,0:T(8,128)S(1)}, u32[]{:S(2)}, u32[]{:S(2)}) async-start(f32[8,32,128]{2,1,0:T(8,128)} %get-tuple-element.59), calls=%async_computation | async-start | bytes 262144 | tf_op jit(solution)/shard_map/all_to_all | solution.py:642
  9.8 13.0 %collective-permute-start.5 = (f32[160,128]{1,0:T(8,128)S(1)}, f32[160,128]{1,0:T(8,128)S(1)}, u32[]{:S(2)}, u32[]{:S(2)}) collective-permute-start(f32[160,128]{1,0:T(8,128)S(1)} %get-tuple-element.66.own), channel_id=1, source_target_pairs={{0,32},{8,40},{16,48},{24,56},{32,0},{40,8},{48,16},{56,24},{64,96... | collective-permute-start | bytes 245768 | tf_op jit(solution)/shard_map/ppermute | solution.py:617
  13.4 9.7 %collective-permute-start.6 = (f32[160,128]{1,0:T(8,128)S(1)}, f32[160,128]{1,0:T(8,128)S(1)}, u32[]{:S(2)}, u32[]{:S(2)}) collective-permute-start(f32[160,128]{1,0:T(8,128)S(1)} %get-tuple-element.66.own), channel_id=1, source_target_pairs={{0,56},{8,48},{16,40},{24,32},{32,24},{40,16},{48,8},{56,0},{64,12... | collective-permute-start | bytes 245768 | tf_op jit(solution)/shard_map/ppermute | solution.py:617
  14.3 8.8 %collective-permute-start.7 = (f32[160,128]{1,0:T(8,128)S(1)}, f32[160,128]{1,0:T(8,128)S(1)}, u32[]{:S(2)}, u32[]{:S(2)}) collective-permute-start(f32[160,128]{1,0:T(8,128)S(1)} %get-tuple-element.66.own), channel_id=1, source_target_pairs={{0,24},{8,16},{16,8},{24,0},{32,56},{40,48},{48,40},{56,32},{64,88... | collective-permute-start | bytes 245768 | tf_op jit(solution)/shard_map/ppermute | solution.py:617
  15.7 2.4 %collective-permute-start.1 = (f32[72,128]{1,0:T(8,128)S(1)}, f32[72,128]{1,0:T(8,128)S(1)}, u32[]{:S(2)}, u32[]{:S(2)}) collective-permute-start(f32[72,128]{1,0:T(8,128)S(1)} %get-tuple-element.63), channel_id=1, source_target_pairs={{0,8},{8,0},{16,24},{24,16},{32,40},{40,32},{48,56},{56,48},{64,72... | collective-permute-start | bytes 110600 | tf_op jit(solution)/shard_map/ppermute | solution.py:617
  18.1 7.5 %collective-permute-start.2 = (f32[72,128]{1,0:T(8,128)S(1)}, f32[72,128]{1,0:T(8,128)S(1)}, u32[]{:S(2)}, u32[]{:S(2)}) collective-permute-start(f32[72,128]{1,0:T(8,128)S(1)} %get-tuple-element.65.own), channel_id=1, source_target_pairs={{0,32},{8,40},{16,48},{24,56},{32,0},{40,8},{48,16},{56,24},{64,96... | collective-permute-start | bytes 110600 | tf_op jit(solution)/shard_map/ppermute | solution.py:617
  21.8 5.2 %collective-permute-start.3 = (f32[72,128]{1,0:T(8,128)S(1)}, f32[72,128]{1,0:T(8,128)S(1)}, u32[]{:S(2)}, u32[]{:S(2)}) collective-permute-start(f32[72,128]{1,0:T(8,128)S(1)} %get-tuple-element.65.own), channel_id=1, source_target_pairs={{0,56},{8,48},{16,40},{24,32},{32,24},{40,16},{48,8},{56,0},{64,12... | collective-permute-start | bytes 110600 | tf_op jit(solution)/shard_map/ppermute | solution.py:617
  22.8 4.2 %collective-permute-start.4 = (f32[72,128]{1,0:T(8,128)S(1)}, f32[72,128]{1,0:T(8,128)S(1)}, u32[]{:S(2)}, u32[]{:S(2)}) collective-permute-start(f32[72,128]{1,0:T(8,128)S(1)} %get-tuple-element.65.own), channel_id=1, source_target_pairs={{0,24},{8,16},{16,8},{24,0},{32,56},{40,48},{48,40},{56,32},{64,88... | collective-permute-start | bytes 110600 | tf_op jit(solution)/shard_map/ppermute | solution.py:617
  23.2 7.1 %collective-permute-start.8 = (f32[64,128]{1,0:T(8,128)S(1)}, f32[64,128]{1,0:T(8,128)S(1)}, u32[]{:S(2)}, u32[]{:S(2)}) collective-permute-start(f32[64,128]{1,0:T(8,128)S(1)} %get-tuple-element.72.near_m), channel_id=1, source_target_pairs={{0,72},{8,64},{16,88},{24,80},{32,104},{40,96},{48,120},{56,112},{... | collective-permute-start | bytes 98312 | tf_op jit(solution)/shard_map/ppermute | solution.py:617
  27.0 4.8 %collective-permute-start.9 = (f32[40,128]{1,0:T(8,128)S(1)}, f32[40,128]{1,0:T(8,128)S(1)}, u32[]{:S(2)}, u32[]{:S(2)}) collective-permute-start(f32[40,128]{1,0:T(8,128)S(1)} %get-tuple-element.73.near), channel_id=1, source_target_pairs={{0,72},{8,64},{16,88},{24,80},{32,104},{40,96},{48,120},{56,112},{... | collective-permute-start | bytes 61448 | tf_op jit(solution)/shard_map/ppermute | solution.py:617
  31.9 1.3 %collective-permute-start.10 = (f32[64,128]{1,0:T(8,128)S(1)}, f32[64,128]{1,0:T(8,128)S(1)}, u32[]{:S(2)}, u32[]{:S(2)}) collective-permute-start(f32[64,128]{1,0:T(8,128)S(1)} %get-tuple-element.88), channel_id=1, source_target_pairs={{0,8},{8,0},{16,24},{24,16},{32,40},{40,32},{48,56},{56,48},{64,72... | collective-permute-start | bytes 98312 | tf_op jit(solution)/shard_map/ppermute | solution.py:617

commit v10 on v9

--- a/solution.py
+++ b/solution.py
@@ -536,6 +536,8 @@
         k_l[rows] = (2.0 * R) * jnp.minimum(k, k_h)
         if z < 63:
             k_z[rows] = (2.0 * R) * jnp.minimum(k, cond[8 * z + 8 : 8 * z + 16])
+        else:
+            k_z[rows] = jnp.zeros((8, 128), F32)
         film = film_y + top * (dep_v - 1 == z).astype(F32)
         if z == 0:
             film = film + BOTTOM
@@ -543,51 +545,82 @@
         base[rows] = cot[rows] - 2.0 * a2[rows]
 
 
-def last_kernel(
-    own, got, xfac, xhfac, k_y, k_l, k_z, k_s, base, sub, temp_out, src_out, s1, fu, t_buf, s_buf, sems
-):
-    core = own_half()
-    for i in range(2):
-        fu[i, pl.ds(pl.multiple_of(32 * core, 32), 32), :] = own[32 * i : 32 * i + 32]
-        fu[i, pl.ds(pl.multiple_of(32 - 32 * core, 32), 32), :] = got[32 * i : 32 * i + 32]
+def expand_rows(xfac, half, flux, last, s1):
+    for chunk in range(4):
+        rows = slice(8 * chunk, 8 * chunk + 8)
+        levels, tie = load_x(xfac.at[4 * half + chunk])
+        u = expand_chain(last[rows], levels, tie, flux[rows])
+        for x in range(8):
+            s1[pl.ds(64 * chunk + x, 8, stride=8), :] = u[x]
+
+
+def stencil(half, uh, s1, k_y, k_l, k_z, k_s, base, sub_v, below, above, src, out, done=None):
+    lane = lax.broadcasted_iota(jnp.int32, (8, 128), 1)
+    first, final = lane == 0, lane == 127
+    up = below
+    for i in range(32):
+        rows = slice(8 * i, 8 * i + 8)
+        at = pl.ds(pl.multiple_of(256 * half + 8 * i, 8), 8)
+        s = s1[rows]
+        s_h = pltpu.roll(uh, 128 - 2 * i, 1) if i else uh
+        f_y = k_y[at, :] * (jnp.where(final, s_h, pltpu.roll(s, 127, 1)) - s)
+        f_l = k_l[at, :] * (s - s_h)
+        total = f_y - jnp.where(first, f_l, pltpu.roll(f_y, 1, 1))
+        f_z = k_z[at, :] * (s1[8 * i + 8 : 8 * i + 16] - s) if i < 31 else above
+        if f_z is not None:
+            total = total + f_z
+        if up is not None:
+            total = total - up
+        up = f_z
+        src[rows] = jnp.where(32 * half + i < sub_v, 1.0, 0.6) * s
+        out[rows] = base[at, :] + k_s[at, :] * s + total
+        if done is not None and i & 7 == 7:
+            done(i // 8)
+
+
+def own_kernel(own, xfac, xhfac, k_y, k_l, k_z, k_s, base, sub, s1, src, out, uh_out):
+    half = own_half()
     levels, tie = load_x(xhfac)
     uh = jnp.concatenate(expand_chain(own[65:66], levels, tie, own[64:65]), axis=0)
-    sub_v = sub[...]
-    lane = lax.broadcasted_iota(jnp.int32, (8, 128), 1)
-    first, final = lane == 0, lane == 127
-    up, copies = None, []
-
-    def expand(chunk):
-        rows = slice(8 * chunk, 8 * chunk + 8)
-        levels, tie = load_x(xfac.at[chunk])
-        u = expand_chain(fu[1, rows], levels, tie, fu[0, rows])
-        for x in range(8):
-            s1[pl.ds(64 * chunk + x, 8, stride=8), :] = u[x]
-
-    expand(0)
-    for z in range(64):
-        if z & 7 == 0 and z < 56:
-            expand(z // 8 + 1)
-        rows = slice(8 * z, 8 * z + 8)
-        s = s1[rows]
-        s_h = pltpu.roll(uh, 128 - 2 * z, 1) if z else uh
-        f_y = k_y[rows] * (jnp.where(final, s_h, pltpu.roll(s, 127, 1)) - s)
-        f_l = k_l[rows] * (s - s_h)
-        total = f_y - jnp.where(first, f_l, pltpu.roll(f_y, 1, 1))
-        if z < 63:
-            f_z = k_z[rows] * (s1[8 * z + 8 : 8 * z + 16] - s)
-            total = total + f_z
-        if z:
-            total = total - up
-        up = f_z
-        s_buf[rows] = jnp.where(z < sub_v, 1.0, 0.6) * s
-        t_buf[rows] = base[rows] + k_s[rows] * s + total
-        if z & 7 == 7:
-            part = slice(8 * z - 56, 8 * z + 8)
-            for i, (buf, out) in enumerate(((s_buf, src_out), (t_buf, temp_out))):
-                cp = pltpu.make_async_copy(buf.at[part], out.at[part], sems.at[2 * (z // 8) + i])
-                cp.start()
-                copies.append(cp)
+    turned = pltpu.roll(uh, 64, 1)
+    uh_out[...] = jnp.where(half == 1, uh, turned)
+    expand_rows(xfac, half, own.at[0:32], own.at[32:64], s1)
+    uh = jnp.where(half == 1, turned, uh)
+    stencil(half, uh, s1, k_y, k_l, k_z, k_s, base, sub[...], None, None, src, out)
+
+
+def last_kernel(
+    got, xfac, k_y, k_l, k_z, k_s, base, sub, s_own, src_own, out_own, uh, temp_out, src_out, s1, ends, t_buf, s_buf, sems
+):
+    mine = own_half()
+    half = 1 - mine
+    copies = []
+
+    def send(buf, rows, out, start):
+        size = rows.stop - rows.start
+        cp = pltpu.make_async_copy(buf.at[rows], out.at[pl.ds(pl.multiple_of(start, 8), size)], sems.at[len(copies)])
+        cp.start()
+        copies.append(cp)
+
+    send(src_own, slice(0, 256), src_out, 256 * mine)
+    send(out_own, slice(8, 248), temp_out, 256 * mine + 8)
+    expand_rows(xfac, half, got.at[0:32], got.at[32:64], s1)
+    inner, outer = s_own[248:256], s_own[0:8]
+    low = jnp.where(half == 0, s1[248:256], inner)
+    high = jnp.where(half == 0, outer, s1[0:8])
+    flux = k_z[248:256] * (high - low)
+    ends[0:8] = out_own[0:8] - jnp.where(mine == 1, flux, 0.0)
+    ends[8:16] = out_own[248:256] + jnp.where(mine == 0, flux, 0.0)
+    send(ends, slice(0, 8), temp_out, 256 * mine)
+    send(ends, slice(8, 16), temp_out, 256 * mine + 248)
+
+    def done(piece):
+        rows = slice(64 * piece, 64 * piece + 64)
+        send(s_buf, rows, src_out, 256 * half + 64 * piece)
+        send(t_buf, rows, temp_out, 256 * half + 64 * piece)
+
+    below, above = jnp.where(half == 1, flux, 0.0), jnp.where(half == 0, flux, 0.0)
+    stencil(half, uh[...], s1, k_y, k_l, k_z, k_s, base, sub[...], below, above, s_buf, t_buf, done)
     for cp in copies:
         cp.wait()
 
@@ -667,13 +700,20 @@
     sv3, coefs = lax.optimization_barrier((sv3, coefs))
     own, out = call(top_kernel, [(72, 128), (64, 128)], [], "top", m3, near_m, near, opposite_m, opposite, sv1, sv2, sv3)
     got = swap(out, 1)
+    part = call(
+        own_kernel,
+        [(256, 128), (256, 128), (256, 128), (8, 128)],
+        [],
+        "own_rows",
+        own, xfac, xhfac, *coefs, sub,
+    )
     grad_temp, grad_source = call(
         last_kernel,
         [(512, 128), (512, 128)],
-        [(512, 128), (2, 64, 128), (512, 128), (512, 128)],
+        [(256, 128), (16, 128), (256, 128), (256, 128)],
         "last",
-        own, got, xfac, xhfac, *coefs, sub,
-        far_out=2, sems=16,
+        got, xfac, *coefs, sub, *part,
+        far_out=2, sems=12,
     )
     return grad_temp.reshape(cotangent.shape), grad_source.reshape(cotangent.shape)
 

time: 34.9 us -> 34.5 us (0.989)
    pallas_call x10 -> x11, Pallas kernels: 4.96 us -> 4.77 us  [call(): pl.pallas_call(kernel, out_shape=shapes, in_specs=[HBM if i < far_in else...]
  transfers between devices with their start and end apart: 12 -> 12, of which waited for: 5 -> 5; matrix products, arithmetic and copies ran while one was open for 0% -> 0% of each run, Pallas kernels for 6% -> 7%
where the time goes in v10:
time: 34.5 us; the launch traced here: 34.2 us
  starting transfers between devices  23.8 us (69%)
  waiting for transfers between devices  4.92 us (14%)
  Pallas kernels  4.77 us (14%)
  between operations  0.69 us (2%)
    ppermute x11, starting transfers between devices, swap(): return lax.ppermute(v, 'gx', [(i, i ^ bit) for i in range(16)])  18.7 us
    all_to_all x1, starting transfers between devices, body(): gat = lax.all_to_all(ypack, 'gy', split_axis=0, concat_axis=0, tiled=True)  5.16 us
    pallas_call x11, Pallas kernels, call(): pl.pallas_call(kernel, out_shape=shapes, in_specs=[HBM if i < far_in else...  4.77 us
    ppermute x11, waiting for transfers between devices, swap(): return lax.ppermute(v, 'gx', [(i, i ^ bit) for i in range(16)])  4.33 us
  transfers between devices with their start and end apart: 12, of which 5 were waited for; matrix products, arithmetic and copies ran while one was open for 0% of the time, Pallas kernels for 7%

profile of v10, /device:TPU:1, one launch (start us, length us, event | category | flops | bytes accessed | tf_op | source)
XLA Modules:
  0.0 34.2 jit_solution(142038383705043277)
XLA Ops:
  0.6 1.2 %fields.1 = (f32[512,128]{1,0:T(8,128)S(1)}, f32[160,128]{1,0:T(8,128)S(1)}, f32[160,128]{1,0:T(8,128)S(1)}, f32[512,128]{1,0:T(8,128)S(1)}, s32[8,128]{1,0:T(8,...) custom-call(f32[512,128]{1,0:T(8,128)} %bitcast.4, f32[512,128]{1,0:T(8,128)} %bitcast.5, s32[8,128]{1,0:T(8,128)} %sub_in.1, ...), custom_call_target="tpu_custom_call" | custom-call | tf_op jit(solution)/shard_map/fields/pallas_call | solution.py:638
  1.8 1.5 %collective-permute-start = (f32[160,128]{1,0:T(8,128)S(1)}, f32[160,128]{1,0:T(8,128)S(1)}, u32[]{:S(2)}, u32[]{:S(2)}) collective-permute-start(f32[160,128]{1,0:T(8,128)S(1)} %get-tuple-element.55), channel_id=1, source_target_pairs={{0,8},{8,0},{16,24},{24,16},{32,40},{40,32},{48,56},{56,48},{64,72... | collective-permute-start | bytes 245768 | tf_op jit(solution)/shard_map/ppermute | solution.py:650
  3.3 1.3 %first.1 = (f32[8,32,128]{2,1,0:T(8,128)}, f32[3,63,8,128]{3,2,1,0:T(8,128)S(1)}, f32[12,8,128]{2,1,0:T(8,128)S(1)}) custom-call(f32[512,128]{1,0:T(8,128)S(1)} %get-tuple-element.57.cot, s32[8,128]{1,0:T(8,128)S(1)} %get-tuple-element.58.sub, s32[8,128]{1,0:T(8,128)S(1)} %get-tuple-element.59.dep, s32[8,128]{1,0:T(8,128)S(1)} %get-tuple-element.60.cls, ...), custom_call_target="tpu_custom_call" | custom-call | tf_op jit(solution)/shard_map/first/pallas_call | solution.py:638
  4.6 0.0 collective-permute-done.theirs
  4.6 5.2 %all-to-all-start = ((f32[8,32,128]{2,1,0:T(8,128)}), f32[8,32,128]{2,1,0:T(8,128)S(1)}, u32[]{:S(2)}, u32[]{:S(2)}) async-start(f32[8,32,128]{2,1,0:T(8,128)} %get-tuple-element.63), calls=%async_computation | async-start | bytes 262144 | tf_op jit(solution)/shard_map/all_to_all | solution.py:675
  9.8 3.6 %collective-permute-start.5 = (f32[160,128]{1,0:T(8,128)S(1)}, f32[160,128]{1,0:T(8,128)S(1)}, u32[]{:S(2)}, u32[]{:S(2)}) collective-permute-start(f32[160,128]{1,0:T(8,128)S(1)} %get-tuple-element.70.own), channel_id=1, source_target_pairs={{0,32},{8,40},{16,48},{24,56},{32,0},{40,8},{48,16},{56,24},{64,96... | collective-permute-start | bytes 245768 | tf_op jit(solution)/shard_map/ppermute | solution.py:650
  13.4 0.9 %collective-permute-start.6 = (f32[160,128]{1,0:T(8,128)S(1)}, f32[160,128]{1,0:T(8,128)S(1)}, u32[]{:S(2)}, u32[]{:S(2)}) collective-permute-start(f32[160,128]{1,0:T(8,128)S(1)} %get-tuple-element.70.own), channel_id=1, source_target_pairs={{0,56},{8,48},{16,40},{24,32},{32,24},{40,16},{48,8},{56,0},{64,12... | collective-permute-start | bytes 245768 | tf_op jit(solution)/shard_map/ppermute | solution.py:650
  14.3 0.3 collective-permute-start.7
  14.6 0.6 %all-to-all-done.gat = f32[8,32,128]{2,1,0:T(8,128)S(1)} async-done(((f32[8,32,128]{2,1,0:T(8,128)}), f32[8,32,128]{2,1,0:T(8,128)S(1)}, u32[]{:S(2)}, u32[]{:S(2)}) %all-to-all-start) | async-done | bytes 131104 | tf_op jit(solution)/shard_map/all_to_all | solution.py:675
  15.2 0.5 %second.1 = (f32[72,128]{1,0:T(8,128)S(1)}, f32[72,128]{1,0:T(8,128)S(1)}, f32[8,24,8,128]{3,2,1,0:T(8,128)S(1)}, f32[24,1,128]{2,1,0:T(1,128)S(1)}, f32[512,128]{1,0:T(8,128)S(1)}, /*index=5*/f32[8,128]{1,0:T(8,128)S(1)}) custom-call(f32[8,32,128]{2,1,0:T(8,128)S(1)} %all-to-all-done.gat, f32[3,63,8,128]{3,2,1,0:T(8,128)S(1)} %get-tuple-element.64.fac, ...), custom_call_target="tpu_custom_call" | custom-call | tf_op jit(solution)/shard_map/second/pallas_call | solution.py:638
  15.7 1.6 %collective-permute-start.1 = (f32[72,128]{1,0:T(8,128)S(1)}, f32[72,128]{1,0:T(8,128)S(1)}, u32[]{:S(2)}, u32[]{:S(2)}) collective-permute-start(f32[72,128]{1,0:T(8,128)S(1)} %get-tuple-element.67), channel_id=1, source_target_pairs={{0,8},{8,0},{16,24},{24,16},{32,40},{40,32},{48,56},{56,48},{64,72... | collective-permute-start | bytes 110600 | tf_op jit(solution)/shard_map/ppermute | solution.py:650
  17.2 0.9 %collective-permute-done.1.theirs = f32[72,128]{1,0:T(8,128)S(1)} collective-permute-done((f32[72,128]{1,0:T(8,128)S(1)}, f32[72,128]{1,0:T(8,128)S(1)}, u32[]{:S(2)}, u32[]{:S(2)}) %collective-permute-start.1) | collective-permute-done | bytes 36896 | tf_op jit(solution)/shard_map/ppermute | solution.py:650
  18.1 3.7 %collective-permute-start.2 = (f32[72,128]{1,0:T(8,128)S(1)}, f32[72,128]{1,0:T(8,128)S(1)}, u32[]{:S(2)}, u32[]{:S(2)}) collective-permute-start(f32[72,128]{1,0:T(8,128)S(1)} %get-tuple-element.69.own), channel_id=1, source_target_pairs={{0,32},{8,40},{16,48},{24,56},{32,0},{40,8},{48,16},{56,24},{64,96... | collective-permute-start | bytes 110600 | tf_op jit(solution)/shard_map/ppermute | solution.py:650
  21.8 0.9 %collective-permute-start.3 = (f32[72,128]{1,0:T(8,128)S(1)}, f32[72,128]{1,0:T(8,128)S(1)}, u32[]{:S(2)}, u32[]{:S(2)}) collective-permute-start(f32[72,128]{1,0:T(8,128)S(1)} %get-tuple-element.69.own), channel_id=1, source_target_pairs={{0,56},{8,48},{16,40},{24,32},{32,24},{40,16},{48,8},{56,0},{64,12... | collective-permute-start | bytes 110600 | tf_op jit(solution)/shard_map/ppermute | solution.py:650
  22.8 0.0 collective-permute-done.5.mid
  22.8 0.3 collective-permute-start.4
  23.1 0.0 collective-permute-done.6.far
  23.1 0.1 matrix_ring.1
  23.2 2.5 %collective-permute-start.8 = (f32[64,128]{1,0:T(8,128)S(1)}, f32[64,128]{1,0:T(8,128)S(1)}, u32[]{:S(2)}, u32[]{:S(2)}) collective-permute-start(f32[64,128]{1,0:T(8,128)S(1)} %get-tuple-element.76.near_m), channel_id=1, source_target_pairs={{0,72},{8,64},{16,88},{24,80},{32,104},{40,96},{48,120},{56,112},{... | collective-permute-start | bytes 98312 | tf_op jit(solution)/shard_map/ppermute | solution.py:650
  25.6 0.0 collective-permute-done.2.mid
  25.6 1.3 %collective-permute-done.3.far = f32[72,128]{1,0:T(8,128)S(1)} collective-permute-done((f32[72,128]{1,0:T(8,128)S(1)}, f32[72,128]{1,0:T(8,128)S(1)}, u32[]{:S(2)}, u32[]{:S(2)}) %collective-permute-start.3) | collective-permute-done | bytes 36896 | tf_op jit(solution)/shard_map/ppermute | solution.py:650
  27.0 0.0 collective-permute-done.4.near
  27.0 0.1 merge_ring.1
  27.0 3.0 %collective-permute-start.9 = (f32[40,128]{1,0:T(8,128)S(1)}, f32[40,128]{1,0:T(8,128)S(1)}, u32[]{:S(2)}, u32[]{:S(2)}) collective-permute-start(f32[40,128]{1,0:T(8,128)S(1)} %get-tuple-element.77.near), channel_id=1, source_target_pairs={{0,72},{8,64},{16,88},{24,80},{32,104},{40,96},{48,120},{56,112},{... | collective-permute-start | bytes 61448 | tf_op jit(solution)/shard_map/ppermute | solution.py:650
  30.0 0.2 coef.1
  30.3 0.0 collective-permute-done.8.theirs_m
  30.3 1.5 %collective-permute-done.9.theirs = f32[40,128]{1,0:T(8,128)S(1)} collective-permute-done((f32[40,128]{1,0:T(8,128)S(1)}, f32[40,128]{1,0:T(8,128)S(1)}, u32[]{:S(2)}, u32[]{:S(2)}) %collective-permute-start.9) | collective-permute-done | bytes 20512 | tf_op jit(solution)/shard_map/ppermute | solution.py:650
  31.8 0.1 top.1
  31.9 0.5 %collective-permute-start.10 = (f32[64,128]{1,0:T(8,128)S(1)}, f32[64,128]{1,0:T(8,128)S(1)}, u32[]{:S(2)}, u32[]{:S(2)}) collective-permute-start(f32[64,128]{1,0:T(8,128)S(1)} %get-tuple-element.91), channel_id=1, source_target_pairs={{0,8},{8,0},{16,24},{24,16},{32,40},{40,32},{48,56},{56,48},{64,72... | collective-permute-start | bytes 98312 | tf_op jit(solution)/shard_map/ppermute | solution.py:650
  32.4 0.3 own_rows.1
  32.7 0.6 %collective-permute-done.10.got = f32[64,128]{1,0:T(8,128)S(1)} collective-permute-done((f32[64,128]{1,0:T(8,128)S(1)}, f32[64,128]{1,0:T(8,128)S(1)}, u32[]{:S(2)}, u32[]{:S(2)}) %collective-permute-start.10) | collective-permute-done | bytes 32800 | tf_op jit(solution)/shard_map/ppermute | solution.py:650
  33.2 1.0 %last.1 = (f32[512,128]{1,0:T(8,128)}, f32[512,128]{1,0:T(8,128)}) custom-call(f32[64,128]{1,0:T(8,128)S(1)} %collective-permute-done.10.got, f32[8,24,8,128]{3,2,1,0:T(8,128)S(1)} %get-tuple-element.92.xfac, f32[512,128]{1,0:T(8,128)S(1)} %get-tuple-element.93.k_y, f32[512,128]{1,0:T(8,128)S(1)} %get-tuple-element.94.k_l, ...), custom_call_target="tpu_custom_call" | custom-call | tf_op jit(solution)/shard_map/last/pallas_call | solution.py:638
  (3 shorter events, 0.1 us)
Async XLA Ops:
  1.8 2.8 %collective-permute-start = (f32[160,128]{1,0:T(8,128)S(1)}, f32[160,128]{1,0:T(8,128)S(1)}, u32[]{:S(2)}, u32[]{:S(2)}) collective-permute-start(f32[160,128]{1,0:T(8,128)S(1)} %get-tuple-element.55), channel_id=1, source_target_pairs={{0,8},{8,0},{16,24},{24,16},{32,40},{40,32},{48,56},{56,48},{64,72... | collective-permute-start | bytes 245768 | tf_op jit(solution)/shard_map/ppermute | solution.py:650
  4.6 10.5 %all-to-all-start = ((f32[8,32,128]{2,1,0:T(8,128)}), f32[8,32,128]{2,1,0:T(8,128)S(1)}, u32[]{:S(2)}, u32[]{:S(2)}) async-start(f32[8,32,128]{2,1,0:T(8,128)} %get-tuple-element.63), calls=%async_computation | async-start | bytes 262144 | tf_op jit(solution)/shard_map/all_to_all | solution.py:675
  9.8 13.0 %collective-permute-start.5 = (f32[160,128]{1,0:T(8,128)S(1)}, f32[160,128]{1,0:T(8,128)S(1)}, u32[]{:S(2)}, u32[]{:S(2)}) collective-permute-start(f32[160,128]{1,0:T(8,128)S(1)} %get-tuple-element.70.own), channel_id=1, source_target_pairs={{0,32},{8,40},{16,48},{24,56},{32,0},{40,8},{48,16},{56,24},{64,96... | collective-permute-start | bytes 245768 | tf_op jit(solution)/shard_map/ppermute | solution.py:650
  13.4 9.7 %collective-permute-start.6 = (f32[160,128]{1,0:T(8,128)S(1)}, f32[160,128]{1,0:T(8,128)S(1)}, u32[]{:S(2)}, u32[]{:S(2)}) collective-permute-start(f32[160,128]{1,0:T(8,128)S(1)} %get-tuple-element.70.own), channel_id=1, source_target_pairs={{0,56},{8,48},{16,40},{24,32},{32,24},{40,16},{48,8},{56,0},{64,12... | collective-permute-start | bytes 245768 | tf_op jit(solution)/shard_map/ppermute | solution.py:650
  14.3 8.8 %collective-permute-start.7 = (f32[160,128]{1,0:T(8,128)S(1)}, f32[160,128]{1,0:T(8,128)S(1)}, u32[]{:S(2)}, u32[]{:S(2)}) collective-permute-start(f32[160,128]{1,0:T(8,128)S(1)} %get-tuple-element.70.own), channel_id=1, source_target_pairs={{0,24},{8,16},{16,8},{24,0},{32,56},{40,48},{48,40},{56,32},{64,88... | collective-permute-start | bytes 245768 | tf_op jit(solution)/shard_map/ppermute | solution.py:650
  15.7 2.4 %collective-permute-start.1 = (f32[72,128]{1,0:T(8,128)S(1)}, f32[72,128]{1,0:T(8,128)S(1)}, u32[]{:S(2)}, u32[]{:S(2)}) collective-permute-start(f32[72,128]{1,0:T(8,128)S(1)} %get-tuple-element.67), channel_id=1, source_target_pairs={{0,8},{8,0},{16,24},{24,16},{32,40},{40,32},{48,56},{56,48},{64,72... | collective-permute-start | bytes 110600 | tf_op jit(solution)/shard_map/ppermute | solution.py:650
  18.1 7.5 %collective-permute-start.2 = (f32[72,128]{1,0:T(8,128)S(1)}, f32[72,128]{1,0:T(8,128)S(1)}, u32[]{:S(2)}, u32[]{:S(2)}) collective-permute-start(f32[72,128]{1,0:T(8,128)S(1)} %get-tuple-element.69.own), channel_id=1, source_target_pairs={{0,32},{8,40},{16,48},{24,56},{32,0},{40,8},{48,16},{56,24},{64,96... | collective-permute-start | bytes 110600 | tf_op jit(solution)/shard_map/ppermute | solution.py:650
  21.8 5.2 %collective-permute-start.3 = (f32[72,128]{1,0:T(8,128)S(1)}, f32[72,128]{1,0:T(8,128)S(1)}, u32[]{:S(2)}, u32[]{:S(2)}) collective-permute-start(f32[72,128]{1,0:T(8,128)S(1)} %get-tuple-element.69.own), channel_id=1, source_target_pairs={{0,56},{8,48},{16,40},{24,32},{32,24},{40,16},{48,8},{56,0},{64,12... | collective-permute-start | bytes 110600 | tf_op jit(solution)/shard_map/ppermute | solution.py:650
  22.8 4.2 %collective-permute-start.4 = (f32[72,128]{1,0:T(8,128)S(1)}, f32[72,128]{1,0:T(8,128)S(1)}, u32[]{:S(2)}, u32[]{:S(2)}) collective-permute-start(f32[72,128]{1,0:T(8,128)S(1)} %get-tuple-element.69.own), channel_id=1, source_target_pairs={{0,24},{8,16},{16,8},{24,0},{32,56},{40,48},{48,40},{56,32},{64,88... | collective-permute-start | bytes 110600 | tf_op jit(solution)/shard_map/ppermute | solution.py:650
  23.2 7.1 %collective-permute-start.8 = (f32[64,128]{1,0:T(8,128)S(1)}, f32[64,128]{1,0:T(8,128)S(1)}, u32[]{:S(2)}, u32[]{:S(2)}) collective-permute-start(f32[64,128]{1,0:T(8,128)S(1)} %get-tuple-element.76.near_m), channel_id=1, source_target_pairs={{0,72},{8,64},{16,88},{24,80},{32,104},{40,96},{48,120},{56,112},{... | collective-permute-start | bytes 98312 | tf_op jit(solution)/shard_map/ppermute | solution.py:650
  27.0 4.8 %collective-permute-start.9 = (f32[40,128]{1,0:T(8,128)S(1)}, f32[40,128]{1,0:T(8,128)S(1)}, u32[]{:S(2)}, u32[]{:S(2)}) collective-permute-start(f32[40,128]{1,0:T(8,128)S(1)} %get-tuple-element.77.near), channel_id=1, source_target_pairs={{0,72},{8,64},{16,88},{24,80},{32,104},{40,96},{48,120},{56,112},{... | collective-permute-start | bytes 61448 | tf_op jit(solution)/shard_map/ppermute | solution.py:650
  31.9 1.3 %collective-permute-start.10 = (f32[64,128]{1,0:T(8,128)S(1)}, f32[64,128]{1,0:T(8,128)S(1)}, u32[]{:S(2)}, u32[]{:S(2)}) collective-permute-start(f32[64,128]{1,0:T(8,128)S(1)} %get-tuple-element.91), channel_id=1, source_target_pairs={{0,8},{8,0},{16,24},{24,16},{32,40},{40,32},{48,56},{56,48},{64,72... | collective-permute-start | bytes 98312 | tf_op jit(solution)/shard_map/ppermute | solution.py:650

commit v11 on v10

--- a/solution.py
+++ b/solution.py
@@ -186,7 +186,13 @@
         send[32 * i : 32 * i + 32] = planes[i, pl.ds(pl.multiple_of(32 - 32 * core, 32), 32), :]
 
 
-def fields_kernel(cot_in, temp_in, sub_in, dep_in, cls_in, cond, keep, send, cot, sub, dep, cls, temp, planes, sems):
+def turned(rows, dst, q):
+    block = jnp.transpose(rows)
+    for h in range(2):
+        dst[pl.ds(4 * h + q, 64, stride=8), :] = block[64 * h : 64 * h + 64]
+
+
+def fields_kernel(cot_in, temp_in, sub_in, dep_in, cls_in, cond, keep, send, cot, sub, dep, cls, sub_t, temp, planes, sems):
     pieces = [slice(128 * i, 128 * i + 128) for i in range(4)]
     pairs = [(sub_in, sub), (dep_in, dep)] + [(temp_in.at[r], temp.at[r]) for r in pieces]
     pairs += [(cls_in, cls), (cot_in, cot)]
@@ -196,6 +202,10 @@
     for cp in copies[:2]:
         cp.wait()
     sub_v, dep_v = sub[...], dep[...]
+    subf = sub_v.astype(F32)
+    upper = (lax.broadcasted_iota(jnp.int32, (128, 128), 0) & 1) == 1
+    for q in range(4):
+        turned(jnp.where(upper, subf[q + 4 : q + 5], subf[q : q + 1]), sub_t, q)
     for z in range(64):
         if z % 16 == 0:
             copies[2 + z // 16].wait()
@@ -218,7 +228,7 @@
         cp.wait()
 
 
-def first_kernel(cot, sub, dep, cls, cond, ypack, fac, tie_out, mid, tr):
+def first_kernel(cot, sub, dep, cls, cond, sub_t, ypack, fac, tie_out, mid, tr, pack, sems):
     me_y = lax.axis_index("gy")
     sub_v, dep_v = sub[...], dep[...]
     top = film_top(cls[...])
@@ -237,33 +247,22 @@
     for z in range(64):
         tr[8 * z : 8 * z + 8] = cap[z] * u[z]
 
-    def turned(rows, dst, q):
-        block = jnp.transpose(rows)
-        for h in range(2):
-            dst[pl.ds(4 * h + q, 64, stride=8), :] = block[64 * h : 64 * h + 64]
-
-    subf = sub_v.astype(F32)
-    upper = (lax.broadcasted_iota(jnp.int32, (128, 128), 0) & 1) == 1
     for q in range(4):
         turned(cond[pl.ds(q, 128, stride=4), :], mid.at[0], q)
         turned(tr[pl.ds(q, 128, stride=4), :], mid.at[1], q)
-        turned(jnp.where(upper, subf[q + 4 : q + 5], subf[q : q + 1]), mid.at[2], q)
     z_lane = (lax.broadcasted_iota(jnp.int32, (8, 128), 1) >> 1).astype(F32)
     row = lax.broadcasted_iota(jnp.int32, (8, 128), 0)
     ky, sy, dy = [], [], []
     for y in range(64):
         ky.append(mid[0, 8 * y : 8 * y + 8])
         dy.append(mid[1, 8 * y : 8 * y + 8])
-        sy.append(jnp.where(z_lane < mid[2, 8 * y : 8 * y + 8], 1.0, 0.6))
+        sy.append(jnp.where(z_lane < sub_t[8 * y : 8 * y + 8], 1.0, 0.6))
     low = jnp.where(me_y == 0, R * SIDE, 0.0)
     high = jnp.where(me_y == 7, R * SIDE, 0.0)
     sy[0] = sy[0] + jnp.where(row < 4, low, 0.0)
     sy[63] = sy[63] + jnp.where(row >= 4, high, 0.0)
     cy = [R * jnp.minimum(ky[y], ky[y + 1]) for y in range(63)] + [None]
     g, q, levels, (p, zz, t), ties = reduce_chain(cy, sy, dy, True)
-    put_levels(fac, levels)
-    for lev in range(NLEV):
-        tie_out[lev] = ties[lev]
     kf, kl = ky[0], ky[63]
     side_a = tuple(v[0:4] for v in (kf, kl, zz, t, g, p, q))
     side_b = tuple(v[4:8] for v in (kf, kl, zz, t, g, p, q))
@@ -271,13 +270,49 @@
     for i, v in enumerate(saved):
         tie_out[NLEV + i, 0:4] = v
     lower = lax.broadcasted_iota(jnp.int32, (4, 128), 1) < 64
-    edges = jnp.where(lower, mid[2, 0:4], mid[2, 508:512])
-    pack = jnp.concatenate(list(merged) + [edges], axis=0)
-    for n in range(8):
-        ypack[n] = pack
-
-
-def second_kernel(gat, fac, ties, cond, sub, keep, send, xfac, xhfac, a2_out, kh_out, pick, flat, planes, xp):
+    edges = jnp.where(lower, sub_t[0:4], sub_t[508:512])
+    pack[...] = jnp.concatenate(list(merged) + [edges], axis=0)
+    copies = [pltpu.make_async_copy(pack, ypack.at[n], sems.at[n]) for n in range(8)]
+    for cp in copies:
+        cp.start()
+    put_levels(fac, levels)
+    for lev in range(NLEV):
+        tie_out[lev] = ties[lev]
+    for cp in copies:
+        cp.wait()
+
+
+def x_chain(k, cap, d):
+    low, high = wall_terms()
+    s = list(cap)
+    s[0] = s[0] + low
+    s[7] = s[7] + high
+    c = [R * jnp.minimum(k[x], k[x + 1]) for x in range(7)] + [None]
+    g, q, levels, (p, z, t), tie = reduce_chain(c, s, d, True)
+    return levels, tie, (k[0], k[7], z, t, g, p, q)
+
+
+def x_rows(half, cond, planes, subf, out, xfac):
+    base_z = lax.broadcasted_iota(jnp.int32, (8, 128), 0)
+    for chunk in range(4):
+        zi = base_z + (32 * half + 8 * chunk)
+        k, cap, d = [], [], []
+        for x in range(8):
+            at = pl.ds(256 * half + (64 * chunk + x), 8, stride=8)
+            k.append(cond[at, :])
+            cap.append(jnp.where(zi < subf[x : x + 1], 1.0, 0.6))
+            d.append(cap[x] * planes[at, :])
+        levels, tie, port = x_chain(k, cap, d)
+        store_x(xfac.at[chunk], levels, tie)
+        for i in range(2):
+            out[32 * i + 8 * chunk : 32 * i + 8 * chunk + 8] = port[5 + i]
+
+
+def keep_kernel(cond, planes, sub, keep, xfac):
+    x_rows(own_half(), cond, planes, sub[...], keep, xfac)
+
+
+def second_kernel(gat, fac, ties, cond, sub, send, edge, xfac, xhfac, kh_out, planes, pick, flat):
     me_y = lax.axis_index("gy")
     seg = [[gat[n, 4 * i : 4 * i + 4] for i in range(8)] for n in range(8)]
     gam, rhs = seg[0][4], seg[0][6]
@@ -346,36 +381,12 @@
     for x in range(8):
         kh_out[x : x + 1] = kh[x]
 
-    low, high = wall_terms()
-
-    def x_chain(k, cap, d):
-        s = list(cap)
-        s[0] = s[0] + low
-        s[7] = s[7] + high
-        c = [R * jnp.minimum(k[x], k[x + 1]) for x in range(7)] + [None]
-        g, q, levels, (p, z, t), tie = reduce_chain(c, s, d, True)
-        return levels, tie, (k[0], k[7], z, t, g, p, q)
-
-    base_z = lax.broadcasted_iota(jnp.int32, (8, 128), 0)
-    for chunk in range(8):
-        zi = base_z + 8 * chunk
-        k, cap, d = [], [], []
-        for x in range(8):
-            k.append(cond[pl.ds(64 * chunk + x, 8, stride=8), :])
-            cap.append(jnp.where(zi < subf[x : x + 1], 1.0, 0.6))
-            dx = cap[x] * planes[pl.ds(64 * chunk + x, 8, stride=8), :]
-            a2_out[pl.ds(64 * chunk + x, 8, stride=8), :] = dx
-            d.append(dx)
-        levels, tie, port = x_chain(k, cap, d)
-        store_x(xfac.at[chunk], levels, tie)
-        for i in range(2):
-            xp[i, 8 * chunk : 8 * chunk + 8] = port[5 + i]
     levels, tie, port = x_chain(kh, caph, dh)
     store_x(xhfac, levels, tie)
-    split_halves(xp, keep, send)
     for i in range(7):
-        keep[64 + i : 65 + i] = port[i]
         send[64 + i : 65 + i] = port[i]
+        edge[i : i + 1] = port[i]
+    x_rows(1 - own_half(), cond, planes, subf, send, xfac)
 
 
 def store_x(ref, levels, tie):
@@ -455,9 +466,10 @@
     return main, edge
 
 
-def core_kernel(mine, theirs, coefs, merged_out, saved_out):
+def core_kernel(mine, edge_mine, theirs, coefs, merged_out, saved_out):
     odd, _, _ = spots()
-    m, t = read_sides(mine), read_sides(theirs)
+    m = (mine[0:32], mine[32:64]), tuple(edge_mine[i : i + 1] for i in range(7))
+    t = read_sides(theirs)
     values, saved = port_values(planes_of(coefs, 7), *order(odd, m[0], t[0]))
     edge, edge_saved = merge_ports(*order(odd, m[1], t[1]))
     put_planes(merged_out, values)
@@ -521,7 +533,7 @@
     send[32:64] = final[0][3]
 
 
-def coef_kernel(cond, kh, a2, cot, sub, dep, cls, k_y, k_l, k_z, k_s, base):
+def coef_kernel(cond, kh, planes, cot, sub, dep, cls, k_y, k_l, k_z, k_s, base):
     me_y = lax.axis_index("gy")
     sub_v, dep_v, kh_v = sub[...], dep[...], kh[...]
     top = film_top(cls[...])
@@ -541,14 +553,15 @@
         film = film_y + top * (dep_v - 1 == z).astype(F32)
         if z == 0:
             film = film + BOTTOM
-        k_s[rows] = 2.0 * jnp.where(z < sub_v, 1.0, 0.6) - (2.0 * R) * film
-        base[rows] = cot[rows] - 2.0 * a2[rows]
-
-
-def expand_rows(xfac, half, flux, last, s1):
+        cap = jnp.where(z < sub_v, 1.0, 0.6)
+        k_s[rows] = 2.0 * cap - (2.0 * R) * film
+        base[rows] = cot[rows] - 2.0 * (cap * planes[rows])
+
+
+def expand_rows(xfac, flux, last, s1):
     for chunk in range(4):
         rows = slice(8 * chunk, 8 * chunk + 8)
-        levels, tie = load_x(xfac.at[4 * half + chunk])
+        levels, tie = load_x(xfac.at[chunk])
         u = expand_chain(last[rows], levels, tie, flux[rows])
         for x in range(8):
             s1[pl.ds(64 * chunk + x, 8, stride=8), :] = u[x]
@@ -584,7 +597,7 @@
     uh = jnp.concatenate(expand_chain(own[65:66], levels, tie, own[64:65]), axis=0)
     turned = pltpu.roll(uh, 64, 1)
     uh_out[...] = jnp.where(half == 1, uh, turned)
-    expand_rows(xfac, half, own.at[0:32], own.at[32:64], s1)
+    expand_rows(xfac, own.at[0:32], own.at[32:64], s1)
     uh = jnp.where(half == 1, turned, uh)
     stencil(half, uh, s1, k_y, k_l, k_z, k_s, base, sub[...], None, None, src, out)
 
@@ -604,7 +617,7 @@
 
     send(src_own, slice(0, 256), src_out, 256 * mine)
     send(out_own, slice(8, 248), temp_out, 256 * mine + 8)
-    expand_rows(xfac, half, got.at[0:32], got.at[32:64], s1)
+    expand_rows(xfac, got.at[0:32], got.at[32:64], s1)
     inner, outer = s_own[248:256], s_own[0:8]
     low = jnp.where(half == 0, s1[248:256], inner)
     high = jnp.where(half == 0, outer, s1[0:8])
@@ -654,9 +667,9 @@
     cot = cotangent.reshape(512, 128)
     temp = saved_temp.reshape(512, 128)
     small = jax.ShapeDtypeStruct((8, 128), jnp.int32)
-    cond, keep_m, send_m, cot, sub, dep, cls = call(
+    cond, keep_m, send_m, cot, sub, dep, cls, sub_t = call(
         fields_kernel,
-        [(512, 128), (160, 128), (160, 128), (512, 128), small, small, small],
+        [(512, 128), (160, 128), (160, 128), (512, 128), small, small, small, (512, 128)],
         [(512, 128), (5, 64, 128)],
         "fields",
         cot, temp, substrate_top, deposit_top, top_class,
@@ -666,22 +679,24 @@
     ypack, fac, ties = call(
         first_kernel,
         [(8, 32, 128), (3, 63, 8, 128), (12, 8, 128)],
-        [(3, 512, 128), (512, 128)],
+        [(2, 512, 128), (512, 128), (32, 128)],
         "first",
-        cot, sub, dep, cls, cond,
+        cot, sub, dep, cls, cond, sub_t,
+        far_out=1, sems=8,
     )
     mm, core_c = call(core_matrix_kernel, [(160, 128), (224, 128)], [], "matrix_core", keep_m, other_m)
     mm, ypack = lax.optimization_barrier((mm, ypack))
     gat = lax.all_to_all(ypack, "gy", split_axis=0, concat_axis=0, tiled=True)
     ring_m = [swap(mm, bit) for bit in (4, 7, 3)]
-    keep, send, xfac, xhfac, a2, kh = call(
+    send, edge, xfac, xhfac, kh, planes = call(
         second_kernel,
-        [(72, 128), (72, 128), (8, 24, 8, 128), (24, 1, 128), (512, 128), (8, 128)],
-        [(8, 32, 128), (512, 128), (512, 128), (2, 64, 128)],
+        [(72, 128), (8, 128), (4, 24, 8, 128), (24, 1, 128), (8, 128), (512, 128)],
+        [(8, 32, 128), (512, 128)],
         "second",
         gat, fac, ties, cond, sub,
     )
-    m1, sv1 = call(core_kernel, [(72, 128), (200, 128)], [], "merge_core", keep, swap(send, 1), core_c)
+    keep, xfac_own = call(keep_kernel, [(64, 128), (4, 24, 8, 128)], [], "keep_rows", cond, planes, sub)
+    m1, sv1 = call(core_kernel, [(72, 128), (200, 128)], [], "merge_core", keep, edge, swap(send, 1), core_c)
     ring_v = [swap(m1, bit) for bit in (4, 7, 3)]
     matrix, mine_c, other_c, ring_c, near_m = call(
         ring_matrix_kernel, [(160, 128)] + [(224, 128)] * 3 + [(64, 128)], [], "matrix_ring", mm, *ring_m
@@ -695,7 +710,7 @@
         m1, *ring_v, matrix, mine_c, other_c, ring_c,
     )
     sv3, kh = lax.optimization_barrier((sv3, kh))
-    coefs = call(coef_kernel, [(512, 128)] * 5, [], "coef", cond, kh, a2, cot, sub, dep, cls)
+    coefs = call(coef_kernel, [(512, 128)] * 5, [], "coef", cond, kh, planes, cot, sub, dep, cls)
     opposite = swap(near, 9)
     sv3, coefs = lax.optimization_barrier((sv3, coefs))
     own, out = call(top_kernel, [(72, 128), (64, 128)], [], "top", m3, near_m, near, opposite_m, opposite, sv1, sv2, sv3)
@@ -705,7 +720,7 @@
         [(256, 128), (256, 128), (256, 128), (8, 128)],
         [],
         "own_rows",
-        own, xfac, xhfac, *coefs, sub,
+        own, xfac_own, xhfac, *coefs, sub,
     )
     grad_temp, grad_source = call(
         last_kernel,

time: 34.5 us -> 34.3 us (level)
    pallas_call x11 -> x12, Pallas kernels: 4.77 us -> 4.73 us  [call(): pl.pallas_call(kernel, out_shape=shapes, in_specs=[HBM if i < far_in else...]
where the time goes in v11:
time: 34.3 us; the launch traced here: 34.1 us
  starting transfers between devices  23.8 us (69%)
  waiting for transfers between devices  4.82 us (14%)
  Pallas kernels  4.73 us (14%)
  between operations  0.71 us (2%)
    ppermute x11, starting transfers between devices, swap(): return lax.ppermute(v, 'gx', [(i, i ^ bit) for i in range(16)])  18.7 us
    all_to_all x1, starting transfers between devices, body(): gat = lax.all_to_all(ypack, 'gy', split_axis=0, concat_axis=0, tiled=True)  5.16 us
    pallas_call x12, Pallas kernels, call(): pl.pallas_call(kernel, out_shape=shapes, in_specs=[HBM if i < far_in else...  4.73 us
    ppermute x11, waiting for transfers between devices, swap(): return lax.ppermute(v, 'gx', [(i, i ^ bit) for i in range(16)])  4.23 us
  transfers between devices with their start and end apart: 12, of which 5 were waited for; matrix products, arithmetic and copies ran while one was open for 0% of the time, Pallas kernels for 7%

profile of v11, /device:TPU:1, one launch (start us, length us, event | category | flops | bytes accessed | tf_op | source)
XLA Modules:
  0.0 34.1 jit_solution(7339359743077934240)
XLA Ops:
  0.6 1.2 %fields.1 = (f32[512,128]{1,0:T(8,128)S(1)}, f32[160,128]{1,0:T(8,128)S(1)}, f32[160,128]{1,0:T(8,128)S(1)}, f32[512,128]{1,0:T(8,128)S(1)}, s32[8,128]{1,0:T(8,...) custom-call(f32[512,128]{1,0:T(8,128)} %bitcast.4, f32[512,128]{1,0:T(8,128)} %bitcast.5, ...), custom_call_target="tpu_custom_call" | custom-call | tf_op jit(solution)/shard_map/fields/pallas_call | solution.py:651
  1.8 1.5 %collective-permute-start = (f32[160,128]{1,0:T(8,128)S(1)}, f32[160,128]{1,0:T(8,128)S(1)}, u32[]{:S(2)}, u32[]{:S(2)}) collective-permute-start(f32[160,128]{1,0:T(8,128)S(1)} %get-tuple-element.59), channel_id=1, source_target_pairs={{0,8},{8,0},{16,24},{24,16},{32,40},{40,32},{48,56},{56,48},{64,72... | collective-permute-start | bytes 245768 | tf_op jit(solution)/shard_map/ppermute | solution.py:663
  3.3 1.3 %first.1 = (f32[8,32,128]{2,1,0:T(8,128)}, f32[3,63,8,128]{3,2,1,0:T(8,128)S(1)}, f32[12,8,128]{2,1,0:T(8,128)S(1)}) custom-call(f32[512,128]{1,0:T(8,128)S(1)} %get-tuple-element.61.cot, s32[8,128]{1,0:T(8,128)S(1)} %get-tuple-element.62.sub, s32[8,128]{1,0:T(8,128)S(1)} %get-tuple-element.63.dep, s32[8,128]{1,0:T(8,128)S(1)} %get-tuple-element.64.cls, ...), custom_call_target="tpu_custom_call" | custom-call | tf_op jit(solution)/shard_map/first/pallas_call | solution.py:651
  4.6 0.0 collective-permute-done.theirs
  4.6 5.2 %all-to-all-start = ((f32[8,32,128]{2,1,0:T(8,128)}), f32[8,32,128]{2,1,0:T(8,128)S(1)}, u32[]{:S(2)}, u32[]{:S(2)}) async-start(f32[8,32,128]{2,1,0:T(8,128)} %get-tuple-element.67), calls=%async_computation | async-start | bytes 262144 | tf_op jit(solution)/shard_map/all_to_all | solution.py:689
  9.8 3.6 %collective-permute-start.5 = (f32[160,128]{1,0:T(8,128)S(1)}, f32[160,128]{1,0:T(8,128)S(1)}, u32[]{:S(2)}, u32[]{:S(2)}) collective-permute-start(f32[160,128]{1,0:T(8,128)S(1)} %get-tuple-element.76.own), channel_id=1, source_target_pairs={{0,32},{8,40},{16,48},{24,56},{32,0},{40,8},{48,16},{56,24},{64,96... | collective-permute-start | bytes 245768 | tf_op jit(solution)/shard_map/ppermute | solution.py:663
  13.4 0.9 %collective-permute-start.6 = (f32[160,128]{1,0:T(8,128)S(1)}, f32[160,128]{1,0:T(8,128)S(1)}, u32[]{:S(2)}, u32[]{:S(2)}) collective-permute-start(f32[160,128]{1,0:T(8,128)S(1)} %get-tuple-element.76.own), channel_id=1, source_target_pairs={{0,56},{8,48},{16,40},{24,32},{32,24},{40,16},{48,8},{56,0},{64,12... | collective-permute-start | bytes 245768 | tf_op jit(solution)/shard_map/ppermute | solution.py:663
  14.3 0.3 collective-permute-start.7
  14.6 0.6 %all-to-all-done.gat = f32[8,32,128]{2,1,0:T(8,128)S(1)} async-done(((f32[8,32,128]{2,1,0:T(8,128)}), f32[8,32,128]{2,1,0:T(8,128)S(1)}, u32[]{:S(2)}, u32[]{:S(2)}) %all-to-all-start) | async-done | bytes 131104 | tf_op jit(solution)/shard_map/all_to_all | solution.py:689
  15.2 0.4 %second.1 = (f32[72,128]{1,0:T(8,128)S(1)}, f32[8,128]{1,0:T(8,128)S(1)}, f32[4,24,8,128]{3,2,1,0:T(8,128)S(1)}, f32[24,1,128]{2,1,0:T(1,128)S(1)}, f32[8,128]{1,0:T(8,128)S(1)}, /*index=5*/f32[512,128]{1,0:T(8,128)S(1)}) custom-call(f32[8,32,128]{2,1,0:T(8,128)S(1)} %all-to-all-done.gat, f32[3,63,8,128]{3,2,1,0:T(8,128)S(1)} %get-tuple-element.68.fac, ...), custom_call_target="tpu_custom_call" | custom-call | tf_op jit(solution)/shard_map/second/pallas_call | solution.py:651
  15.6 1.6 %collective-permute-start.1 = (f32[72,128]{1,0:T(8,128)S(1)}, f32[72,128]{1,0:T(8,128)S(1)}, u32[]{:S(2)}, u32[]{:S(2)}) collective-permute-start(f32[72,128]{1,0:T(8,128)S(1)} %get-tuple-element.73), channel_id=1, source_target_pairs={{0,8},{8,0},{16,24},{24,16},{32,40},{40,32},{48,56},{56,48},{64,72... | collective-permute-start | bytes 110600 | tf_op jit(solution)/shard_map/ppermute | solution.py:663
  17.1 0.1 keep_rows.1
  17.2 0.8 %collective-permute-done.1.theirs = f32[72,128]{1,0:T(8,128)S(1)} collective-permute-done((f32[72,128]{1,0:T(8,128)S(1)}, f32[72,128]{1,0:T(8,128)S(1)}, u32[]{:S(2)}, u32[]{:S(2)}) %collective-permute-start.1) | collective-permute-done | bytes 36896 | tf_op jit(solution)/shard_map/ppermute | solution.py:663
  18.0 3.7 %collective-permute-start.2 = (f32[72,128]{1,0:T(8,128)S(1)}, f32[72,128]{1,0:T(8,128)S(1)}, u32[]{:S(2)}, u32[]{:S(2)}) collective-permute-start(f32[72,128]{1,0:T(8,128)S(1)} %get-tuple-element.75.own), channel_id=1, source_target_pairs={{0,32},{8,40},{16,48},{24,56},{32,0},{40,8},{48,16},{56,24},{64,96... | collective-permute-start | bytes 110600 | tf_op jit(solution)/shard_map/ppermute | solution.py:663
  21.7 0.9 %collective-permute-start.3 = (f32[72,128]{1,0:T(8,128)S(1)}, f32[72,128]{1,0:T(8,128)S(1)}, u32[]{:S(2)}, u32[]{:S(2)}) collective-permute-start(f32[72,128]{1,0:T(8,128)S(1)} %get-tuple-element.75.own), channel_id=1, source_target_pairs={{0,56},{8,48},{16,40},{24,32},{32,24},{40,16},{48,8},{56,0},{64,12... | collective-permute-start | bytes 110600 | tf_op jit(solution)/shard_map/ppermute | solution.py:663
  22.7 0.0 collective-permute-done.5.mid
  22.7 0.3 collective-permute-start.4
  23.0 0.0 collective-permute-done.6.far
  23.0 0.0 collective-permute-done.7.near
  23.0 0.1 matrix_ring.1
  23.1 2.5 %collective-permute-start.8 = (f32[64,128]{1,0:T(8,128)S(1)}, f32[64,128]{1,0:T(8,128)S(1)}, u32[]{:S(2)}, u32[]{:S(2)}) collective-permute-start(f32[64,128]{1,0:T(8,128)S(1)} %get-tuple-element.82.near_m), channel_id=1, source_target_pairs={{0,72},{8,64},{16,88},{24,80},{32,104},{40,96},{48,120},{56,112},{... | collective-permute-start | bytes 98312 | tf_op jit(solution)/shard_map/ppermute | solution.py:663
  25.5 0.0 collective-permute-done.2.mid
  25.5 1.3 %collective-permute-done.3.far = f32[72,128]{1,0:T(8,128)S(1)} collective-permute-done((f32[72,128]{1,0:T(8,128)S(1)}, f32[72,128]{1,0:T(8,128)S(1)}, u32[]{:S(2)}, u32[]{:S(2)}) %collective-permute-start.3) | collective-permute-done | bytes 36896 | tf_op jit(solution)/shard_map/ppermute | solution.py:663
  26.9 0.1 merge_ring.1
  26.9 3.0 %collective-permute-start.9 = (f32[40,128]{1,0:T(8,128)S(1)}, f32[40,128]{1,0:T(8,128)S(1)}, u32[]{:S(2)}, u32[]{:S(2)}) collective-permute-start(f32[40,128]{1,0:T(8,128)S(1)} %get-tuple-element.83.near), channel_id=1, source_target_pairs={{0,72},{8,64},{16,88},{24,80},{32,104},{40,96},{48,120},{56,112},{... | collective-permute-start | bytes 61448 | tf_op jit(solution)/shard_map/ppermute | solution.py:663
  29.9 0.3 coef.1
  30.2 1.5 %collective-permute-done.9.theirs = f32[40,128]{1,0:T(8,128)S(1)} collective-permute-done((f32[40,128]{1,0:T(8,128)S(1)}, f32[40,128]{1,0:T(8,128)S(1)}, u32[]{:S(2)}, u32[]{:S(2)}) %collective-permute-start.9) | collective-permute-done | bytes 20512 | tf_op jit(solution)/shard_map/ppermute | solution.py:663
  31.7 0.1 top.1
  31.8 0.5 %collective-permute-start.10 = (f32[64,128]{1,0:T(8,128)S(1)}, f32[64,128]{1,0:T(8,128)S(1)}, u32[]{:S(2)}, u32[]{:S(2)}) collective-permute-start(f32[64,128]{1,0:T(8,128)S(1)} %get-tuple-element.96), channel_id=1, source_target_pairs={{0,8},{8,0},{16,24},{24,16},{32,40},{40,32},{48,56},{56,48},{64,72... | collective-permute-start | bytes 98312 | tf_op jit(solution)/shard_map/ppermute | solution.py:663
  32.3 0.3 own_rows.1
  32.6 0.6 %collective-permute-done.10.got = f32[64,128]{1,0:T(8,128)S(1)} collective-permute-done((f32[64,128]{1,0:T(8,128)S(1)}, f32[64,128]{1,0:T(8,128)S(1)}, u32[]{:S(2)}, u32[]{:S(2)}) %collective-permute-start.10) | collective-permute-done | bytes 32800 | tf_op jit(solution)/shard_map/ppermute | solution.py:663
  33.1 1.0 %last.1 = (f32[512,128]{1,0:T(8,128)}, f32[512,128]{1,0:T(8,128)}) custom-call(f32[64,128]{1,0:T(8,128)S(1)} %collective-permute-done.10.got, f32[4,24,8,128]{3,2,1,0:T(8,128)S(1)} %get-tuple-element.97.xfac, f32[512,128]{1,0:T(8,128)S(1)} %get-tuple-element.98.k_y, f32[512,128]{1,0:T(8,128)S(1)} %get-tuple-element.99.k_l, ...), custom_call_target="tpu_custom_call" | custom-call | tf_op jit(solution)/shard_map/last/pallas_call | solution.py:651
  (4 shorter events, 0.1 us)
Async XLA Ops:
  1.8 2.7 %collective-permute-start = (f32[160,128]{1,0:T(8,128)S(1)}, f32[160,128]{1,0:T(8,128)S(1)}, u32[]{:S(2)}, u32[]{:S(2)}) collective-permute-start(f32[160,128]{1,0:T(8,128)S(1)} %get-tuple-element.59), channel_id=1, source_target_pairs={{0,8},{8,0},{16,24},{24,16},{32,40},{40,32},{48,56},{56,48},{64,72... | collective-permute-start | bytes 245768 | tf_op jit(solution)/shard_map/ppermute | solution.py:663
  4.6 10.5 %all-to-all-start = ((f32[8,32,128]{2,1,0:T(8,128)}), f32[8,32,128]{2,1,0:T(8,128)S(1)}, u32[]{:S(2)}, u32[]{:S(2)}) async-start(f32[8,32,128]{2,1,0:T(8,128)} %get-tuple-element.67), calls=%async_computation | async-start | bytes 262144 | tf_op jit(solution)/shard_map/all_to_all | solution.py:689
  9.8 12.9 %collective-permute-start.5 = (f32[160,128]{1,0:T(8,128)S(1)}, f32[160,128]{1,0:T(8,128)S(1)}, u32[]{:S(2)}, u32[]{:S(2)}) collective-permute-start(f32[160,128]{1,0:T(8,128)S(1)} %get-tuple-element.76.own), channel_id=1, source_target_pairs={{0,32},{8,40},{16,48},{24,56},{32,0},{40,8},{48,16},{56,24},{64,96... | collective-permute-start | bytes 245768 | tf_op jit(solution)/shard_map/ppermute | solution.py:663
  13.4 9.6 %collective-permute-start.6 = (f32[160,128]{1,0:T(8,128)S(1)}, f32[160,128]{1,0:T(8,128)S(1)}, u32[]{:S(2)}, u32[]{:S(2)}) collective-permute-start(f32[160,128]{1,0:T(8,128)S(1)} %get-tuple-element.76.own), channel_id=1, source_target_pairs={{0,56},{8,48},{16,40},{24,32},{32,24},{40,16},{48,8},{56,0},{64,12... | collective-permute-start | bytes 245768 | tf_op jit(solution)/shard_map/ppermute | solution.py:663
  14.3 8.7 %collective-permute-start.7 = (f32[160,128]{1,0:T(8,128)S(1)}, f32[160,128]{1,0:T(8,128)S(1)}, u32[]{:S(2)}, u32[]{:S(2)}) collective-permute-start(f32[160,128]{1,0:T(8,128)S(1)} %get-tuple-element.76.own), channel_id=1, source_target_pairs={{0,24},{8,16},{16,8},{24,0},{32,56},{40,48},{48,40},{56,32},{64,88... | collective-permute-start | bytes 245768 | tf_op jit(solution)/shard_map/ppermute | solution.py:663
  15.6 2.4 %collective-permute-start.1 = (f32[72,128]{1,0:T(8,128)S(1)}, f32[72,128]{1,0:T(8,128)S(1)}, u32[]{:S(2)}, u32[]{:S(2)}) collective-permute-start(f32[72,128]{1,0:T(8,128)S(1)} %get-tuple-element.73), channel_id=1, source_target_pairs={{0,8},{8,0},{16,24},{24,16},{32,40},{40,32},{48,56},{56,48},{64,72... | collective-permute-start | bytes 110600 | tf_op jit(solution)/shard_map/ppermute | solution.py:663
  18.0 7.5 %collective-permute-start.2 = (f32[72,128]{1,0:T(8,128)S(1)}, f32[72,128]{1,0:T(8,128)S(1)}, u32[]{:S(2)}, u32[]{:S(2)}) collective-permute-start(f32[72,128]{1,0:T(8,128)S(1)} %get-tuple-element.75.own), channel_id=1, source_target_pairs={{0,32},{8,40},{16,48},{24,56},{32,0},{40,8},{48,16},{56,24},{64,96... | collective-permute-start | bytes 110600 | tf_op jit(solution)/shard_map/ppermute | solution.py:663
  21.7 5.2 %collective-permute-start.3 = (f32[72,128]{1,0:T(8,128)S(1)}, f32[72,128]{1,0:T(8,128)S(1)}, u32[]{:S(2)}, u32[]{:S(2)}) collective-permute-start(f32[72,128]{1,0:T(8,128)S(1)} %get-tuple-element.75.own), channel_id=1, source_target_pairs={{0,56},{8,48},{16,40},{24,32},{32,24},{40,16},{48,8},{56,0},{64,12... | collective-permute-start | bytes 110600 | tf_op jit(solution)/shard_map/ppermute | solution.py:663
  22.7 4.2 %collective-permute-start.4 = (f32[72,128]{1,0:T(8,128)S(1)}, f32[72,128]{1,0:T(8,128)S(1)}, u32[]{:S(2)}, u32[]{:S(2)}) collective-permute-start(f32[72,128]{1,0:T(8,128)S(1)} %get-tuple-element.75.own), channel_id=1, source_target_pairs={{0,24},{8,16},{16,8},{24,0},{32,56},{40,48},{48,40},{56,32},{64,88... | collective-permute-start | bytes 110600 | tf_op jit(solution)/shard_map/ppermute | solution.py:663
  23.1 7.1 %collective-permute-start.8 = (f32[64,128]{1,0:T(8,128)S(1)}, f32[64,128]{1,0:T(8,128)S(1)}, u32[]{:S(2)}, u32[]{:S(2)}) collective-permute-start(f32[64,128]{1,0:T(8,128)S(1)} %get-tuple-element.82.near_m), channel_id=1, source_target_pairs={{0,72},{8,64},{16,88},{24,80},{32,104},{40,96},{48,120},{56,112},{... | collective-permute-start | bytes 98312 | tf_op jit(solution)/shard_map/ppermute | solution.py:663
  26.9 4.8 %collective-permute-start.9 = (f32[40,128]{1,0:T(8,128)S(1)}, f32[40,128]{1,0:T(8,128)S(1)}, u32[]{:S(2)}, u32[]{:S(2)}) collective-permute-start(f32[40,128]{1,0:T(8,128)S(1)} %get-tuple-element.83.near), channel_id=1, source_target_pairs={{0,72},{8,64},{16,88},{24,80},{32,104},{40,96},{48,120},{56,112},{... | collective-permute-start | bytes 61448 | tf_op jit(solution)/shard_map/ppermute | solution.py:663
  31.8 1.3 %collective-permute-start.10 = (f32[64,128]{1,0:T(8,128)S(1)}, f32[64,128]{1,0:T(8,128)S(1)}, u32[]{:S(2)}, u32[]{:S(2)}) collective-permute-start(f32[64,128]{1,0:T(8,128)S(1)} %get-tuple-element.96), channel_id=1, source_target_pairs={{0,8},{8,0},{16,24},{24,16},{32,40},{40,32},{48,56},{56,48},{64,72... | collective-permute-start | bytes 98312 | tf_op jit(solution)/shard_map/ppermute | solution.py:663

commit v12 on v11

--- a/solution.py
+++ b/solution.py
@@ -186,13 +186,7 @@
         send[32 * i : 32 * i + 32] = planes[i, pl.ds(pl.multiple_of(32 - 32 * core, 32), 32), :]
 
 
-def turned(rows, dst, q):
-    block = jnp.transpose(rows)
-    for h in range(2):
-        dst[pl.ds(4 * h + q, 64, stride=8), :] = block[64 * h : 64 * h + 64]
-
-
-def fields_kernel(cot_in, temp_in, sub_in, dep_in, cls_in, cond, keep, send, cot, sub, dep, cls, sub_t, temp, planes, sems):
+def fields_kernel(cot_in, temp_in, sub_in, dep_in, cls_in, cond, keep, send, cot, sub, dep, cls, temp, planes, sems):
     pieces = [slice(128 * i, 128 * i + 128) for i in range(4)]
     pairs = [(sub_in, sub), (dep_in, dep)] + [(temp_in.at[r], temp.at[r]) for r in pieces]
     pairs += [(cls_in, cls), (cot_in, cot)]
@@ -202,10 +196,6 @@
     for cp in copies[:2]:
         cp.wait()
     sub_v, dep_v = sub[...], dep[...]
-    subf = sub_v.astype(F32)
-    upper = (lax.broadcasted_iota(jnp.int32, (128, 128), 0) & 1) == 1
-    for q in range(4):
-        turned(jnp.where(upper, subf[q + 4 : q + 5], subf[q : q + 1]), sub_t, q)
     for z in range(64):
         if z % 16 == 0:
             copies[2 + z // 16].wait()
@@ -228,7 +218,7 @@
         cp.wait()
 
 
-def first_kernel(cot, sub, dep, cls, cond, sub_t, ypack, fac, tie_out, mid, tr, pack, sems):
+def first_kernel(cot, sub, dep, cls, cond, ypack, fac, tie_out, mid, tr):
     me_y = lax.axis_index("gy")
     sub_v, dep_v = sub[...], dep[...]
     top = film_top(cls[...])
@@ -247,22 +237,33 @@
     for z in range(64):
         tr[8 * z : 8 * z + 8] = cap[z] * u[z]
 
+    def turned(rows, dst, q):
+        block = jnp.transpose(rows)
+        for h in range(2):
+            dst[pl.ds(4 * h + q, 64, stride=8), :] = block[64 * h : 64 * h + 64]
+
+    subf = sub_v.astype(F32)
+    upper = (lax.broadcasted_iota(jnp.int32, (128, 128), 0) & 1) == 1
     for q in range(4):
         turned(cond[pl.ds(q, 128, stride=4), :], mid.at[0], q)
         turned(tr[pl.ds(q, 128, stride=4), :], mid.at[1], q)
+        turned(jnp.where(upper, subf[q + 4 : q + 5], subf[q : q + 1]), mid.at[2], q)
     z_lane = (lax.broadcasted_iota(jnp.int32, (8, 128), 1) >> 1).astype(F32)
     row = lax.broadcasted_iota(jnp.int32, (8, 128), 0)
     ky, sy, dy = [], [], []
     for y in range(64):
         ky.append(mid[0, 8 * y : 8 * y + 8])
         dy.append(mid[1, 8 * y : 8 * y + 8])
-        sy.append(jnp.where(z_lane < sub_t[8 * y : 8 * y + 8], 1.0, 0.6))
+        sy.append(jnp.where(z_lane < mid[2, 8 * y : 8 * y + 8], 1.0, 0.6))
     low = jnp.where(me_y == 0, R * SIDE, 0.0)
     high = jnp.where(me_y == 7, R * SIDE, 0.0)
     sy[0] = sy[0] + jnp.where(row < 4, low, 0.0)
     sy[63] = sy[63] + jnp.where(row >= 4, high, 0.0)
     cy = [R * jnp.minimum(ky[y], ky[y + 1]) for y in range(63)] + [None]
     g, q, levels, (p, zz, t), ties = reduce_chain(cy, sy, dy, True)
+    put_levels(fac, levels)
+    for lev in range(NLEV):
+        tie_out[lev] = ties[lev]
     kf, kl = ky[0], ky[63]
     side_a = tuple(v[0:4] for v in (kf, kl, zz, t, g, p, q))
     side_b = tuple(v[4:8] for v in (kf, kl, zz, t, g, p, q))
@@ -270,16 +271,10 @@
     for i, v in enumerate(saved):
         tie_out[NLEV + i, 0:4] = v
     lower = lax.broadcasted_iota(jnp.int32, (4, 128), 1) < 64
-    edges = jnp.where(lower, sub_t[0:4], sub_t[508:512])
-    pack[...] = jnp.concatenate(list(merged) + [edges], axis=0)
-    copies = [pltpu.make_async_copy(pack, ypack.at[n], sems.at[n]) for n in range(8)]
-    for cp in copies:
-        cp.start()
-    put_levels(fac, levels)
-    for lev in range(NLEV):
-        tie_out[lev] = ties[lev]
-    for cp in copies:
-        cp.wait()
+    edges = jnp.where(lower, mid[2, 0:4], mid[2, 508:512])
+    pack = jnp.concatenate(list(merged) + [edges], axis=0)
+    for n in range(8):
+        ypack[n] = pack
 
 
 def x_chain(k, cap, d):
@@ -667,9 +662,9 @@
     cot = cotangent.reshape(512, 128)
     temp = saved_temp.reshape(512, 128)
     small = jax.ShapeDtypeStruct((8, 128), jnp.int32)
-    cond, keep_m, send_m, cot, sub, dep, cls, sub_t = call(
+    cond, keep_m, send_m, cot, sub, dep, cls = call(
         fields_kernel,
-        [(512, 128), (160, 128), (160, 128), (512, 128), small, small, small, (512, 128)],
+        [(512, 128), (160, 128), (160, 128), (512, 128), small, small, small],
         [(512, 128), (5, 64, 128)],
         "fields",
         cot, temp, substrate_top, deposit_top, top_class,
@@ -679,10 +674,9 @@
     ypack, fac, ties = call(
         first_kernel,
         [(8, 32, 128), (3, 63, 8, 128), (12, 8, 128)],
-        [(2, 512, 128), (512, 128), (32, 128)],
+        [(3, 512, 128), (512, 128)],
         "first",
-        cot, sub, dep, cls, cond, sub_t,
-        far_out=1, sems=8,
+        cot, sub, dep, cls, cond,
     )
     mm, core_c = call(core_matrix_kernel, [(160, 128), (224, 128)], [], "matrix_core", keep_m, other_m)
     mm, ypack = lax.optimization_barrier((mm, ypack))

time: 34.3 us -> 34.3 us (level)
  no operation moved by 1% of the time
where the time goes in v12:
time: 34.3 us; the launch traced here: 34.1 us
  starting transfers between devices  23.8 us (69%)
  waiting for transfers between devices  4.82 us (14%)
  Pallas kernels  4.75 us (14%)
  between operations  0.7 us (2%)
    ppermute x11, starting transfers between devices, swap(): return lax.ppermute(v, 'gx', [(i, i ^ bit) for i in range(16)])  18.7 us
    all_to_all x1, starting transfers between devices, body(): gat = lax.all_to_all(ypack, 'gy', split_axis=0, concat_axis=0, tiled=True)  5.16 us
    pallas_call x12, Pallas kernels, call(): pl.pallas_call(kernel, out_shape=shapes, in_specs=[HBM if i < far_in else...  4.75 us
    ppermute x11, waiting for transfers between devices, swap(): return lax.ppermute(v, 'gx', [(i, i ^ bit) for i in range(16)])  4.23 us
  transfers between devices with their start and end apart: 12, of which 5 were waited for; matrix products, arithmetic and copies ran while one was open for 0% of the time, Pallas kernels for 7%

profile of v12, /device:TPU:1, one launch (start us, length us, event | category | flops | bytes accessed | tf_op | source)
XLA Modules:
  0.0 34.1 jit_solution(17022593696908778730)
XLA Ops:
  0.6 1.2 %fields.1 = (f32[512,128]{1,0:T(8,128)S(1)}, f32[160,128]{1,0:T(8,128)S(1)}, f32[160,128]{1,0:T(8,128)S(1)}, f32[512,128]{1,0:T(8,128)S(1)}, s32[8,128]{1,0:T(8,...) custom-call(f32[512,128]{1,0:T(8,128)} %bitcast.4, f32[512,128]{1,0:T(8,128)} %bitcast.5, s32[8,128]{1,0:T(8,128)} %sub_in.1, ...), custom_call_target="tpu_custom_call" | custom-call | tf_op jit(solution)/shard_map/fields/pallas_call | solution.py:646
  1.8 1.5 %collective-permute-start = (f32[160,128]{1,0:T(8,128)S(1)}, f32[160,128]{1,0:T(8,128)S(1)}, u32[]{:S(2)}, u32[]{:S(2)}) collective-permute-start(f32[160,128]{1,0:T(8,128)S(1)} %get-tuple-element.58), channel_id=1, source_target_pairs={{0,8},{8,0},{16,24},{24,16},{32,40},{40,32},{48,56},{56,48},{64,72... | collective-permute-start | bytes 245768 | tf_op jit(solution)/shard_map/ppermute | solution.py:658
  3.3 1.3 %first.1 = (f32[8,32,128]{2,1,0:T(8,128)}, f32[3,63,8,128]{3,2,1,0:T(8,128)S(1)}, f32[12,8,128]{2,1,0:T(8,128)S(1)}) custom-call(f32[512,128]{1,0:T(8,128)S(1)} %get-tuple-element.60.cot, s32[8,128]{1,0:T(8,128)S(1)} %get-tuple-element.61.sub, s32[8,128]{1,0:T(8,128)S(1)} %get-tuple-element.62.dep, s32[8,128]{1,0:T(8,128)S(1)} %get-tuple-element.63.cls, ...), custom_call_target="tpu_custom_call" | custom-call | tf_op jit(solution)/shard_map/first/pallas_call | solution.py:646
  4.6 0.0 collective-permute-done.theirs
  4.6 5.2 %all-to-all-start = ((f32[8,32,128]{2,1,0:T(8,128)}), f32[8,32,128]{2,1,0:T(8,128)S(1)}, u32[]{:S(2)}, u32[]{:S(2)}) async-start(f32[8,32,128]{2,1,0:T(8,128)} %get-tuple-element.65), calls=%async_computation | async-start | bytes 262144 | tf_op jit(solution)/shard_map/all_to_all | solution.py:683
  9.8 3.6 %collective-permute-start.5 = (f32[160,128]{1,0:T(8,128)S(1)}, f32[160,128]{1,0:T(8,128)S(1)}, u32[]{:S(2)}, u32[]{:S(2)}) collective-permute-start(f32[160,128]{1,0:T(8,128)S(1)} %get-tuple-element.74.own), channel_id=1, source_target_pairs={{0,32},{8,40},{16,48},{24,56},{32,0},{40,8},{48,16},{56,24},{64,96... | collective-permute-start | bytes 245768 | tf_op jit(solution)/shard_map/ppermute | solution.py:658
  13.4 0.9 %collective-permute-start.6 = (f32[160,128]{1,0:T(8,128)S(1)}, f32[160,128]{1,0:T(8,128)S(1)}, u32[]{:S(2)}, u32[]{:S(2)}) collective-permute-start(f32[160,128]{1,0:T(8,128)S(1)} %get-tuple-element.74.own), channel_id=1, source_target_pairs={{0,56},{8,48},{16,40},{24,32},{32,24},{40,16},{48,8},{56,0},{64,12... | collective-permute-start | bytes 245768 | tf_op jit(solution)/shard_map/ppermute | solution.py:658
  14.3 0.3 collective-permute-start.7
  14.6 0.6 %all-to-all-done.gat = f32[8,32,128]{2,1,0:T(8,128)S(1)} async-done(((f32[8,32,128]{2,1,0:T(8,128)}), f32[8,32,128]{2,1,0:T(8,128)S(1)}, u32[]{:S(2)}, u32[]{:S(2)}) %all-to-all-start) | async-done | bytes 131104 | tf_op jit(solution)/shard_map/all_to_all | solution.py:683
  15.2 0.4 %second.1 = (f32[72,128]{1,0:T(8,128)S(1)}, f32[8,128]{1,0:T(8,128)S(1)}, f32[4,24,8,128]{3,2,1,0:T(8,128)S(1)}, f32[24,1,128]{2,1,0:T(1,128)S(1)}, f32[8,128]{1,0:T(8,128)S(1)}, /*index=5*/f32[512,128]{1,0:T(8,128)S(1)}) custom-call(f32[8,32,128]{2,1,0:T(8,128)S(1)} %all-to-all-done.gat, f32[3,63,8,128]{3,2,1,0:T(8,128)S(1)} %get-tuple-element.66.fac, ...), custom_call_target="tpu_custom_call" | custom-call | tf_op jit(solution)/shard_map/second/pallas_call | solution.py:646
  15.6 1.6 %collective-permute-start.1 = (f32[72,128]{1,0:T(8,128)S(1)}, f32[72,128]{1,0:T(8,128)S(1)}, u32[]{:S(2)}, u32[]{:S(2)}) collective-permute-start(f32[72,128]{1,0:T(8,128)S(1)} %get-tuple-element.71), channel_id=1, source_target_pairs={{0,8},{8,0},{16,24},{24,16},{32,40},{40,32},{48,56},{56,48},{64,72... | collective-permute-start | bytes 110600 | tf_op jit(solution)/shard_map/ppermute | solution.py:658
  17.1 0.1 keep_rows.1
  17.2 0.8 %collective-permute-done.1.theirs = f32[72,128]{1,0:T(8,128)S(1)} collective-permute-done((f32[72,128]{1,0:T(8,128)S(1)}, f32[72,128]{1,0:T(8,128)S(1)}, u32[]{:S(2)}, u32[]{:S(2)}) %collective-permute-start.1) | collective-permute-done | bytes 36896 | tf_op jit(solution)/shard_map/ppermute | solution.py:658
  18.0 3.7 %collective-permute-start.2 = (f32[72,128]{1,0:T(8,128)S(1)}, f32[72,128]{1,0:T(8,128)S(1)}, u32[]{:S(2)}, u32[]{:S(2)}) collective-permute-start(f32[72,128]{1,0:T(8,128)S(1)} %get-tuple-element.73.own), channel_id=1, source_target_pairs={{0,32},{8,40},{16,48},{24,56},{32,0},{40,8},{48,16},{56,24},{64,96... | collective-permute-start | bytes 110600 | tf_op jit(solution)/shard_map/ppermute | solution.py:658
  21.7 0.9 %collective-permute-start.3 = (f32[72,128]{1,0:T(8,128)S(1)}, f32[72,128]{1,0:T(8,128)S(1)}, u32[]{:S(2)}, u32[]{:S(2)}) collective-permute-start(f32[72,128]{1,0:T(8,128)S(1)} %get-tuple-element.73.own), channel_id=1, source_target_pairs={{0,56},{8,48},{16,40},{24,32},{32,24},{40,16},{48,8},{56,0},{64,12... | collective-permute-start | bytes 110600 | tf_op jit(solution)/shard_map/ppermute | solution.py:658
  22.7 0.3 collective-permute-start.4
  23.0 0.0 collective-permute-done.6.far
  23.0 0.0 collective-permute-done.7.near
  23.0 0.1 matrix_ring.1
  23.1 2.5 %collective-permute-start.8 = (f32[64,128]{1,0:T(8,128)S(1)}, f32[64,128]{1,0:T(8,128)S(1)}, u32[]{:S(2)}, u32[]{:S(2)}) collective-permute-start(f32[64,128]{1,0:T(8,128)S(1)} %get-tuple-element.80.near_m), channel_id=1, source_target_pairs={{0,72},{8,64},{16,88},{24,80},{32,104},{40,96},{48,120},{56,112},{... | collective-permute-start | bytes 98312 | tf_op jit(solution)/shard_map/ppermute | solution.py:658
  25.5 0.0 collective-permute-done.2.mid
  25.5 1.3 %collective-permute-done.3.far = f32[72,128]{1,0:T(8,128)S(1)} collective-permute-done((f32[72,128]{1,0:T(8,128)S(1)}, f32[72,128]{1,0:T(8,128)S(1)}, u32[]{:S(2)}, u32[]{:S(2)}) %collective-permute-start.3) | collective-permute-done | bytes 36896 | tf_op jit(solution)/shard_map/ppermute | solution.py:658
  26.9 0.0 collective-permute-done.4.near
  26.9 0.1 merge_ring.1
  27.0 3.0 %collective-permute-start.9 = (f32[40,128]{1,0:T(8,128)S(1)}, f32[40,128]{1,0:T(8,128)S(1)}, u32[]{:S(2)}, u32[]{:S(2)}) collective-permute-start(f32[40,128]{1,0:T(8,128)S(1)} %get-tuple-element.81.near), channel_id=1, source_target_pairs={{0,72},{8,64},{16,88},{24,80},{32,104},{40,96},{48,120},{56,112},{... | collective-permute-start | bytes 61448 | tf_op jit(solution)/shard_map/ppermute | solution.py:658
  29.9 0.3 coef.1
  30.2 1.5 %collective-permute-done.9.theirs = f32[40,128]{1,0:T(8,128)S(1)} collective-permute-done((f32[40,128]{1,0:T(8,128)S(1)}, f32[40,128]{1,0:T(8,128)S(1)}, u32[]{:S(2)}, u32[]{:S(2)}) %collective-permute-start.9) | collective-permute-done | bytes 20512 | tf_op jit(solution)/shard_map/ppermute | solution.py:658
  31.7 0.1 top.1
  31.8 0.5 %collective-permute-start.10 = (f32[64,128]{1,0:T(8,128)S(1)}, f32[64,128]{1,0:T(8,128)S(1)}, u32[]{:S(2)}, u32[]{:S(2)}) collective-permute-start(f32[64,128]{1,0:T(8,128)S(1)} %get-tuple-element.94), channel_id=1, source_target_pairs={{0,8},{8,0},{16,24},{24,16},{32,40},{40,32},{48,56},{56,48},{64,72... | collective-permute-start | bytes 98312 | tf_op jit(solution)/shard_map/ppermute | solution.py:658
  32.3 0.3 own_rows.1
  32.6 0.6 %collective-permute-done.10.got = f32[64,128]{1,0:T(8,128)S(1)} collective-permute-done((f32[64,128]{1,0:T(8,128)S(1)}, f32[64,128]{1,0:T(8,128)S(1)}, u32[]{:S(2)}, u32[]{:S(2)}) %collective-permute-start.10) | collective-permute-done | bytes 32800 | tf_op jit(solution)/shard_map/ppermute | solution.py:658
  33.1 1.0 %last.1 = (f32[512,128]{1,0:T(8,128)}, f32[512,128]{1,0:T(8,128)}) custom-call(f32[64,128]{1,0:T(8,128)S(1)} %collective-permute-done.10.got, f32[4,24,8,128]{3,2,1,0:T(8,128)S(1)} %get-tuple-element.95.xfac, f32[512,128]{1,0:T(8,128)S(1)} %get-tuple-element.96.k_y, f32[512,128]{1,0:T(8,128)S(1)} %get-tuple-element.97.k_l, ...), custom_call_target="tpu_custom_call" | custom-call | tf_op jit(solution)/shard_map/last/pallas_call | solution.py:646
  (4 shorter events, 0.1 us)
Async XLA Ops:
  1.8 2.8 %collective-permute-start = (f32[160,128]{1,0:T(8,128)S(1)}, f32[160,128]{1,0:T(8,128)S(1)}, u32[]{:S(2)}, u32[]{:S(2)}) collective-permute-start(f32[160,128]{1,0:T(8,128)S(1)} %get-tuple-element.58), channel_id=1, source_target_pairs={{0,8},{8,0},{16,24},{24,16},{32,40},{40,32},{48,56},{56,48},{64,72... | collective-permute-start | bytes 245768 | tf_op jit(solution)/shard_map/ppermute | solution.py:658
  4.6 10.5 %all-to-all-start = ((f32[8,32,128]{2,1,0:T(8,128)}), f32[8,32,128]{2,1,0:T(8,128)S(1)}, u32[]{:S(2)}, u32[]{:S(2)}) async-start(f32[8,32,128]{2,1,0:T(8,128)} %get-tuple-element.65), calls=%async_computation | async-start | bytes 262144 | tf_op jit(solution)/shard_map/all_to_all | solution.py:683
  9.8 12.9 %collective-permute-start.5 = (f32[160,128]{1,0:T(8,128)S(1)}, f32[160,128]{1,0:T(8,128)S(1)}, u32[]{:S(2)}, u32[]{:S(2)}) collective-permute-start(f32[160,128]{1,0:T(8,128)S(1)} %get-tuple-element.74.own), channel_id=1, source_target_pairs={{0,32},{8,40},{16,48},{24,56},{32,0},{40,8},{48,16},{56,24},{64,96... | collective-permute-start | bytes 245768 | tf_op jit(solution)/shard_map/ppermute | solution.py:658
  13.4 9.6 %collective-permute-start.6 = (f32[160,128]{1,0:T(8,128)S(1)}, f32[160,128]{1,0:T(8,128)S(1)}, u32[]{:S(2)}, u32[]{:S(2)}) collective-permute-start(f32[160,128]{1,0:T(8,128)S(1)} %get-tuple-element.74.own), channel_id=1, source_target_pairs={{0,56},{8,48},{16,40},{24,32},{32,24},{40,16},{48,8},{56,0},{64,12... | collective-permute-start | bytes 245768 | tf_op jit(solution)/shard_map/ppermute | solution.py:658
  14.3 8.7 %collective-permute-start.7 = (f32[160,128]{1,0:T(8,128)S(1)}, f32[160,128]{1,0:T(8,128)S(1)}, u32[]{:S(2)}, u32[]{:S(2)}) collective-permute-start(f32[160,128]{1,0:T(8,128)S(1)} %get-tuple-element.74.own), channel_id=1, source_target_pairs={{0,24},{8,16},{16,8},{24,0},{32,56},{40,48},{48,40},{56,32},{64,88... | collective-permute-start | bytes 245768 | tf_op jit(solution)/shard_map/ppermute | solution.py:658
  15.6 2.4 %collective-permute-start.1 = (f32[72,128]{1,0:T(8,128)S(1)}, f32[72,128]{1,0:T(8,128)S(1)}, u32[]{:S(2)}, u32[]{:S(2)}) collective-permute-start(f32[72,128]{1,0:T(8,128)S(1)} %get-tuple-element.71), channel_id=1, source_target_pairs={{0,8},{8,0},{16,24},{24,16},{32,40},{40,32},{48,56},{56,48},{64,72... | collective-permute-start | bytes 110600 | tf_op jit(solution)/shard_map/ppermute | solution.py:658
  18.0 7.5 %collective-permute-start.2 = (f32[72,128]{1,0:T(8,128)S(1)}, f32[72,128]{1,0:T(8,128)S(1)}, u32[]{:S(2)}, u32[]{:S(2)}) collective-permute-start(f32[72,128]{1,0:T(8,128)S(1)} %get-tuple-element.73.own), channel_id=1, source_target_pairs={{0,32},{8,40},{16,48},{24,56},{32,0},{40,8},{48,16},{56,24},{64,96... | collective-permute-start | bytes 110600 | tf_op jit(solution)/shard_map/ppermute | solution.py:658
  21.7 5.2 %collective-permute-start.3 = (f32[72,128]{1,0:T(8,128)S(1)}, f32[72,128]{1,0:T(8,128)S(1)}, u32[]{:S(2)}, u32[]{:S(2)}) collective-permute-start(f32[72,128]{1,0:T(8,128)S(1)} %get-tuple-element.73.own), channel_id=1, source_target_pairs={{0,56},{8,48},{16,40},{24,32},{32,24},{40,16},{48,8},{56,0},{64,12... | collective-permute-start | bytes 110600 | tf_op jit(solution)/shard_map/ppermute | solution.py:658
  22.7 4.2 %collective-permute-start.4 = (f32[72,128]{1,0:T(8,128)S(1)}, f32[72,128]{1,0:T(8,128)S(1)}, u32[]{:S(2)}, u32[]{:S(2)}) collective-permute-start(f32[72,128]{1,0:T(8,128)S(1)} %get-tuple-element.73.own), channel_id=1, source_target_pairs={{0,24},{8,16},{16,8},{24,0},{32,56},{40,48},{48,40},{56,32},{64,88... | collective-permute-start | bytes 110600 | tf_op jit(solution)/shard_map/ppermute | solution.py:658
  23.1 7.1 %collective-permute-start.8 = (f32[64,128]{1,0:T(8,128)S(1)}, f32[64,128]{1,0:T(8,128)S(1)}, u32[]{:S(2)}, u32[]{:S(2)}) collective-permute-start(f32[64,128]{1,0:T(8,128)S(1)} %get-tuple-element.80.near_m), channel_id=1, source_target_pairs={{0,72},{8,64},{16,88},{24,80},{32,104},{40,96},{48,120},{56,112},{... | collective-permute-start | bytes 98312 | tf_op jit(solution)/shard_map/ppermute | solution.py:658
  27.0 4.8 %collective-permute-start.9 = (f32[40,128]{1,0:T(8,128)S(1)}, f32[40,128]{1,0:T(8,128)S(1)}, u32[]{:S(2)}, u32[]{:S(2)}) collective-permute-start(f32[40,128]{1,0:T(8,128)S(1)} %get-tuple-element.81.near), channel_id=1, source_target_pairs={{0,72},{8,64},{16,88},{24,80},{32,104},{40,96},{48,120},{56,112},{... | collective-permute-start | bytes 61448 | tf_op jit(solution)/shard_map/ppermute | solution.py:658
  31.8 1.3 %collective-permute-start.10 = (f32[64,128]{1,0:T(8,128)S(1)}, f32[64,128]{1,0:T(8,128)S(1)}, u32[]{:S(2)}, u32[]{:S(2)}) collective-permute-start(f32[64,128]{1,0:T(8,128)S(1)} %get-tuple-element.94), channel_id=1, source_target_pairs={{0,8},{8,0},{16,24},{24,16},{32,40},{40,32},{48,56},{56,48},{64,72... | collective-permute-start | bytes 98312 | tf_op jit(solution)/shard_map/ppermute | solution.py:658

commit v13 on v12

--- a/solution.py
+++ b/solution.py
@@ -187,7 +187,7 @@
 
 
 def fields_kernel(cot_in, temp_in, sub_in, dep_in, cls_in, cond, keep, send, cot, sub, dep, cls, temp, planes, sems):
-    pieces = [slice(128 * i, 128 * i + 128) for i in range(4)]
+    pieces = [slice(64 * i, 64 * i + 64) for i in range(8)]
     pairs = [(sub_in, sub), (dep_in, dep)] + [(temp_in.at[r], temp.at[r]) for r in pieces]
     pairs += [(cls_in, cls), (cot_in, cot)]
     copies = [pltpu.make_async_copy(a, b, sems.at[i]) for i, (a, b) in enumerate(pairs)]
@@ -197,8 +197,8 @@
         cp.wait()
     sub_v, dep_v = sub[...], dep[...]
     for z in range(64):
-        if z % 16 == 0:
-            copies[2 + z // 16].wait()
+        if z % 8 == 0:
+            copies[2 + z // 8].wait()
         base = jnp.where(z < sub_v, 1.0, 0.45)
         sg = 0.5 + jax.nn.sigmoid(temp[8 * z : 8 * z + 8])
         cond[8 * z : 8 * z + 8] = jnp.where(z < dep_v, base * sg, 0.0)
@@ -214,7 +214,7 @@
         for i, v in enumerate((k[0], k[7]) + chain_matrix(c, s)):
             planes[i, 8 * chunk : 8 * chunk + 8] = v
     split_halves(planes, keep, send)
-    for cp in copies[6:]:
+    for cp in copies[10:]:
         cp.wait()
 
 
@@ -668,7 +668,7 @@
         [(512, 128), (5, 64, 128)],
         "fields",
         cot, temp, substrate_top, deposit_top, top_class,
-        far_in=5, sems=8,
+        far_in=5, sems=12,
     )
     other_m = swap(send_m, 1)
     ypack, fac, ties = call(

time: 34.3 us -> 34.4 us (level)
  no operation moved by 1% of the time
where the time goes in v13:
time: 34.4 us; the launch traced here: 34.1 us
  starting transfers between devices  23.8 us (69%)
  waiting for transfers between devices  4.82 us (14%)
  Pallas kernels  4.79 us (14%)
  between operations  0.7 us (2%)
    ppermute x11, starting transfers between devices, swap(): return lax.ppermute(v, 'gx', [(i, i ^ bit) for i in range(16)])  18.7 us
    all_to_all x1, starting transfers between devices, body(): gat = lax.all_to_all(ypack, 'gy', split_axis=0, concat_axis=0, tiled=True)  5.16 us
    pallas_call x12, Pallas kernels, call(): pl.pallas_call(kernel, out_shape=shapes, in_specs=[HBM if i < far_in else...  4.79 us
    ppermute x11, waiting for transfers between devices, swap(): return lax.ppermute(v, 'gx', [(i, i ^ bit) for i in range(16)])  4.23 us
  transfers between devices with their start and end apart: 12, of which 5 were waited for; matrix products, arithmetic and copies ran while one was open for 0% of the time, Pallas kernels for 7%

profile of v13, /device:TPU:1, one launch (start us, length us, event | category | flops | bytes accessed | tf_op | source)
XLA Modules:
  0.0 34.1 jit_solution(8132781965249164244)
XLA Ops:
  0.6 1.2 %fields.1 = (f32[512,128]{1,0:T(8,128)S(1)}, f32[160,128]{1,0:T(8,128)S(1)}, f32[160,128]{1,0:T(8,128)S(1)}, f32[512,128]{1,0:T(8,128)S(1)}, s32[8,128]{1,0:T(8,...) custom-call(f32[512,128]{1,0:T(8,128)} %bitcast.4, f32[512,128]{1,0:T(8,128)} %bitcast.5, s32[8,128]{1,0:T(8,128)} %sub_in.1, ...), custom_call_target="tpu_custom_call" | custom-call | tf_op jit(solution)/shard_map/fields/pallas_call | solution.py:646
  1.9 1.5 %collective-permute-start = (f32[160,128]{1,0:T(8,128)S(1)}, f32[160,128]{1,0:T(8,128)S(1)}, u32[]{:S(2)}, u32[]{:S(2)}) collective-permute-start(f32[160,128]{1,0:T(8,128)S(1)} %get-tuple-element.58), channel_id=1, source_target_pairs={{0,8},{8,0},{16,24},{24,16},{32,40},{40,32},{48,56},{56,48},{64,72... | collective-permute-start | bytes 245768 | tf_op jit(solution)/shard_map/ppermute | solution.py:658
  3.3 1.3 %first.1 = (f32[8,32,128]{2,1,0:T(8,128)}, f32[3,63,8,128]{3,2,1,0:T(8,128)S(1)}, f32[12,8,128]{2,1,0:T(8,128)S(1)}) custom-call(f32[512,128]{1,0:T(8,128)S(1)} %get-tuple-element.60.cot, s32[8,128]{1,0:T(8,128)S(1)} %get-tuple-element.61.sub, s32[8,128]{1,0:T(8,128)S(1)} %get-tuple-element.62.dep, s32[8,128]{1,0:T(8,128)S(1)} %get-tuple-element.63.cls, ...), custom_call_target="tpu_custom_call" | custom-call | tf_op jit(solution)/shard_map/first/pallas_call | solution.py:646
  4.7 5.2 %all-to-all-start = ((f32[8,32,128]{2,1,0:T(8,128)}), f32[8,32,128]{2,1,0:T(8,128)S(1)}, u32[]{:S(2)}, u32[]{:S(2)}) async-start(f32[8,32,128]{2,1,0:T(8,128)} %get-tuple-element.65), calls=%async_computation | async-start | bytes 262144 | tf_op jit(solution)/shard_map/all_to_all | solution.py:683
  9.8 3.6 %collective-permute-start.5 = (f32[160,128]{1,0:T(8,128)S(1)}, f32[160,128]{1,0:T(8,128)S(1)}, u32[]{:S(2)}, u32[]{:S(2)}) collective-permute-start(f32[160,128]{1,0:T(8,128)S(1)} %get-tuple-element.74.own), channel_id=1, source_target_pairs={{0,32},{8,40},{16,48},{24,56},{32,0},{40,8},{48,16},{56,24},{64,96... | collective-permute-start | bytes 245768 | tf_op jit(solution)/shard_map/ppermute | solution.py:658
  13.4 0.9 %collective-permute-start.6 = (f32[160,128]{1,0:T(8,128)S(1)}, f32[160,128]{1,0:T(8,128)S(1)}, u32[]{:S(2)}, u32[]{:S(2)}) collective-permute-start(f32[160,128]{1,0:T(8,128)S(1)} %get-tuple-element.74.own), channel_id=1, source_target_pairs={{0,56},{8,48},{16,40},{24,32},{32,24},{40,16},{48,8},{56,0},{64,12... | collective-permute-start | bytes 245768 | tf_op jit(solution)/shard_map/ppermute | solution.py:658
  14.3 0.3 collective-permute-start.7
  14.6 0.6 %all-to-all-done.gat = f32[8,32,128]{2,1,0:T(8,128)S(1)} async-done(((f32[8,32,128]{2,1,0:T(8,128)}), f32[8,32,128]{2,1,0:T(8,128)S(1)}, u32[]{:S(2)}, u32[]{:S(2)}) %all-to-all-start) | async-done | bytes 131104 | tf_op jit(solution)/shard_map/all_to_all | solution.py:683
  15.2 0.4 %second.1 = (f32[72,128]{1,0:T(8,128)S(1)}, f32[8,128]{1,0:T(8,128)S(1)}, f32[4,24,8,128]{3,2,1,0:T(8,128)S(1)}, f32[24,1,128]{2,1,0:T(1,128)S(1)}, f32[8,128]{1,0:T(8,128)S(1)}, /*index=5*/f32[512,128]{1,0:T(8,128)S(1)}) custom-call(f32[8,32,128]{2,1,0:T(8,128)S(1)} %all-to-all-done.gat, f32[3,63,8,128]{3,2,1,0:T(8,128)S(1)} %get-tuple-element.66.fac, ...), custom_call_target="tpu_custom_call" | custom-call | tf_op jit(solution)/shard_map/second/pallas_call | solution.py:646
  15.6 1.6 %collective-permute-start.1 = (f32[72,128]{1,0:T(8,128)S(1)}, f32[72,128]{1,0:T(8,128)S(1)}, u32[]{:S(2)}, u32[]{:S(2)}) collective-permute-start(f32[72,128]{1,0:T(8,128)S(1)} %get-tuple-element.71), channel_id=1, source_target_pairs={{0,8},{8,0},{16,24},{24,16},{32,40},{40,32},{48,56},{56,48},{64,72... | collective-permute-start | bytes 110600 | tf_op jit(solution)/shard_map/ppermute | solution.py:658
  17.2 0.1 keep_rows.1
  17.3 0.8 %collective-permute-done.1.theirs = f32[72,128]{1,0:T(8,128)S(1)} collective-permute-done((f32[72,128]{1,0:T(8,128)S(1)}, f32[72,128]{1,0:T(8,128)S(1)}, u32[]{:S(2)}, u32[]{:S(2)}) %collective-permute-start.1) | collective-permute-done | bytes 36896 | tf_op jit(solution)/shard_map/ppermute | solution.py:658
  18.1 3.7 %collective-permute-start.2 = (f32[72,128]{1,0:T(8,128)S(1)}, f32[72,128]{1,0:T(8,128)S(1)}, u32[]{:S(2)}, u32[]{:S(2)}) collective-permute-start(f32[72,128]{1,0:T(8,128)S(1)} %get-tuple-element.73.own), channel_id=1, source_target_pairs={{0,32},{8,40},{16,48},{24,56},{32,0},{40,8},{48,16},{56,24},{64,96... | collective-permute-start | bytes 110600 | tf_op jit(solution)/shard_map/ppermute | solution.py:658
  21.8 0.9 %collective-permute-start.3 = (f32[72,128]{1,0:T(8,128)S(1)}, f32[72,128]{1,0:T(8,128)S(1)}, u32[]{:S(2)}, u32[]{:S(2)}) collective-permute-start(f32[72,128]{1,0:T(8,128)S(1)} %get-tuple-element.73.own), channel_id=1, source_target_pairs={{0,56},{8,48},{16,40},{24,32},{32,24},{40,16},{48,8},{56,0},{64,12... | collective-permute-start | bytes 110600 | tf_op jit(solution)/shard_map/ppermute | solution.py:658
  22.7 0.0 collective-permute-done.5.mid
  22.7 0.3 collective-permute-start.4
  23.0 0.0 collective-permute-done.6.far
  23.0 0.0 collective-permute-done.7.near
  23.0 0.1 matrix_ring.1
  23.1 2.5 %collective-permute-start.8 = (f32[64,128]{1,0:T(8,128)S(1)}, f32[64,128]{1,0:T(8,128)S(1)}, u32[]{:S(2)}, u32[]{:S(2)}) collective-permute-start(f32[64,128]{1,0:T(8,128)S(1)} %get-tuple-element.80.near_m), channel_id=1, source_target_pairs={{0,72},{8,64},{16,88},{24,80},{32,104},{40,96},{48,120},{56,112},{... | collective-permute-start | bytes 98312 | tf_op jit(solution)/shard_map/ppermute | solution.py:658
  25.6 1.3 %collective-permute-done.3.far = f32[72,128]{1,0:T(8,128)S(1)} collective-permute-done((f32[72,128]{1,0:T(8,128)S(1)}, f32[72,128]{1,0:T(8,128)S(1)}, u32[]{:S(2)}, u32[]{:S(2)}) %collective-permute-start.3) | collective-permute-done | bytes 36896 | tf_op jit(solution)/shard_map/ppermute | solution.py:658
  26.9 0.0 collective-permute-done.4.near
  26.9 0.1 merge_ring.1
  27.0 3.0 %collective-permute-start.9 = (f32[40,128]{1,0:T(8,128)S(1)}, f32[40,128]{1,0:T(8,128)S(1)}, u32[]{:S(2)}, u32[]{:S(2)}) collective-permute-start(f32[40,128]{1,0:T(8,128)S(1)} %get-tuple-element.81.near), channel_id=1, source_target_pairs={{0,72},{8,64},{16,88},{24,80},{32,104},{40,96},{48,120},{56,112},{... | collective-permute-start | bytes 61448 | tf_op jit(solution)/shard_map/ppermute | solution.py:658
  30.0 0.3 coef.1
  30.2 0.0 collective-permute-done.8.theirs_m
  30.2 1.5 %collective-permute-done.9.theirs = f32[40,128]{1,0:T(8,128)S(1)} collective-permute-done((f32[40,128]{1,0:T(8,128)S(1)}, f32[40,128]{1,0:T(8,128)S(1)}, u32[]{:S(2)}, u32[]{:S(2)}) %collective-permute-start.9) | collective-permute-done | bytes 20512 | tf_op jit(solution)/shard_map/ppermute | solution.py:658
  31.8 0.1 top.1
  31.9 0.5 %collective-permute-start.10 = (f32[64,128]{1,0:T(8,128)S(1)}, f32[64,128]{1,0:T(8,128)S(1)}, u32[]{:S(2)}, u32[]{:S(2)}) collective-permute-start(f32[64,128]{1,0:T(8,128)S(1)} %get-tuple-element.94), channel_id=1, source_target_pairs={{0,8},{8,0},{16,24},{24,16},{32,40},{40,32},{48,56},{56,48},{64,72... | collective-permute-start | bytes 98312 | tf_op jit(solution)/shard_map/ppermute | solution.py:658
  32.3 0.3 own_rows.1
  32.6 0.6 %collective-permute-done.10.got = f32[64,128]{1,0:T(8,128)S(1)} collective-permute-done((f32[64,128]{1,0:T(8,128)S(1)}, f32[64,128]{1,0:T(8,128)S(1)}, u32[]{:S(2)}, u32[]{:S(2)}) %collective-permute-start.10) | collective-permute-done | bytes 32800 | tf_op jit(solution)/shard_map/ppermute | solution.py:658
  33.2 1.0 %last.1 = (f32[512,128]{1,0:T(8,128)}, f32[512,128]{1,0:T(8,128)}) custom-call(f32[64,128]{1,0:T(8,128)S(1)} %collective-permute-done.10.got, f32[4,24,8,128]{3,2,1,0:T(8,128)S(1)} %get-tuple-element.95.xfac, f32[512,128]{1,0:T(8,128)S(1)} %get-tuple-element.96.k_y, f32[512,128]{1,0:T(8,128)S(1)} %get-tuple-element.97.k_l, ...), custom_call_target="tpu_custom_call" | custom-call | tf_op jit(solution)/shard_map/last/pallas_call | solution.py:646
  (4 shorter events, 0.1 us)
Async XLA Ops:
  1.9 2.8 %collective-permute-start = (f32[160,128]{1,0:T(8,128)S(1)}, f32[160,128]{1,0:T(8,128)S(1)}, u32[]{:S(2)}, u32[]{:S(2)}) collective-permute-start(f32[160,128]{1,0:T(8,128)S(1)} %get-tuple-element.58), channel_id=1, source_target_pairs={{0,8},{8,0},{16,24},{24,16},{32,40},{40,32},{48,56},{56,48},{64,72... | collective-permute-start | bytes 245768 | tf_op jit(solution)/shard_map/ppermute | solution.py:658
  4.7 10.5 %all-to-all-start = ((f32[8,32,128]{2,1,0:T(8,128)}), f32[8,32,128]{2,1,0:T(8,128)S(1)}, u32[]{:S(2)}, u32[]{:S(2)}) async-start(f32[8,32,128]{2,1,0:T(8,128)} %get-tuple-element.65), calls=%async_computation | async-start | bytes 262144 | tf_op jit(solution)/shard_map/all_to_all | solution.py:683
  9.8 12.9 %collective-permute-start.5 = (f32[160,128]{1,0:T(8,128)S(1)}, f32[160,128]{1,0:T(8,128)S(1)}, u32[]{:S(2)}, u32[]{:S(2)}) collective-permute-start(f32[160,128]{1,0:T(8,128)S(1)} %get-tuple-element.74.own), channel_id=1, source_target_pairs={{0,32},{8,40},{16,48},{24,56},{32,0},{40,8},{48,16},{56,24},{64,96... | collective-permute-start | bytes 245768 | tf_op jit(solution)/shard_map/ppermute | solution.py:658
  13.4 9.6 %collective-permute-start.6 = (f32[160,128]{1,0:T(8,128)S(1)}, f32[160,128]{1,0:T(8,128)S(1)}, u32[]{:S(2)}, u32[]{:S(2)}) collective-permute-start(f32[160,128]{1,0:T(8,128)S(1)} %get-tuple-element.74.own), channel_id=1, source_target_pairs={{0,56},{8,48},{16,40},{24,32},{32,24},{40,16},{48,8},{56,0},{64,12... | collective-permute-start | bytes 245768 | tf_op jit(solution)/shard_map/ppermute | solution.py:658
  14.3 8.7 %collective-permute-start.7 = (f32[160,128]{1,0:T(8,128)S(1)}, f32[160,128]{1,0:T(8,128)S(1)}, u32[]{:S(2)}, u32[]{:S(2)}) collective-permute-start(f32[160,128]{1,0:T(8,128)S(1)} %get-tuple-element.74.own), channel_id=1, source_target_pairs={{0,24},{8,16},{16,8},{24,0},{32,56},{40,48},{48,40},{56,32},{64,88... | collective-permute-start | bytes 245768 | tf_op jit(solution)/shard_map/ppermute | solution.py:658
  15.6 2.4 %collective-permute-start.1 = (f32[72,128]{1,0:T(8,128)S(1)}, f32[72,128]{1,0:T(8,128)S(1)}, u32[]{:S(2)}, u32[]{:S(2)}) collective-permute-start(f32[72,128]{1,0:T(8,128)S(1)} %get-tuple-element.71), channel_id=1, source_target_pairs={{0,8},{8,0},{16,24},{24,16},{32,40},{40,32},{48,56},{56,48},{64,72... | collective-permute-start | bytes 110600 | tf_op jit(solution)/shard_map/ppermute | solution.py:658
  18.1 7.5 %collective-permute-start.2 = (f32[72,128]{1,0:T(8,128)S(1)}, f32[72,128]{1,0:T(8,128)S(1)}, u32[]{:S(2)}, u32[]{:S(2)}) collective-permute-start(f32[72,128]{1,0:T(8,128)S(1)} %get-tuple-element.73.own), channel_id=1, source_target_pairs={{0,32},{8,40},{16,48},{24,56},{32,0},{40,8},{48,16},{56,24},{64,96... | collective-permute-start | bytes 110600 | tf_op jit(solution)/shard_map/ppermute | solution.py:658
  21.8 5.2 %collective-permute-start.3 = (f32[72,128]{1,0:T(8,128)S(1)}, f32[72,128]{1,0:T(8,128)S(1)}, u32[]{:S(2)}, u32[]{:S(2)}) collective-permute-start(f32[72,128]{1,0:T(8,128)S(1)} %get-tuple-element.73.own), channel_id=1, source_target_pairs={{0,56},{8,48},{16,40},{24,32},{32,24},{40,16},{48,8},{56,0},{64,12... | collective-permute-start | bytes 110600 | tf_op jit(solution)/shard_map/ppermute | solution.py:658
  22.7 4.2 %collective-permute-start.4 = (f32[72,128]{1,0:T(8,128)S(1)}, f32[72,128]{1,0:T(8,128)S(1)}, u32[]{:S(2)}, u32[]{:S(2)}) collective-permute-start(f32[72,128]{1,0:T(8,128)S(1)} %get-tuple-element.73.own), channel_id=1, source_target_pairs={{0,24},{8,16},{16,8},{24,0},{32,56},{40,48},{48,40},{56,32},{64,88... | collective-permute-start | bytes 110600 | tf_op jit(solution)/shard_map/ppermute | solution.py:658
  23.1 7.1 %collective-permute-start.8 = (f32[64,128]{1,0:T(8,128)S(1)}, f32[64,128]{1,0:T(8,128)S(1)}, u32[]{:S(2)}, u32[]{:S(2)}) collective-permute-start(f32[64,128]{1,0:T(8,128)S(1)} %get-tuple-element.80.near_m), channel_id=1, source_target_pairs={{0,72},{8,64},{16,88},{24,80},{32,104},{40,96},{48,120},{56,112},{... | collective-permute-start | bytes 98312 | tf_op jit(solution)/shard_map/ppermute | solution.py:658
  27.0 4.8 %collective-permute-start.9 = (f32[40,128]{1,0:T(8,128)S(1)}, f32[40,128]{1,0:T(8,128)S(1)}, u32[]{:S(2)}, u32[]{:S(2)}) collective-permute-start(f32[40,128]{1,0:T(8,128)S(1)} %get-tuple-element.81.near), channel_id=1, source_target_pairs={{0,72},{8,64},{16,88},{24,80},{32,104},{40,96},{48,120},{56,112},{... | collective-permute-start | bytes 61448 | tf_op jit(solution)/shard_map/ppermute | solution.py:658
  31.9 1.3 %collective-permute-start.10 = (f32[64,128]{1,0:T(8,128)S(1)}, f32[64,128]{1,0:T(8,128)S(1)}, u32[]{:S(2)}, u32[]{:S(2)}) collective-permute-start(f32[64,128]{1,0:T(8,128)S(1)} %get-tuple-element.94), channel_id=1, source_target_pairs={{0,8},{8,0},{16,24},{24,16},{32,40},{40,32},{48,56},{56,48},{64,72... | collective-permute-start | bytes 98312 | tf_op jit(solution)/shard_map/ppermute | solution.py:658
